TPU v7x, 128 devices: a whole 4x4x4 slice. The times are simulated.
128 devices in a mesh: row: 16 (over z, y), col: 8 (over x, core).
Axes of the slice: x: 4, y: 4, z: 4, core: 2. Of those that a mesh axis runs over, the one named last changes fastest.
Arguments:
- trail_adjoint: float32 [16384, 16384], P('row', 'col'), may hold values from -6 to 6
- lower_new: float32 [16384, 256], P('row', 'col'), may hold values from -0.046875 to 0.046875
- upper_new: float32 [256, 16384], P('row', 'col'), may hold values from -0.046875 to 0.046875
- lower_old_top: float32 [256, 256], replicated, may hold values from -0.375 to 0.375
- lower_old: float32 [16384, 256], P('row', 'col'), may hold values from -0.046875 to 0.046875
- upper_old_left: float32 [256, 256], replicated, may hold values from -0.375 to 0.375
- upper_old: float32 [256, 16384], P('row', 'col'), may hold values from -0.046875 to 0.046875
- diag_lower_new: float32 [256, 256], replicated, as said below
- diag_upper_new: float32 [256, 256], replicated, as said below
- inverse_lower_new: float32 [256, 256], replicated, as said below
- inverse_upper_new: float32 [256, 256], replicated, as said below
- diag_lower_old: float32 [256, 256], replicated, as said below
- diag_upper_old: float32 [256, 256], replicated, as said below
- inverse_lower_old: float32 [256, 256], replicated, as said below
- inverse_upper_old: float32 [256, 256], replicated, as said below
Outputs:
- corner_old: float32 [256, 256], replicated
- strip_top: float32 [256, 256], replicated
- strip_bottom: float32 [16384, 256], P(('row', 'col'))
- band_left: float32 [256, 256], replicated
- band_right: float32 [256, 16384], P(None, 'col')
Inputs may be any that keep to these rules, and one draw needn't show every extreme that they name: `diag_lower_new`: unit lower triangular. `diag_upper_new`: upper triangular, diagonal from 1 to 2. `inverse_lower_new`: the inverse of diag_lower_new. `inverse_upper_new`: the inverse of diag_upper_new. `diag_lower_old`: unit lower triangular. `diag_upper_old`: upper triangular, diagonal from 1 to 2. `inverse_lower_old`: the inverse of diag_lower_old. `inverse_upper_old`: the inverse of diag_upper_old.
All inputs are finite; a program needn't handle non-finite values.
Results may differ from a plain program's by a relative error of at most 0.000075.
Values sent between devices are 32-bit elements; how exact they have to be, the bound alone decides.
No kernel may reach another device: no remote copies, remote signals or barrier semaphores. Data moves between devices by JAX's collectives and lax.ppermute only.
A program may use at most 128 MiB of HBM per device.

v0:
```python
import functools

import jax
import jax.numpy as jnp
from jax import lax
from jax.experimental import pallas as pl
from jax.experimental.pallas import tpu as pltpu
from jax.sharding import Mesh, PartitionSpec as P

HALF = jnp.bfloat16
FULL = jnp.float32
VMEM = pl.BlockSpec(memory_space=pltpu.VMEM)


def mul(left, right, dims):
    return lax.dot_general(left, right, (dims, ((), ())), preferred_element_type=FULL)


def exact(left, right, dims=((1,), (0,))):
    return lax.dot_general(
        left,
        right,
        (dims, ((), ())),
        precision=lax.Precision.HIGHEST,
        preferred_element_type=FULL,
    )


def parts(value):
    high = value.astype(HALF)
    return high, (value - high.astype(FULL)).astype(HALF)


def close(left, right, dims=((1,), (0,))):
    (lh, ll), (rh, rl) = left, right
    return mul(lh, rl, dims) + mul(ll, rh, dims) + mul(lh, rh, dims)


X_NEW, Y_NEW, U_PAIR, U_TRIPLE, L_PAIR, L_TRIPLE = range(6)


def prepare_kernel(lot, uol, ldn, udn, lin, uin, lio, uio, out):
    upper_pair = exact(uol[...].T, uio[...].T)
    lower_pair = exact(lio[...].T, lot[...].T)
    out[X_NEW] = exact(ldn[...].T, lin[...].T)
    out[Y_NEW] = exact(uin[...].T, udn[...].T)
    out[U_PAIR] = upper_pair
    out[L_PAIR] = lower_pair
    out[U_TRIPLE] = exact(uin[...].T, upper_pair)
    out[L_TRIPLE] = exact(lower_pair, lin[...].T)


def prepare(*factors):
    width = factors[0].shape[0]
    return pl.pallas_call(
        prepare_kernel,
        out_shape=jax.ShapeDtypeStruct((6, width, width), FULL),
        in_specs=[VMEM] * len(factors),
        out_specs=VMEM,
        name="prepare",
        cost_estimate=pl.CostEstimate(
            flops=72 * width**3, bytes_accessed=56 * width**2, transcendentals=0
        ),
    )(*factors)


def lower_rows(lower, panel, count, piece):
    return jnp.concatenate(
        [
            lower[pl.ds((2 * k + panel) * piece, piece), :]
            for k in range(count)
        ],
        axis=0,
    )


def band_kernel(count, small, lio, lower, trail, out, weight_high, weight_low):
    width = lio.shape[0]
    piece = width // count

    @pl.when(pl.program_id(0) == 0)
    def _():
        new = parts(lower_rows(lower, 0, count, piece))
        old = parts(lower_rows(lower, 1, count, piece))
        weight = close(parts(small[0]), new) - close(parts(lio[...].T), old)
        high, low = parts(weight)
        weight_high[...] = high
        weight_low[...] = low

    band = close((weight_high[...], weight_low[...]), parts(trail[...]))
    size = out.shape[1] // 2
    for k in range(16):
        turned = 4 * (k % 4) + k // 4
        first, second = k * size, width // 2 + turned * size
        out[k, :size, :] = band[first : first + size, :]
        out[k, size:, :] = band[second : second + size, :]


def band_products(small, lio, lower, trail, ranks, count, tile=512):
    rows, columns = trail.shape
    width = lio.shape[0]
    return pl.pallas_call(
        functools.partial(band_kernel, count),
        out_shape=jax.ShapeDtypeStruct((ranks, width // ranks, columns), FULL),
        grid=(columns // tile,),
        in_specs=[
            pl.BlockSpec((1, width, width), lambda j: (L_TRIPLE, 0, 0)),
            pl.BlockSpec((width, width), lambda j: (0, 0)),
            pl.BlockSpec((2 * width, rows), lambda j: (0, 0)),
            pl.BlockSpec((rows, tile), lambda j: (0, j)),
        ],
        out_specs=pl.BlockSpec((ranks, width // ranks, tile), lambda j: (0, 0, j)),
        scratch_shapes=[pltpu.VMEM((width, rows), HALF)] * 2,
        compiler_params=pltpu.CompilerParams(vmem_limit_bytes=48 << 20),
        name="band_products",
        cost_estimate=pl.CostEstimate(
            flops=6 * width * rows * columns,
            bytes_accessed=4 * (rows * columns + 2 * width * rows + width * columns),
            transcendentals=0,
        ),
    )(small, lio, lower, trail)


def panel_kernel(count, place, small, uio, lower, trail, *rest):
    pieces, (inner, strip, upper_high, upper_low, side_high, side_low) = rest[:8], rest[8:]
    width = uio.shape[0]
    z, y = place[0], place[1]

    @pl.when(pl.program_id(0) == 0)
    def _():
        inner[...] = jnp.zeros_like(inner)
        high, low = parts(small[0])
        side_high[:width, :] = high
        side_low[:width, :] = low
        high, low = parts(-uio[...].T)
        side_high[width:, :] = high
        side_low[width:, :] = low
        for k in range(4):
            high, low = parts(pieces[k][...])
            chunk = high.shape[0] // 4
            for zz in range(4):
                at = pl.ds(pl.multiple_of((4 * zz + (y ^ k)) * chunk, chunk), chunk)
                upper_high[at, :] = high[zz * chunk : (zz + 1) * chunk, :]
                upper_low[at, :] = low[zz * chunk : (zz + 1) * chunk, :]
            high, low = parts(pieces[4 + k][...])
            size = high.shape[0]
            at = pl.ds(pl.multiple_of(width + (z ^ k) * size, size), size)
            upper_high[at, :] = high
            upper_low[at, :] = low

    product = close(parts(trail[...]), (upper_high[...], upper_low[...]), ((1,), (1,)))
    product = parts(product)
    strip[...] = close(product, (side_high[...], side_low[...]))
    piece = width // count
    for panel in range(2):
        left = parts(lower_rows(lower, panel, count, piece))
        inner[panel * width : (panel + 1) * width, :] += close(left, product)


def panel_products(place, small, uio, lower, trail, pieces, count, tile=256):
    rows, columns = trail.shape
    width = uio.shape[0]
    once = pl.Buffered(1)
    size = pieces[0].shape[0]
    return pl.pallas_call(
        functools.partial(panel_kernel, count),
        out_shape=(
            jax.ShapeDtypeStruct((2 * width, 2 * width), FULL),
            jax.ShapeDtypeStruct((rows, width), FULL),
        ),
        grid_spec=pltpu.PrefetchScalarGridSpec(
            num_scalar_prefetch=1,
            grid=(rows // tile,),
            in_specs=[
                pl.BlockSpec((1, width, width), lambda i, p: (U_TRIPLE, 0, 0)),
                pl.BlockSpec((width, width), lambda i, p: (0, 0)),
                pl.BlockSpec((2 * width, tile), lambda i, p: (0, i)),
                pl.BlockSpec((tile, columns), lambda i, p: (i, 0)),
            ]
            + [pl.BlockSpec((size, columns), lambda i, p: (0, 0), pipeline_mode=once)] * 8,
            out_specs=(
                pl.BlockSpec((2 * width, 2 * width), lambda i, p: (0, 0)),
                pl.BlockSpec((tile, width), lambda i, p: (i, 0)),
            ),
            scratch_shapes=[pltpu.VMEM((2 * width, columns), HALF)] * 2
            + [pltpu.VMEM((2 * width, width), HALF)] * 2,
        ),
        compiler_params=pltpu.CompilerParams(vmem_limit_bytes=48 << 20),
        name="panel_products",
        cost_estimate=pl.CostEstimate(
            flops=3 * (4 * width * rows * columns + 12 * width * width * rows),
            bytes_accessed=4 * (rows * columns + 2 * width * columns + 3 * width * rows),
            transcendentals=0,
        ),
    )(place, small, uio, lower, trail, *pieces)


def finish_kernel(
    inner, small, lot, uol, lin, uin, ldo, udo, lio, uio, corner_out, top_out, left_out
):
    width = lin.shape[0]
    row = lax.broadcasted_iota(jnp.int32, (width, width), 0)
    column = lax.broadcasted_iota(jnp.int32, (width, width), 1)
    below = row > column
    g11, g12 = inner[:width, :width], inner[:width, width:]
    g21, g22 = inner[width:, :width], inner[width:, width:]
    lin_t, uin_t, lio_t, uio_t = lin[...].T, uin[...].T, lio[...].T, uio[...].T
    inside = jnp.where(below, exact(small[X_NEW], g11), exact(g11, small[Y_NEW]))
    corner = exact(exact(lin_t, inside), uin_t)
    top = exact(exact(lin_t, g12), uio_t) - exact(corner, small[U_PAIR])
    left = exact(lio_t, exact(g21, uin_t)) - exact(small[L_PAIR], corner)
    top_out[...] = top
    left_out[...] = left
    outer = exact(small[L_TRIPLE], g12) - exact(lio_t, g22)
    under = exact(g21, small[U_TRIPLE]) - exact(g22, uio_t)
    lower_grad = -(exact(left, uol[...].T) + outer)
    upper_grad = -(exact(lot[...].T, top) + under)
    inside = jnp.where(
        below, exact(ldo[...].T, lower_grad), exact(upper_grad, udo[...].T)
    )
    corner_out[...] = exact(exact(lio_t, inside), uio_t)


def finish(inner, small, *factors):
    width = factors[0].shape[0]
    return pl.pallas_call(
        finish_kernel,
        out_shape=(jax.ShapeDtypeStruct((width, width), FULL),) * 3,
        in_specs=[VMEM] * (2 + len(factors)),
        out_specs=(VMEM,) * 3,
        name="finish",
        cost_estimate=pl.CostEstimate(
            flops=240 * width**3, bytes_accessed=84 * width**2, transcendentals=0
        ),
    )(inner, small, *factors)


def swap(value, axis, step):
    size = lax.axis_size(axis)
    return lax.ppermute(value, axis, [(i, i ^ step) for i in range(size)])


def block(value, index, size):
    return lax.dynamic_slice_in_dim(value, index * size, size, 0)


def scatter_sum(value, axis):
    count = lax.axis_size(axis)
    me = lax.axis_index(axis)
    size = value.shape[0] // count
    total = block(value, me, size)
    for step in range(1, count):
        total = total + swap(block(value, me ^ step, size), axis, step)
    return total


def pieces_of(value, axis):
    return [value] + [swap(value, axis, step) for step in range(1, lax.axis_size(axis))]


def placed(pieces, axis):
    me = lax.axis_index(axis)
    size = pieces[0].shape[0]
    out = jnp.zeros((len(pieces) * size, *pieces[0].shape[1:]), pieces[0].dtype)
    for step, piece in enumerate(pieces):
        out = lax.dynamic_update_slice_in_dim(out, piece, (me ^ step) * size, 0)
    return out


def gather(value, axis):
    return placed(pieces_of(value, axis), axis)


def together(*values):
    return lax.optimization_barrier(values)


def total(value, axis):
    own, first, second, third = pieces_of(value, axis)
    return (own + first) + (second + third)


def body(
    trail,
    lower_new,
    upper_new,
    lot,
    lower_old,
    uol,
    upper_old,
    ldn,
    udn,
    lin,
    uin,
    ldo,
    udo,
    lio,
    uio,
):
    row, col = ("z", "y"), ("x", "c")
    count = lax.axis_size(col)
    ranks = lax.axis_size(row)

    lower_mine = jnp.concatenate((lower_new.T, lower_old.T), axis=0)
    lower_stack = lax.all_gather(lower_mine, col, axis=0, tiled=True)
    near = together(*pieces_of(upper_new, "z"), *pieces_of(upper_old, "y"))
    near_new, near_old = together(placed(near[:4], "z"), placed(near[4:], "y"))
    pieces = pieces_of(near_new, "y") + pieces_of(near_old, "z")

    small = prepare(lot, uol, ldn, udn, lin, uin, lio, uio)
    band = band_products(small, lio, lower_stack, trail, ranks, count)
    *pieces, _ = together(*pieces, band)
    band = lax.all_to_all(band, row, 0, 0, tiled=True)

    place = jnp.stack((lax.axis_index("z"), lax.axis_index("y"))).astype(jnp.int32)
    inner, strip = panel_products(place, small, uio, lower_stack, trail, pieces, count)
    strip_bottom = lax.psum_scatter(strip, col, scatter_dimension=0, tiled=True)

    inner = scatter_sum(scatter_sum(inner, "c"), "x")
    inner, band = together(inner, band.sum(0))
    half = band.shape[0] // 2
    first = pieces_of(band[:half], "y")
    second = pieces_of(band[half:], "z")
    inner = total(total(inner, "y"), "z")
    inner, *band = together(inner, *first, *second)
    first = pieces_of(placed(band[:4], "y"), "z")
    second = pieces_of(placed(band[4:], "z"), "y")
    inner, strip_bottom = together(inner, strip_bottom)
    inner = gather(gather(inner, "x"), "c")
    small_outs = finish(inner, small, lot, uol, lin, uin, ldo, udo, lio, uio)
    *band, corner_old, strip_top, band_left = together(*first, *second, *small_outs)
    band_right = jnp.concatenate((placed(band[:4], "z"), placed(band[4:], "y")), axis=0)
    return corner_old, strip_top, strip_bottom, band_left, band_right


def solution(mesh):
    fine = Mesh(mesh.devices.reshape(4, 4, 4, 2), ("z", "y", "x", "c"))
    row, col = ("z", "y"), ("x", "c")
    split, whole = P(row, col), P()
    return jax.shard_map(
        body,
        mesh=fine,
        in_specs=(split, split, split, whole, split, whole, split) + (whole,) * 8,
        out_specs=(whole, whole, P(row + col, None), whole, P(None, col)),
        check_vma=False,
    )
```

profile of v0, /device:TPU:1, one launch (start us, length us, event | category | flops | bytes accessed | tf_op | source)
XLA Modules:
  0.0 169.2 jit_solution(12980650086292051507)
XLA Ops:
  7.2 1.7 %pad_maximum_fusion.1 = f32[64,1024]{1,0:T(8,128)} fusion(f32[32,1024]{1,0:T(8,128)} %bitcast.4, f32[32,1024]{1,0:T(8,128)} %bitcast.5), kind=kLoop, calls=%fused_computation.2 | loop fusion | flops 65536 | bytes 524288 | tf_op jit(solution)/shard_map/concatenate | solution.py:304
  9.0 2.5 %collective-permute-start = (f32[16,2048]{1,0:T(8,128)}, f32[16,2048]{1,0:T(8,128)S(1)}, u32[]{:S(2)}, u32[]{:S(2)}) collective-permute-start(f32[16,2048]{1,0:T(8,128)} %param.17), channel_id=1, source_target_pairs={{0,32},{32,0},{64,96},{96,64},{1,33},{33,1},{65,97},{97,65},{2,34}... | collective-permute-start | bytes 393224 | tf_op jit(solution)/shard_map/ppermute | solution.py:240
  11.5 3.3 %collective-permute-start.1 = (f32[16,2048]{1,0:T(8,128)}, f32[16,2048]{1,0:T(8,128)S(1)}, u32[]{:S(2)}, u32[]{:S(2)}) collective-permute-start(f32[16,2048]{1,0:T(8,128)} %param.17), channel_id=1, source_target_pairs={{0,64},{32,96},{64,0},{96,32},{1,65},{33,97},{65,1},{97,33},{2,66}... | collective-permute-start | bytes 393224 | tf_op jit(solution)/shard_map/ppermute | solution.py:240
  16.1 2.6 %collective-permute-start.4 = (f32[16,2048]{1,0:T(8,128)}, f32[16,2048]{1,0:T(8,128)S(1)}, u32[]{:S(2)}, u32[]{:S(2)}) collective-permute-start(f32[16,2048]{1,0:T(8,128)} %param.21), channel_id=1, source_target_pairs={{0,16},{8,24},{16,0},{24,8},{1,17},{9,25},{17,1},{25,9},{2,18},{10... | collective-permute-start | bytes 393224 | tf_op jit(solution)/shard_map/ppermute | solution.py:240
  18.7 2.0 %collective-permute-done.1 = f32[16,2048]{1,0:T(8,128)S(1)} collective-permute-done((f32[16,2048]{1,0:T(8,128)}, f32[16,2048]{1,0:T(8,128)S(1)}, u32[]{:S(2)}, u32[]{:S(2)}) %collective-permute-start.1) | collective-permute-done | bytes 131104 | tf_op jit(solution)/shard_map/ppermute | solution.py:240
  20.7 2.5 %collective-permute-done.2 = f32[16,2048]{1,0:T(8,128)S(1)} collective-permute-done((f32[16,2048]{1,0:T(8,128)}, f32[16,2048]{1,0:T(8,128)S(1)}, u32[]{:S(2)}, u32[]{:S(2)}) %collective-permute-start.2) | collective-permute-done | bytes 131104 | tf_op jit(solution)/shard_map/ppermute | solution.py:240
  23.8 2.8 %collective-permute-done.5 = f32[16,2048]{1,0:T(8,128)S(1)} collective-permute-done((f32[16,2048]{1,0:T(8,128)}, f32[16,2048]{1,0:T(8,128)S(1)}, u32[]{:S(2)}, u32[]{:S(2)}) %collective-permute-start.5) | collective-permute-done | bytes 131104 | tf_op jit(solution)/shard_map/ppermute | solution.py:240
  30.3 2.2 %collective-permute-start.7 = (f32[64,2048]{1,0:T(8,128)S(1)}, f32[64,2048]{1,0:T(8,128)S(1)}, u32[]{:S(2)}, u32[]{:S(2)}) collective-permute-start(f32[64,2048]{1,0:T(8,128)S(1)} %get-tuple-element.62.rest_0_), channel_id=1, source_target_pairs={{0,16},{8,24},{16,0},{24,8},{1,17},{9,25},{17,1},{25,9},{2,18},{10... | collective-permute-start | bytes 1572872 | tf_op jit(solution)/shard_map/ppermute | solution.py:240
  34.2 7.1 %collective-permute-done.10.rest_6_ = f32[64,2048]{1,0:T(8,128)S(1)} collective-permute-done((f32[64,2048]{1,0:T(8,128)S(1)}, f32[64,2048]{1,0:T(8,128)S(1)}, u32[]{:S(2)}, u32[]{:S(2)}) %collective-permute-start.10) | collective-permute-done | bytes 524320 | tf_op jit(solution)/shard_map/ppermute | solution.py:240
  41.6 4.4 %prepare.1.small = f32[6,256,256]{2,1,0:T(8,128)} custom-call(f32[256,256]{1,0:T(8,128)} %lot.3, f32[256,256]{1,0:T(8,128)} %uol.3, f32[256,256]{1,0:T(8,128)} %ldn.1, f32[256,256]{1,0:T(8,128)} %udn.1, f32[256,256]{1,0:T(8,128)} %lin.3, f32[256,256]{1,0:T(8,128)} %uin.3, f32[256,256]{1,0:T(8,128)} %lio.5, f32[256,256]{1,0:T(8,128)} %uio.5), custom_call_target="tpu_custom_call" | custom-call | flops 1207959552 | bytes 3670016 | tf_op jit(solution)/shard_map/prepare/pallas_call | solution.py:55
  49.0 8.3 %band_products.1 = f32[16,16,2048]{2,1,0:T(8,128)} custom-call(f32[6,256,256]{2,1,0:T(8,128)S(1)} %copy-done.1, f32[256,256]{1,0:T(8,128)S(1)} %copy-done.2, f32[512,1024]{1,0:T(8,128)S(1)} %copy-done, f32[1024,2048]{1,0:T(8,128)} %trail.3), custom_call_target="tpu_custom_call" | custom-call | flops 3221225472 | bytes 12582912 | tf_op jit(solution)/shard_map/band_products/pallas_call | solution.py:102
  57.3 5.8 %all-to-all-start = ((f32[16,16,2048]{2,1,0:T(8,128)}), f32[16,16,2048]{2,1,0:T(8,128)}, u32[]{:S(2)}, u32[]{:S(2)}) async-start(f32[16,16,2048]{2,1,0:T(8,128)} %band_products.1), calls=%async_computation | async-start | bytes 4194304 | tf_op jit(solution)/shard_map/all_to_all | solution.py:313
  66.9 14.7 %panel_products.1 = (f32[512,512]{1,0:T(8,128)S(1)}, f32[1024,256]{1,0:T(8,128)}) custom-call(s32[2]{0:T(128)S(1)} %pad_add_fusion.place, f32[6,256,256]{2,1,0:T(8,128)} %prepare.1.small, f32[256,256]{1,0:T(8,128)S(1)} %copy-done.7, f32[512,1024]{1,0:T(8,128)} %all-gather.2.cloned.1.call-done.lower, f32[1024,2048]{1,0:T(8,128)} %trail.3, ...), custom_call_target="tpu_custom_call" | custom-call | flops 8858370048 | bytes 15728640 | tf_op jit(solution)/shard_map/panel_products/pallas_call | solution.py:165
  81.6 3.0 %collective-permute-start.12 = (f32[256,512]{1,0:T(8,128)S(1)}, f32[256,512]{1,0:T(8,128)S(1)}, u32[]{:S(2)}, u32[]{:S(2)}) collective-permute-start(f32[256,512]{1,0:T(8,128)S(1)} %constant_dynamic-slice_fusion.3), channel_id=1, source_target_pairs={{0,1},{1,0},{2,3},{3,2},{4,5},{5,4},{6,7},{7,6},{8,9},{9,8},{10,11... | collective-permute-start | bytes 1572872 | tf_op jit(solution)/shard_map/ppermute | solution.py:240
  87.5 2.5 %collective-permute-start.14 = (f32[64,512]{1,0:T(8,128)S(1)}, f32[64,512]{1,0:T(8,128)S(1)}, u32[]{:S(2)}, u32[]{:S(2)}) collective-permute-start(f32[64,512]{1,0:T(8,128)S(1)} %get-tuple-element.101), channel_id=1, source_target_pairs={{0,4},{2,6},{4,0},{6,2},{1,5},{3,7},{5,1},{7,3},{8,12},{10,14},{12... | collective-permute-start | bytes 393224 | tf_op jit(solution)/shard_map/ppermute | solution.py:240
  91.0 5.0 %collective-permute-done.14 = f32[64,512]{1,0:T(8,128)S(1)} collective-permute-done((f32[64,512]{1,0:T(8,128)S(1)}, f32[64,512]{1,0:T(8,128)S(1)}, u32[]{:S(2)}, u32[]{:S(2)}) %collective-permute-start.14) | collective-permute-done | bytes 131104 | tf_op jit(solution)/shard_map/ppermute | solution.py:240
  96.1 3.0 %collective-permute-done.15 = f32[64,512]{1,0:T(8,128)S(1)} collective-permute-done((f32[64,512]{1,0:T(8,128)S(1)}, f32[64,512]{1,0:T(8,128)S(1)}, u32[]{:S(2)}, u32[]{:S(2)}) %collective-permute-start.15) | collective-permute-done | bytes 131104 | tf_op jit(solution)/shard_map/ppermute | solution.py:240
  100.9 1.9 %collective-permute-start.16 = (f32[64,512]{1,0:T(8,128)S(1)}, f32[64,512]{1,0:T(8,128)S(1)}, u32[]{:S(2)}, u32[]{:S(2)}) collective-permute-start(f32[64,512]{1,0:T(8,128)S(1)} %add_add_fusion.2), channel_id=1, source_target_pairs={{0,8},{8,0},{16,24},{24,16},{1,9},{9,1},{17,25},{25,17},{2,10},{10... | collective-permute-start | bytes 393224 | tf_op jit(solution)/shard_map/ppermute | solution.py:240
  102.8 2.4 %collective-permute-start.17 = (f32[64,512]{1,0:T(8,128)S(1)}, f32[64,512]{1,0:T(8,128)S(1)}, u32[]{:S(2)}, u32[]{:S(2)}) collective-permute-start(f32[64,512]{1,0:T(8,128)S(1)} %add_add_fusion.2), channel_id=1, source_target_pairs={{0,16},{8,24},{16,0},{24,8},{1,17},{9,25},{17,1},{25,9},{2,18},{10... | collective-permute-start | bytes 393224 | tf_op jit(solution)/shard_map/ppermute | solution.py:240
  105.6 4.6 %collective-permute-done.17 = f32[64,512]{1,0:T(8,128)S(1)} collective-permute-done((f32[64,512]{1,0:T(8,128)S(1)}, f32[64,512]{1,0:T(8,128)S(1)}, u32[]{:S(2)}, u32[]{:S(2)}) %collective-permute-start.17) | collective-permute-done | bytes 131104 | tf_op jit(solution)/shard_map/ppermute | solution.py:240
  110.2 2.9 %collective-permute-done.18 = f32[64,512]{1,0:T(8,128)S(1)} collective-permute-done((f32[64,512]{1,0:T(8,128)S(1)}, f32[64,512]{1,0:T(8,128)S(1)}, u32[]{:S(2)}, u32[]{:S(2)}) %collective-permute-start.18) | collective-permute-done | bytes 131104 | tf_op jit(solution)/shard_map/ppermute | solution.py:240
  114.3 2.1 %collective-permute-start.20 = (f32[64,512]{1,0:T(8,128)S(1)}, f32[64,512]{1,0:T(8,128)S(1)}, u32[]{:S(2)}, u32[]{:S(2)}) collective-permute-start(f32[64,512]{1,0:T(8,128)S(1)} %add_add_fusion.1), channel_id=1, source_target_pairs={{0,64},{32,96},{64,0},{96,32},{1,65},{33,97},{65,1},{97,33},{2,66}... | collective-permute-start | bytes 393224 | tf_op jit(solution)/shard_map/ppermute | solution.py:240
  117.3 2.2 %collective-permute-start.23 = (f32[8,2048]{1,0:T(8,128)S(1)}, f32[8,2048]{1,0:T(8,128)S(1)}, u32[]{:S(2)}, u32[]{:S(2)}) collective-permute-start(f32[8,2048]{1,0:T(8,128)S(1)} %get-tuple-element.73), channel_id=1, source_target_pairs={{0,16},{8,24},{16,0},{24,8},{1,17},{9,25},{17,1},{25,9},{2,18},{10... | collective-permute-start | bytes 196616 | tf_op jit(solution)/shard_map/ppermute | solution.py:240
  121.5 3.4 %collective-permute-start.26 = (f32[8,2048]{1,0:T(8,128)S(1)}, f32[8,2048]{1,0:T(8,128)S(1)}, u32[]{:S(2)}, u32[]{:S(2)}) collective-permute-start(f32[8,2048]{1,0:T(8,128)S(1)} %get-tuple-element.77), channel_id=1, source_target_pairs={{0,64},{32,96},{64,0},{96,32},{1,65},{33,97},{65,1},{97,33},{2,66}... | collective-permute-start | bytes 196616 | tf_op jit(solution)/shard_map/ppermute | solution.py:240
  125.3 1.9 %collective-permute-done.26 = f32[8,2048]{1,0:T(8,128)S(1)} collective-permute-done((f32[8,2048]{1,0:T(8,128)S(1)}, f32[8,2048]{1,0:T(8,128)S(1)}, u32[]{:S(2)}, u32[]{:S(2)}) %collective-permute-start.26) | collective-permute-done | bytes 65568 | tf_op jit(solution)/shard_map/ppermute | solution.py:240
  127.2 2.0 %collective-permute-done.27 = f32[8,2048]{1,0:T(8,128)S(1)} collective-permute-done((f32[8,2048]{1,0:T(8,128)S(1)}, f32[8,2048]{1,0:T(8,128)S(1)}, u32[]{:S(2)}, u32[]{:S(2)}) %collective-permute-start.27) | collective-permute-done | bytes 65568 | tf_op jit(solution)/shard_map/ppermute | solution.py:240
  130.3 2.8 %collective-permute-start.36 = (f32[64,512]{1,0:T(8,128)S(1)}, f32[64,512]{1,0:T(8,128)S(1)}, u32[]{:S(2)}, u32[]{:S(2)}) collective-permute-start(f32[64,512]{1,0:T(8,128)S(1)} %add_add_fusion), channel_id=1, source_target_pairs={{0,6},{2,4},{4,2},{6,0},{1,7},{3,5},{5,3},{7,1},{8,14},{10,12},{12... | collective-permute-start | bytes 393224 | tf_op jit(solution)/shard_map/ppermute | solution.py:240
  133.3 2.5 %collective-permute-start.32 = (f32[32,2048]{1,0:T(8,128)S(1)}, f32[32,2048]{1,0:T(8,128)S(1)}, u32[]{:S(2)}, u32[]{:S(2)}) collective-permute-start(f32[32,2048]{1,0:T(8,128)S(1)} %constant_dynamic-update-slice_fusion.14), channel_id=1, source_target_pairs={{0,16},{8,24},{16,0},{24,8},{1,17},{9,25},{17,1},{25,9},{2,18},{10... | collective-permute-start | bytes 786440 | tf_op jit(solution)/shard_map/ppermute | solution.py:240
  137.4 6.5 %collective-permute-start.37 = (f32[256,512]{1,0:T(8,128)S(1)}, f32[256,512]{1,0:T(8,128)S(1)}, u32[]{:S(2)}, u32[]{:S(2)}) collective-permute-start(f32[256,512]{1,0:T(8,128)S(1)} %constant_dynamic-update-slice_fusion.10), channel_id=1, source_target_pairs={{0,1},{1,0},{2,3},{3,2},{4,5},{5,4},{6,7},{7,6},{8,9},{9,8},{10,11... | collective-permute-start | bytes 1572872 | tf_op jit(solution)/shard_map/ppermute | solution.py:240
  146.0 2.6 %collective-permute-start.30 = (f32[32,2048]{1,0:T(8,128)S(1)}, f32[32,2048]{1,0:T(8,128)S(1)}, u32[]{:S(2)}, u32[]{:S(2)}) collective-permute-start(f32[32,2048]{1,0:T(8,128)S(1)} %constant_dynamic-update-slice_fusion.18), channel_id=1, source_target_pairs={{0,96},{32,64},{64,32},{96,0},{1,97},{33,65},{65,33},{97,1},{2,98}... | collective-permute-start | bytes 786440 | tf_op jit(solution)/shard_map/ppermute | solution.py:240
  148.6 8.8 %finish.1 = (f32[256,256]{1,0:T(8,128)}, f32[256,256]{1,0:T(8,128)}, f32[256,256]{1,0:T(8,128)}) custom-call(f32[512,512]{1,0:T(8,128)} %copy-done.8, f32[6,256,256]{2,1,0:T(8,128)} %prepare.1.small, f32[256,256]{1,0:T(8,128)} %lot.3, f32[256,256]{1,0:T(8,128)} %uol.3, f32[256,256]{1,0:T(8,128)} %lin.3, f32[256,256]{1,0:T(8,128)} %uin.3, f32[256,256]{1,0:T(8,128)} %ldo.1, ...), custom_call_target="tpu_custom_call" | custom-call | flops 4026531840 | bytes 5505024 | tf_op jit(solution)/shard_map/finish/pallas_call | solution.py:226
  157.7 2.6 %collective-permute-done.30 = f32[32,2048]{1,0:T(8,128)S(1)} collective-permute-done((f32[32,2048]{1,0:T(8,128)S(1)}, f32[32,2048]{1,0:T(8,128)S(1)}, u32[]{:S(2)}, u32[]{:S(2)}) %collective-permute-start.30) | collective-permute-done | bytes 262176 | tf_op jit(solution)/shard_map/ppermute | solution.py:240
  (124 shorter events, 31.8 us)
Async XLA Ops:
  7.2 38.8 %all-gather.2.cloned.1.call-start = ((), (), s32[]{:S(2)}) async-start(), calls=%async_computation.2 | async-start | bytes 2359296 | tf_op jit(solution)/shard_map/all_gather | solution.py:305
  9.0 9.8 %collective-permute-start = (f32[16,2048]{1,0:T(8,128)}, f32[16,2048]{1,0:T(8,128)S(1)}, u32[]{:S(2)}, u32[]{:S(2)}) collective-permute-start(f32[16,2048]{1,0:T(8,128)} %param.17), channel_id=1, source_target_pairs={{0,32},{32,0},{64,96},{96,64},{1,33},{33,1},{65,97},{97,65},{2,34}... | collective-permute-start | bytes 393224 | tf_op jit(solution)/shard_map/ppermute | solution.py:240
  11.5 9.2 %collective-permute-start.1 = (f32[16,2048]{1,0:T(8,128)}, f32[16,2048]{1,0:T(8,128)S(1)}, u32[]{:S(2)}, u32[]{:S(2)}) collective-permute-start(f32[16,2048]{1,0:T(8,128)} %param.17), channel_id=1, source_target_pairs={{0,64},{32,96},{64,0},{96,32},{1,65},{33,97},{65,1},{97,33},{2,66}... | collective-permute-start | bytes 393224 | tf_op jit(solution)/shard_map/ppermute | solution.py:240
  14.8 8.4 %collective-permute-start.2 = (f32[16,2048]{1,0:T(8,128)}, f32[16,2048]{1,0:T(8,128)S(1)}, u32[]{:S(2)}, u32[]{:S(2)}) collective-permute-start(f32[16,2048]{1,0:T(8,128)} %param.17), channel_id=1, source_target_pairs={{0,96},{32,64},{64,32},{96,0},{1,97},{33,65},{65,33},{97,1},{2,98}... | collective-permute-start | bytes 393224 | tf_op jit(solution)/shard_map/ppermute | solution.py:240
  14.8 8.4 %collective-permute-start.3 = (f32[16,2048]{1,0:T(8,128)}, f32[16,2048]{1,0:T(8,128)S(1)}, u32[]{:S(2)}, u32[]{:S(2)}) collective-permute-start(f32[16,2048]{1,0:T(8,128)} %param.21), channel_id=1, source_target_pairs={{0,8},{8,0},{16,24},{24,16},{1,9},{9,1},{17,25},{25,17},{2,10},{10... | collective-permute-start | bytes 393224 | tf_op jit(solution)/shard_map/ppermute | solution.py:240
  16.1 7.6 %collective-permute-start.4 = (f32[16,2048]{1,0:T(8,128)}, f32[16,2048]{1,0:T(8,128)S(1)}, u32[]{:S(2)}, u32[]{:S(2)}) collective-permute-start(f32[16,2048]{1,0:T(8,128)} %param.21), channel_id=1, source_target_pairs={{0,16},{8,24},{16,0},{24,8},{1,17},{9,25},{17,1},{25,9},{2,18},{10... | collective-permute-start | bytes 393224 | tf_op jit(solution)/shard_map/ppermute | solution.py:240
  18.7 7.8 %collective-permute-start.5 = (f32[16,2048]{1,0:T(8,128)}, f32[16,2048]{1,0:T(8,128)S(1)}, u32[]{:S(2)}, u32[]{:S(2)}) collective-permute-start(f32[16,2048]{1,0:T(8,128)} %param.21), channel_id=1, source_target_pairs={{0,24},{8,16},{16,8},{24,0},{1,25},{9,17},{17,9},{25,1},{2,26},{10... | collective-permute-start | bytes 393224 | tf_op jit(solution)/shard_map/ppermute | solution.py:240
  27.7 13.5 %collective-permute-start.10 = (f32[64,2048]{1,0:T(8,128)S(1)}, f32[64,2048]{1,0:T(8,128)S(1)}, u32[]{:S(2)}, u32[]{:S(2)}) collective-permute-start(f32[64,2048]{1,0:T(8,128)S(1)} %get-tuple-element.66.rest_4_), channel_id=1, source_target_pairs={{0,64},{32,96},{64,0},{96,32},{1,65},{33,97},{65,1},{97,33},{2,66}... | collective-permute-start | bytes 1572872 | tf_op jit(solution)/shard_map/ppermute | solution.py:240
  28.8 34.3 %collective-permute-start.11 = (f32[64,2048]{1,0:T(8,128)S(1)}, f32[64,2048]{1,0:T(8,128)S(1)}, u32[]{:S(2)}, u32[]{:S(2)}) collective-permute-start(f32[64,2048]{1,0:T(8,128)S(1)} %get-tuple-element.66.rest_4_), channel_id=1, source_target_pairs={{0,96},{32,64},{64,32},{96,0},{1,97},{33,65},{65,33},{97,1},{2,98}... | collective-permute-start | bytes 1572872 | tf_op jit(solution)/shard_map/ppermute | solution.py:240
  30.3 32.9 %collective-permute-start.6 = (f32[64,2048]{1,0:T(8,128)S(1)}, f32[64,2048]{1,0:T(8,128)S(1)}, u32[]{:S(2)}, u32[]{:S(2)}) collective-permute-start(f32[64,2048]{1,0:T(8,128)S(1)} %get-tuple-element.62.rest_0_), channel_id=1, source_target_pairs={{0,8},{8,0},{16,24},{24,16},{1,9},{9,1},{17,25},{25,17},{2,10},{10... | collective-permute-start | bytes 1572872 | tf_op jit(solution)/shard_map/ppermute | solution.py:240
  30.3 33.7 %collective-permute-start.7 = (f32[64,2048]{1,0:T(8,128)S(1)}, f32[64,2048]{1,0:T(8,128)S(1)}, u32[]{:S(2)}, u32[]{:S(2)}) collective-permute-start(f32[64,2048]{1,0:T(8,128)S(1)} %get-tuple-element.62.rest_0_), channel_id=1, source_target_pairs={{0,16},{8,24},{16,0},{24,8},{1,17},{9,25},{17,1},{25,9},{2,18},{10... | collective-permute-start | bytes 1572872 | tf_op jit(solution)/shard_map/ppermute | solution.py:240
  32.5 32.3 %collective-permute-start.8 = (f32[64,2048]{1,0:T(8,128)S(1)}, f32[64,2048]{1,0:T(8,128)}, u32[]{:S(2)}, u32[]{:S(2)}) collective-permute-start(f32[64,2048]{1,0:T(8,128)S(1)} %get-tuple-element.62.rest_0_), channel_id=1, source_target_pairs={{0,24},{8,16},{16,8},{24,0},{1,25},{9,17},{17,9},{25,1},{2,26},{10... | collective-permute-start | bytes 1572872 | tf_op jit(solution)/shard_map/ppermute | solution.py:240
  41.3 23.5 %collective-permute-start.9 = (f32[64,2048]{1,0:T(8,128)S(1)}, f32[64,2048]{1,0:T(8,128)}, u32[]{:S(2)}, u32[]{:S(2)}) collective-permute-start(f32[64,2048]{1,0:T(8,128)S(1)} %get-tuple-element.66.rest_4_), channel_id=1, source_target_pairs={{0,32},{32,0},{64,96},{96,64},{1,33},{33,1},{65,97},{97,65},{2,34}... | collective-permute-start | bytes 1572872 | tf_op jit(solution)/shard_map/ppermute | solution.py:240
  57.3 41.8 %all-to-all-start = ((f32[16,16,2048]{2,1,0:T(8,128)}), f32[16,16,2048]{2,1,0:T(8,128)}, u32[]{:S(2)}, u32[]{:S(2)}) async-start(f32[16,16,2048]{2,1,0:T(8,128)} %band_products.1), calls=%async_computation | async-start | bytes 4194304 | tf_op jit(solution)/shard_map/all_to_all | solution.py:313
  63.1 66.1 %reduce-scatter.2.cloned.1.call-start = ((), (), s32[]{:S(2)}) async-start(), calls=%async_computation.3 | async-start | bytes 1179648 | tf_op jit(solution)/shard_map/reduce_scatter | solution.py:317
  87.5 8.5 %collective-permute-start.14 = (f32[64,512]{1,0:T(8,128)S(1)}, f32[64,512]{1,0:T(8,128)S(1)}, u32[]{:S(2)}, u32[]{:S(2)}) collective-permute-start(f32[64,512]{1,0:T(8,128)S(1)} %get-tuple-element.101), channel_id=1, source_target_pairs={{0,4},{2,6},{4,0},{6,2},{1,5},{3,7},{5,1},{7,3},{8,12},{10,14},{12... | collective-permute-start | bytes 393224 | tf_op jit(solution)/shard_map/ppermute | solution.py:240
  90.0 9.1 %collective-permute-start.15 = (f32[64,512]{1,0:T(8,128)S(1)}, f32[64,512]{1,0:T(8,128)S(1)}, u32[]{:S(2)}, u32[]{:S(2)}) collective-permute-start(f32[64,512]{1,0:T(8,128)S(1)} %get-tuple-element.100), channel_id=1, source_target_pairs={{0,6},{2,4},{4,2},{6,0},{1,7},{3,5},{5,3},{7,1},{8,14},{10,12},{12... | collective-permute-start | bytes 393224 | tf_op jit(solution)/shard_map/ppermute | solution.py:240
  102.8 7.4 %collective-permute-start.17 = (f32[64,512]{1,0:T(8,128)S(1)}, f32[64,512]{1,0:T(8,128)S(1)}, u32[]{:S(2)}, u32[]{:S(2)}) collective-permute-start(f32[64,512]{1,0:T(8,128)S(1)} %add_add_fusion.2), channel_id=1, source_target_pairs={{0,16},{8,24},{16,0},{24,8},{1,17},{9,25},{17,1},{25,9},{2,18},{10... | collective-permute-start | bytes 393224 | tf_op jit(solution)/shard_map/ppermute | solution.py:240
  105.2 8.0 %collective-permute-start.18 = (f32[64,512]{1,0:T(8,128)S(1)}, f32[64,512]{1,0:T(8,128)S(1)}, u32[]{:S(2)}, u32[]{:S(2)}) collective-permute-start(f32[64,512]{1,0:T(8,128)S(1)} %add_add_fusion.2), channel_id=1, source_target_pairs={{0,24},{8,16},{16,8},{24,0},{1,25},{9,17},{17,9},{25,1},{2,26},{10... | collective-permute-start | bytes 393224 | tf_op jit(solution)/shard_map/ppermute | solution.py:240
  113.2 8.2 %collective-permute-start.19 = (f32[64,512]{1,0:T(8,128)S(1)}, f32[64,512]{1,0:T(8,128)S(1)}, u32[]{:S(2)}, u32[]{:S(2)}) collective-permute-start(f32[64,512]{1,0:T(8,128)S(1)} %add_add_fusion.1), channel_id=1, source_target_pairs={{0,32},{32,0},{64,96},{96,64},{1,33},{33,1},{65,97},{97,65},{2,34}... | collective-permute-start | bytes 393224 | tf_op jit(solution)/shard_map/ppermute | solution.py:240
  114.3 7.2 %collective-permute-start.20 = (f32[64,512]{1,0:T(8,128)S(1)}, f32[64,512]{1,0:T(8,128)S(1)}, u32[]{:S(2)}, u32[]{:S(2)}) collective-permute-start(f32[64,512]{1,0:T(8,128)S(1)} %add_add_fusion.1), channel_id=1, source_target_pairs={{0,64},{32,96},{64,0},{96,32},{1,65},{33,97},{65,1},{97,33},{2,66}... | collective-permute-start | bytes 393224 | tf_op jit(solution)/shard_map/ppermute | solution.py:240
  116.4 8.5 %collective-permute-start.21 = (f32[64,512]{1,0:T(8,128)S(1)}, f32[64,512]{1,0:T(8,128)S(1)}, u32[]{:S(2)}, u32[]{:S(2)}) collective-permute-start(f32[64,512]{1,0:T(8,128)S(1)} %add_add_fusion.1), channel_id=1, source_target_pairs={{0,96},{32,64},{64,32},{96,0},{1,97},{33,65},{65,33},{97,1},{2,98}... | collective-permute-start | bytes 393224 | tf_op jit(solution)/shard_map/ppermute | solution.py:240
  117.3 8.0 %collective-permute-start.23 = (f32[8,2048]{1,0:T(8,128)S(1)}, f32[8,2048]{1,0:T(8,128)S(1)}, u32[]{:S(2)}, u32[]{:S(2)}) collective-permute-start(f32[8,2048]{1,0:T(8,128)S(1)} %get-tuple-element.73), channel_id=1, source_target_pairs={{0,16},{8,24},{16,0},{24,8},{1,17},{9,25},{17,1},{25,9},{2,18},{10... | collective-permute-start | bytes 196616 | tf_op jit(solution)/shard_map/ppermute | solution.py:240
  129.2 8.2 %collective-permute-start.35 = (f32[64,512]{1,0:T(8,128)S(1)}, f32[64,512]{1,0:T(8,128)S(1)}, u32[]{:S(2)}, u32[]{:S(2)}) collective-permute-start(f32[64,512]{1,0:T(8,128)S(1)} %add_add_fusion), channel_id=1, source_target_pairs={{0,4},{2,6},{4,0},{6,2},{1,5},{3,7},{5,1},{7,3},{8,12},{10,14},{12... | collective-permute-start | bytes 393224 | tf_op jit(solution)/shard_map/ppermute | solution.py:240
  130.3 7.1 %collective-permute-start.36 = (f32[64,512]{1,0:T(8,128)S(1)}, f32[64,512]{1,0:T(8,128)S(1)}, u32[]{:S(2)}, u32[]{:S(2)}) collective-permute-start(f32[64,512]{1,0:T(8,128)S(1)} %add_add_fusion), channel_id=1, source_target_pairs={{0,6},{2,4},{4,2},{6,0},{1,7},{3,5},{5,3},{7,1},{8,14},{10,12},{12... | collective-permute-start | bytes 393224 | tf_op jit(solution)/shard_map/ppermute | solution.py:240
  133.2 12.8 %collective-permute-start.31 = (f32[32,2048]{1,0:T(8,128)S(1)}, f32[32,2048]{1,0:T(8,128)S(1)}, u32[]{:S(2)}, u32[]{:S(2)}) collective-permute-start(f32[32,2048]{1,0:T(8,128)S(1)} %constant_dynamic-update-slice_fusion.14), channel_id=1, source_target_pairs={{0,8},{8,0},{16,24},{24,16},{1,9},{9,1},{17,25},{25,17},{2,10},{10... | collective-permute-start | bytes 786440 | tf_op jit(solution)/shard_map/ppermute | solution.py:240
  133.3 24.1 %collective-permute-start.32 = (f32[32,2048]{1,0:T(8,128)S(1)}, f32[32,2048]{1,0:T(8,128)S(1)}, u32[]{:S(2)}, u32[]{:S(2)}) collective-permute-start(f32[32,2048]{1,0:T(8,128)S(1)} %constant_dynamic-update-slice_fusion.14), channel_id=1, source_target_pairs={{0,16},{8,24},{16,0},{24,8},{1,17},{9,25},{17,1},{25,9},{2,18},{10... | collective-permute-start | bytes 786440 | tf_op jit(solution)/shard_map/ppermute | solution.py:240
  135.9 21.5 %collective-permute-start.33 = (f32[32,2048]{1,0:T(8,128)S(1)}, f32[32,2048]{1,0:T(8,128)S(1)}, u32[]{:S(2)}, u32[]{:S(2)}) collective-permute-start(f32[32,2048]{1,0:T(8,128)S(1)} %constant_dynamic-update-slice_fusion.14), channel_id=1, source_target_pairs={{0,24},{8,16},{16,8},{24,0},{1,25},{9,17},{17,9},{25,1},{2,26},{10... | collective-permute-start | bytes 786440 | tf_op jit(solution)/shard_map/ppermute | solution.py:240
  137.4 8.1 %collective-permute-start.37 = (f32[256,512]{1,0:T(8,128)S(1)}, f32[256,512]{1,0:T(8,128)S(1)}, u32[]{:S(2)}, u32[]{:S(2)}) collective-permute-start(f32[256,512]{1,0:T(8,128)S(1)} %constant_dynamic-update-slice_fusion.10), channel_id=1, source_target_pairs={{0,1},{1,0},{2,3},{3,2},{4,5},{5,4},{6,7},{7,6},{8,9},{9,8},{10,11... | collective-permute-start | bytes 1572872 | tf_op jit(solution)/shard_map/ppermute | solution.py:240
  144.0 13.4 %collective-permute-start.28 = (f32[32,2048]{1,0:T(8,128)S(1)}, f32[32,2048]{1,0:T(8,128)S(1)}, u32[]{:S(2)}, u32[]{:S(2)}) collective-permute-start(f32[32,2048]{1,0:T(8,128)S(1)} %constant_dynamic-update-slice_fusion.18), channel_id=1, source_target_pairs={{0,32},{32,0},{64,96},{96,64},{1,33},{33,1},{65,97},{97,65},{2,34}... | collective-permute-start | bytes 786440 | tf_op jit(solution)/shard_map/ppermute | solution.py:240
  145.5 12.2 %collective-permute-start.29 = (f32[32,2048]{1,0:T(8,128)S(1)}, f32[32,2048]{1,0:T(8,128)S(1)}, u32[]{:S(2)}, u32[]{:S(2)}) collective-permute-start(f32[32,2048]{1,0:T(8,128)S(1)} %constant_dynamic-update-slice_fusion.18), channel_id=1, source_target_pairs={{0,64},{32,96},{64,0},{96,32},{1,65},{33,97},{65,1},{97,33},{2,66}... | collective-permute-start | bytes 786440 | tf_op jit(solution)/shard_map/ppermute | solution.py:240
  146.0 14.4 %collective-permute-start.30 = (f32[32,2048]{1,0:T(8,128)S(1)}, f32[32,2048]{1,0:T(8,128)S(1)}, u32[]{:S(2)}, u32[]{:S(2)}) collective-permute-start(f32[32,2048]{1,0:T(8,128)S(1)} %constant_dynamic-update-slice_fusion.18), channel_id=1, source_target_pairs={{0,96},{32,64},{64,32},{96,0},{1,97},{33,65},{65,33},{97,1},{2,98}... | collective-permute-start | bytes 786440 | tf_op jit(solution)/shard_map/ppermute | solution.py:240
  (19 other events, 84.5 us)
Sparse Core Ops, SparseCore 0:
  10.3 28.7 all-gather.1
  84.7 31.1 reduce-scatter.1
where the time goes:
time: 170 us; the launch traced here: 169 us
  starting transfers between devices  62 us (36%)
  waiting for transfers between devices  42.4 us (25%)
  Pallas kernels  36.2 us (21%)
  between operations  14.6 us (9%)
  local copies, waits for them, and re-layouts  8.68 us (5%)
  other arithmetic  5.16 us (3%)
    ppermute x38, starting transfers between devices, swap(): return lax.ppermute(value, axis, [(i, i ^ step) for i in range(size)])  56.2 us
    ppermute x38, waiting for transfers between devices, swap(): return lax.ppermute(value, axis, [(i, i ^ step) for i in range(size)])  42.4 us
    pallas_call x1, Pallas kernels, panel_products(): pl.pallas_call(functools.partial(panel_kernel, count), out_shape=(jax.Sha...  14.7 us
    pallas_call x1, Pallas kernels, finish(): pl.pallas_call(finish_kernel, out_shape=(jax.ShapeDtypeStruct((width, wid...  8.77 us
    pallas_call x1, Pallas kernels, band_products(): pl.pallas_call(functools.partial(band_kernel, count), out_shape=jax.Shape...  8.35 us
    unnamed x20, local copies, waits for them, and re-layouts  6.67 us
    all_to_all x1, starting transfers between devices, body(): band = lax.all_to_all(band, row, 0, 0, tiled=True)  5.76 us
    pallas_call x1, Pallas kernels, prepare(): pl.pallas_call(prepare_kernel, out_shape=jax.ShapeDtypeStruct((6, width,...  4.38 us
  transfers between devices with their start and end apart: 41, of which 18 were waited for; matrix products, arithmetic and copies ran while one was open for 2% of the time, Pallas kernels for 21%

commit v1 on v0

v1 whole, which is shorter than its diff:
```python
import functools

import jax
import jax.numpy as jnp
from jax import lax
from jax.experimental import pallas as pl
from jax.experimental.pallas import tpu as pltpu
from jax.sharding import Mesh, PartitionSpec as P

HALF = jnp.bfloat16
FULL = jnp.float32
VMEM = pl.BlockSpec(memory_space=pltpu.VMEM)


def mul(left, right, dims):
    return lax.dot_general(left, right, (dims, ((), ())), preferred_element_type=FULL)


def parts(value):
    high = value.astype(HALF)
    return high, (value - high.astype(FULL)).astype(HALF)


def close(left, right, dims=((1,), (0,))):
    (lh, ll), (rh, rl) = left, right
    return mul(lh, rl, dims) + mul(ll, rh, dims) + mul(lh, rh, dims)


def times(left, right):
    return close(parts(left), parts(right))


def far(*arrays):
    return [pltpu.with_memory_space_constraint(a, pltpu.HBM) for a in arrays]


X_NEW, Y_NEW, U_PAIR, U_TRIPLE, L_PAIR, L_TRIPLE = range(6)


def prepare_kernel(lot, uol, ldn, udn, lin, uin, lio, uio, out):
    upper_pair = times(uol[...].T, uio[...].T)
    lower_pair = times(lio[...].T, lot[...].T)
    out[X_NEW] = times(ldn[...].T, lin[...].T)
    out[Y_NEW] = times(uin[...].T, udn[...].T)
    out[U_PAIR] = upper_pair
    out[L_PAIR] = lower_pair
    out[U_TRIPLE] = times(uin[...].T, upper_pair)
    out[L_TRIPLE] = times(lower_pair, lin[...].T)


def prepare(*factors):
    width = factors[0].shape[0]
    return pl.pallas_call(
        prepare_kernel,
        out_shape=jax.ShapeDtypeStruct((6, width, width), FULL),
        in_specs=[VMEM] * len(factors),
        out_specs=VMEM,
        name="prepare",
        cost_estimate=pl.CostEstimate(
            flops=72 * width**3, bytes_accessed=56 * width**2, transcendentals=0
        ),
    )(*factors)


def lower_rows(lower, panel, count, piece):
    return jnp.concatenate(
        [
            lower[pl.ds((2 * k + panel) * piece, piece), :]
            for k in range(count)
        ],
        axis=0,
    )


def band_kernel(count, small, lio, lower, trail, out, weight_high, weight_low):
    width = lio.shape[0]
    piece = width // count

    @pl.when(pl.program_id(0) == 0)
    def _():
        new = parts(lower_rows(lower, 0, count, piece))
        old = parts(lower_rows(lower, 1, count, piece))
        weight = close(parts(small[0]), new) - close(parts(lio[...].T), old)
        high, low = parts(weight)
        weight_high[...] = high
        weight_low[...] = low

    band = close((weight_high[...], weight_low[...]), parts(trail[...]))
    size = out.shape[1]
    for k in range(out.shape[0]):
        out[k] = band[k * size : (k + 1) * size, :]


def band_products(small, lio, lower, trail, ranks, count, tile=512):
    rows, columns = trail.shape
    width = lio.shape[0]
    small, lio, lower, trail = far(small, lio, lower, trail)
    return pl.pallas_call(
        functools.partial(band_kernel, count),
        out_shape=jax.ShapeDtypeStruct((ranks, width // ranks, columns), FULL),
        grid=(columns // tile,),
        in_specs=[
            pl.BlockSpec((1, width, width), lambda j: (L_TRIPLE, 0, 0)),
            pl.BlockSpec((width, width), lambda j: (0, 0)),
            pl.BlockSpec((2 * width, rows), lambda j: (0, 0)),
            pl.BlockSpec((rows, tile), lambda j: (0, j)),
        ],
        out_specs=pl.BlockSpec((ranks, width // ranks, tile), lambda j: (0, 0, j)),
        scratch_shapes=[pltpu.VMEM((width, rows), HALF)] * 2,
        compiler_params=pltpu.CompilerParams(vmem_limit_bytes=24 << 20),
        name="band_products",
        cost_estimate=pl.CostEstimate(
            flops=6 * width * rows * columns,
            bytes_accessed=4 * (rows * columns + 2 * width * rows + width * columns),
            transcendentals=0,
        ),
    )(small, lio, lower, trail)


def panel_kernel(count, place, small, uio, lower, trail, *rest):
    pieces = rest[:8]
    mine, other, strip_out, upper_high, upper_low, side_high, side_low, inner = rest[8:]
    width = uio.shape[0]
    z, y, x, c = place[0], place[1], place[2], place[3]

    @pl.when(pl.program_id(0) == 0)
    def _():
        inner[...] = jnp.zeros_like(inner)
        high, low = parts(small[0])
        side_high[:width, :] = high
        side_low[:width, :] = low
        high, low = parts(-uio[...].T)
        side_high[width:, :] = high
        side_low[width:, :] = low
        for k in range(4):
            high, low = parts(pieces[k][...])
            chunk = high.shape[0] // 4
            for zz in range(4):
                at = pl.ds(pl.multiple_of((4 * zz + (y ^ k)) * chunk, chunk), chunk)
                upper_high[at, :] = high[zz * chunk : (zz + 1) * chunk, :]
                upper_low[at, :] = low[zz * chunk : (zz + 1) * chunk, :]
            high, low = parts(pieces[4 + k][...])
            size = high.shape[0]
            at = pl.ds(pl.multiple_of(width + (z ^ k) * size, size), size)
            upper_high[at, :] = high
            upper_low[at, :] = low

    product = close(parts(trail[...]), (upper_high[...], upper_low[...]), ((1,), (1,)))
    product = parts(product)
    strip = close(product, (side_high[...], side_low[...]))
    strip_out[...] = strip
    piece = width // count
    for panel in range(2):
        left = parts(lower_rows(lower, panel, count, piece))
        inner[panel * width : (panel + 1) * width, :] += close(left, product)

    @pl.when(pl.program_id(0) == pl.num_programs(0) - 1)
    def _():
        rows, share = mine.shape[2], width // 4
        for k in range(4):
            for p in range(mine.shape[1]):
                start, column = (x ^ k) * share + rows * (p // 2), width * (p % 2)
                near = pl.ds(pl.multiple_of(c * width + start, rows), rows)
                beside = pl.ds(pl.multiple_of((1 - c) * width + start, rows), rows)
                mine[k, p] = inner[near, column : column + width]
                other[k, p] = inner[beside, column : column + width]


def panel_products(place, small, uio, lower, trail, pieces, count, tile=256):
    rows, columns = trail.shape
    width = uio.shape[0]
    once = pl.Buffered(1)
    size = pieces[0].shape[0]
    share = (4, 16, width // 32, width)
    small, uio, lower, trail = far(small, uio, lower, trail)
    return pl.pallas_call(
        functools.partial(panel_kernel, count),
        out_shape=(
            jax.ShapeDtypeStruct(share, FULL),
            jax.ShapeDtypeStruct(share, FULL),
            jax.ShapeDtypeStruct((rows, width), FULL),
        ),
        grid_spec=pltpu.PrefetchScalarGridSpec(
            num_scalar_prefetch=1,
            grid=(rows // tile,),
            in_specs=[
                pl.BlockSpec((1, width, width), lambda i, p: (U_TRIPLE, 0, 0)),
                pl.BlockSpec((width, width), lambda i, p: (0, 0)),
                pl.BlockSpec((2 * width, tile), lambda i, p: (0, i)),
                pl.BlockSpec((tile, columns), lambda i, p: (i, 0)),
            ]
            + [pl.BlockSpec((size, columns), lambda i, p: (0, 0), pipeline_mode=once)] * 8,
            out_specs=(
                pl.BlockSpec(share, lambda i, p: (0, 0, 0, 0)),
                pl.BlockSpec(share, lambda i, p: (0, 0, 0, 0)),
                pl.BlockSpec((tile, width), lambda i, p: (i, 0)),
            ),
            scratch_shapes=[pltpu.VMEM((2 * width, columns), HALF)] * 2
            + [pltpu.VMEM((2 * width, width), HALF)] * 2
            + [pltpu.VMEM((2 * width, 2 * width), FULL)],
        ),
        compiler_params=pltpu.CompilerParams(vmem_limit_bytes=36 << 20),
        name="panel_products",
        cost_estimate=pl.CostEstimate(
            flops=3 * (4 * width * rows * columns + 12 * width * width * rows),
            bytes_accessed=4 * (rows * columns + 2 * width * columns + 4 * width * rows),
            transcendentals=0,
        ),
    )(place, small, uio, lower, trail, *pieces)


def finish_kernel(
    place,
    mine,
    other,
    small,
    lot,
    uol,
    lin,
    uin,
    ldo,
    udo,
    lio,
    uio,
    corner_out,
    top_out,
    left_out,
    inner,
):
    width = lin.shape[0]
    c = place[3]
    rows, share = mine.shape[2], width // 4
    for k in range(4):
        for p in range(mine.shape[1]):
            start, column = k * share + rows * (p // 2), width * (p % 2)
            near = pl.ds(pl.multiple_of(c * width + start, rows), rows)
            beside = pl.ds(pl.multiple_of((1 - c) * width + start, rows), rows)
            inner[near, column : column + width] = mine[k, p]
            inner[beside, column : column + width] = other[k, p]
    row = lax.broadcasted_iota(jnp.int32, (width, width), 0)
    column = lax.broadcasted_iota(jnp.int32, (width, width), 1)
    below = row > column
    g11, g12 = inner[:width, :width], inner[:width, width:]
    g21, g22 = inner[width:, :width], inner[width:, width:]
    lin_t, uin_t, lio_t, uio_t = lin[...].T, uin[...].T, lio[...].T, uio[...].T
    inside = jnp.where(below, times(small[X_NEW], g11), times(g11, small[Y_NEW]))
    corner = times(times(lin_t, inside), uin_t)
    top = times(times(lin_t, g12), uio_t) - times(corner, small[U_PAIR])
    left = times(lio_t, times(g21, uin_t)) - times(small[L_PAIR], corner)
    top_out[...] = top
    left_out[...] = left
    outer = times(small[L_TRIPLE], g12) - times(lio_t, g22)
    under = times(g21, small[U_TRIPLE]) - times(g22, uio_t)
    lower_grad = -(times(left, uol[...].T) + outer)
    upper_grad = -(times(lot[...].T, top) + under)
    inside = jnp.where(
        below, times(ldo[...].T, lower_grad), times(upper_grad, udo[...].T)
    )
    corner_out[...] = times(times(lio_t, inside), uio_t)


def finish(place, mine, other, small, *factors):
    width = factors[0].shape[0]
    return pl.pallas_call(
        finish_kernel,
        out_shape=(jax.ShapeDtypeStruct((width, width), FULL),) * 3,
        in_specs=[pl.BlockSpec(memory_space=pltpu.SMEM)] + [VMEM] * (3 + len(factors)),
        out_specs=(VMEM,) * 3,
        scratch_shapes=[pltpu.VMEM((2 * width, 2 * width), FULL)],
        name="finish",
        cost_estimate=pl.CostEstimate(
            flops=240 * width**3, bytes_accessed=84 * width**2, transcendentals=0
        ),
    )(place, mine, other, small, *factors)


def swap(value, axis, step):
    size = lax.axis_size(axis)
    return lax.ppermute(value, axis, [(i, i ^ step) for i in range(size)])


def exchange(value, axes):
    return lax.all_to_all(value, axes, 0, 0, tiled=True)


def pieces_of(value, axis):
    return [value] + [swap(value, axis, step) for step in range(1, lax.axis_size(axis))]


def placed(pieces, axis):
    me = lax.axis_index(axis)
    size = pieces[0].shape[0]
    out = jnp.zeros((len(pieces) * size, *pieces[0].shape[1:]), pieces[0].dtype)
    for step, piece in enumerate(pieces):
        out = lax.dynamic_update_slice_in_dim(out, piece, (me ^ step) * size, 0)
    return out


def together(*values):
    return lax.optimization_barrier(values)


def body(
    trail,
    lower_new,
    upper_new,
    lot,
    lower_old,
    uol,
    upper_old,
    ldn,
    udn,
    lin,
    uin,
    ldo,
    udo,
    lio,
    uio,
):
    row, col = ("z", "y"), ("x", "c")
    count = lax.axis_size(col)
    ranks = lax.axis_size(row)

    lower_mine = jnp.concatenate((lower_new.T, lower_old.T), axis=0)
    lower_stack = lax.all_gather(lower_mine, col, axis=0, tiled=True)
    small = prepare(lot, uol, ldn, udn, lin, uin, lio, uio)
    *near, small = together(*pieces_of(upper_new, "z"), *pieces_of(upper_old, "y"), small)
    near_new, near_old = together(placed(near[:4], "z"), placed(near[4:], "y"))
    pieces = pieces_of(near_new, "y") + pieces_of(near_old, "z")

    band = band_products(small, lio, lower_stack, trail, ranks, count)
    *pieces, _ = together(*pieces, band)
    band = lax.all_to_all(band, row, 0, 0, tiled=True)

    place = jnp.stack([lax.axis_index(a) for a in row + col]).astype(jnp.int32)
    mine, other, strip = panel_products(
        place, small, uio, lower_stack, trail, pieces, count
    )
    mine = mine + swap(other, "c", 1)
    mine = mine[0] + sum(swap(mine[k], "x", k) for k in (1, 2, 3))
    mine, band = together(mine, band.sum(0))
    band_right = lax.all_gather(band, row, axis=0, tiled=True)
    mine = exchange(mine, row).sum(0)
    mine = exchange(jnp.broadcast_to(mine[None], (ranks, *mine.shape)), row)
    mine = exchange(jnp.broadcast_to(mine[None], (4, *mine.shape)), "x")
    mine, strip = together(mine, strip)
    strip = exchange(strip.reshape(count, -1, strip.shape[1]), col)
    other = swap(mine, "c", 1)
    corner_old, strip_top, band_left = finish(
        place, mine, other, small, lot, uol, lin, uin, ldo, udo, lio, uio
    )
    strip_bottom, corner_old = together(strip, corner_old)
    return corner_old, strip_top, strip_bottom.sum(0), band_left, band_right


def solution(mesh):
    fine = Mesh(mesh.devices.reshape(4, 4, 4, 2), ("z", "y", "x", "c"))
    row, col = ("z", "y"), ("x", "c")
    split, whole = P(row, col), P()
    return jax.shard_map(
        body,
        mesh=fine,
        in_specs=(split, split, split, whole, split, whole, split) + (whole,) * 8,
        out_specs=(whole, whole, P(row + col, None), whole, P(None, col)),
        check_vma=False,
    )
```

time: 170 us -> 158 us (0.929)
  blocking collectives: 0 us -> 32.8 us
  starting transfers between devices: 62 us -> 37.4 us
  waiting for transfers between devices: 42.4 us -> 28.8 us
  local copies, waits for them, and re-layouts: 8.68 us -> 4.22 us
    all_to_all x0 -> x3, blocking collectives: none -> 32.8 us  [exchange(): return lax.all_to_all(value, axes, 0, 0, tiled=True)]
    ppermute x38 -> x17, starting transfers between devices: 56.2 us -> 23.5 us  [swap(): return lax.ppermute(value, axis, [(i, i ^ step) for i in range(size)])]
    ppermute x38 -> x17, waiting for transfers between devices: 42.4 us -> 22.7 us  [swap(): return lax.ppermute(value, axis, [(i, i ^ step) for i in range(size)])]
    all_to_all x0 -> x1, starting transfers between devices: none -> 8.2 us  [exchange(): return lax.all_to_all(value, axes, 0, 0, tiled=True)]
    all_to_all x0 -> x1, waiting for transfers between devices: none -> 6.1 us  [exchange(): return lax.all_to_all(value, axes, 0, 0, tiled=True)]
    unnamed x20 -> x11, local copies, waits for them, and re-layouts: 6.67 us -> 3.95 us
    pallas_call x1, Pallas kernels: 8.77 us -> 6.3 us  [finish(): pl.pallas_call(finish_kernel, out_shape=(jax.ShapeDtypeStruct((width, wid...]
  transfers between devices with their start and end apart: 41 -> 21, of which waited for: 18 -> 10; matrix products, arithmetic and copies ran while one was open for 2% -> 1% of each run, Pallas kernels for 21% -> 22%
where the time goes in v1:
time: 158 us; the launch traced here: 157 us
  starting transfers between devices  37.4 us (24%)
  Pallas kernels  34.6 us (22%)
  blocking collectives  32.8 us (21%)
  waiting for transfers between devices  28.8 us (18%)
  between operations  14.2 us (9%)
  other arithmetic  4.97 us (3%)
  local copies, waits for them, and re-layouts  4.22 us (3%)
    all_to_all x3, blocking collectives, exchange(): return lax.all_to_all(value, axes, 0, 0, tiled=True)  32.8 us
    ppermute x17, starting transfers between devices, swap(): return lax.ppermute(value, axis, [(i, i ^ step) for i in range(size)])  23.5 us
    ppermute x17, waiting for transfers between devices, swap(): return lax.ppermute(value, axis, [(i, i ^ step) for i in range(size)])  22.7 us
    pallas_call x1, Pallas kernels, panel_products(): pl.pallas_call(functools.partial(panel_kernel, count), out_shape=(jax.Sha...  15.2 us
    pallas_call x1, Pallas kernels, band_products(): pl.pallas_call(functools.partial(band_kernel, count), out_shape=jax.Shape...  9.16 us
    all_to_all x1, starting transfers between devices, exchange(): return lax.all_to_all(value, axes, 0, 0, tiled=True)  8.2 us
    pallas_call x1, Pallas kernels, finish(): pl.pallas_call(finish_kernel, out_shape=(jax.ShapeDtypeStruct((width, wid...  6.3 us
    all_to_all x1, waiting for transfers between devices, exchange(): return lax.all_to_all(value, axes, 0, 0, tiled=True)  6.1 us
  transfers between devices with their start and end apart: 21, of which 10 were waited for; matrix products, arithmetic and copies ran while one was open for 1% of the time, Pallas kernels for 22%

profile of v1, /device:TPU:1, one launch (start us, length us, event | category | flops | bytes accessed | tf_op | source)
XLA Modules:
  0.0 157.0 jit_solution(4608337596086623781)
XLA Ops:
  7.2 1.7 %pad_maximum_fusion = f32[64,1024]{1,0:T(8,128)} fusion(f32[32,1024]{1,0:T(8,128)} %bitcast.17, f32[32,1024]{1,0:T(8,128)} %bitcast.18), kind=kLoop, calls=%fused_computation | loop fusion | flops 65536 | bytes 524288 | tf_op jit(solution)/shard_map/concatenate | solution.py:324
  8.9 2.5 %collective-permute-start = (f32[16,2048]{1,0:T(8,128)}, f32[16,2048]{1,0:T(8,128)S(1)}, u32[]{:S(2)}, u32[]{:S(2)}) collective-permute-start(f32[16,2048]{1,0:T(8,128)} %param.17), channel_id=1, source_target_pairs={{0,32},{32,0},{64,96},{96,64},{1,33},{33,1},{65,97},{97,65},{2,34}... | collective-permute-start | bytes 393224 | tf_op jit(solution)/shard_map/ppermute | solution.py:279
  11.5 3.3 %collective-permute-start.1 = (f32[16,2048]{1,0:T(8,128)}, f32[16,2048]{1,0:T(8,128)S(1)}, u32[]{:S(2)}, u32[]{:S(2)}) collective-permute-start(f32[16,2048]{1,0:T(8,128)} %param.17), channel_id=1, source_target_pairs={{0,64},{32,96},{64,0},{96,32},{1,65},{33,97},{65,1},{97,33},{2,66}... | collective-permute-start | bytes 393224 | tf_op jit(solution)/shard_map/ppermute | solution.py:279
  14.8 1.3 collective-permute-start.3
  16.1 2.6 %collective-permute-start.4 = (f32[16,2048]{1,0:T(8,128)}, f32[16,2048]{1,0:T(8,128)S(1)}, u32[]{:S(2)}, u32[]{:S(2)}) collective-permute-start(f32[16,2048]{1,0:T(8,128)} %param.21), channel_id=1, source_target_pairs={{0,16},{8,24},{16,0},{24,8},{1,17},{9,25},{17,1},{25,9},{2,18},{10... | collective-permute-start | bytes 393224 | tf_op jit(solution)/shard_map/ppermute | solution.py:279
  18.7 3.9 %prepare.1.small = f32[6,256,256]{2,1,0:T(8,128)} custom-call(f32[256,256]{1,0:T(8,128)} %lot.3, f32[256,256]{1,0:T(8,128)} %uol.3, f32[256,256]{1,0:T(8,128)} %ldn.1, f32[256,256]{1,0:T(8,128)} %udn.1, f32[256,256]{1,0:T(8,128)} %lin.3, f32[256,256]{1,0:T(8,128)} %uin.3, f32[256,256]{1,0:T(8,128)} %lio.5, f32[256,256]{1,0:T(8,128)} %uio.5), custom_call_target="tpu_custom_call" | custom-call | flops 1207959552 | bytes 3670016 | tf_op jit(solution)/shard_map/prepare/pallas_call | solution.py:53
  23.7 2.8 %collective-permute-done.5 = f32[16,2048]{1,0:T(8,128)S(1)} collective-permute-done((f32[16,2048]{1,0:T(8,128)}, f32[16,2048]{1,0:T(8,128)S(1)}, u32[]{:S(2)}, u32[]{:S(2)}) %collective-permute-start.5) | collective-permute-done | bytes 131104 | tf_op jit(solution)/shard_map/ppermute | solution.py:279
  26.8 1.1 collective-permute-start.10
  27.9 1.5 collective-permute-start.11
  29.4 2.2 %collective-permute-start.7 = (f32[64,2048]{1,0:T(8,128)S(1)}, f32[64,2048]{1,0:T(8,128)S(1)}, u32[]{:S(2)}, u32[]{:S(2)}) collective-permute-start(f32[64,2048]{1,0:T(8,128)S(1)} %get-tuple-element.47.rest_0_), channel_id=1, source_target_pairs={{0,16},{8,24},{16,0},{24,8},{1,17},{9,25},{17,1},{25,9},{2,18},{10... | collective-permute-start | bytes 1572872 | tf_op jit(solution)/shard_map/ppermute | solution.py:279
  31.6 1.7 %collective-permute-start.8 = (f32[64,2048]{1,0:T(8,128)S(1)}, f32[64,2048]{1,0:T(8,128)}, u32[]{:S(2)}, u32[]{:S(2)}) collective-permute-start(f32[64,2048]{1,0:T(8,128)S(1)} %get-tuple-element.47.rest_0_), channel_id=1, source_target_pairs={{0,24},{8,16},{16,8},{24,0},{1,25},{9,17},{17,9},{25,1},{2,26},{10... | collective-permute-start | bytes 1572872 | tf_op jit(solution)/shard_map/ppermute | solution.py:279
  33.2 7.1 %collective-permute-done.10.rest_6_ = f32[64,2048]{1,0:T(8,128)S(1)} collective-permute-done((f32[64,2048]{1,0:T(8,128)S(1)}, f32[64,2048]{1,0:T(8,128)S(1)}, u32[]{:S(2)}, u32[]{:S(2)}) %collective-permute-start.10) | collective-permute-done | bytes 524320 | tf_op jit(solution)/shard_map/ppermute | solution.py:279
  40.6 9.2 %band_products.1 = f32[16,16,2048]{2,1,0:T(8,128)} custom-call(f32[6,256,256]{2,1,0:T(8,128)} %prepare.1.small, f32[256,256]{1,0:T(8,128)} %lio.5, f32[512,1024]{1,0:T(8,128)} %all-gather.3.cloned.1.call-done.lower, f32[1024,2048]{1,0:T(8,128)} %trail.3), custom_call_target="tpu_custom_call" | custom-call | flops 3221225472 | bytes 12582912 | tf_op jit(solution)/shard_map/band_products/pallas_call | solution.py:98
  49.8 5.6 %all-to-all-start = ((f32[16,16,2048]{2,1,0:T(8,128)}), f32[16,16,2048]{2,1,0:T(8,128)}, u32[]{:S(2)}, u32[]{:S(2)}) async-start(f32[16,16,2048]{2,1,0:T(8,128)} %band_products.1), calls=%async_computation | async-start | bytes 4194304 | tf_op jit(solution)/shard_map/all_to_all | solution.py:333
  55.6 15.2 %panel_products.1 = (f32[4,16,8,256]{3,2,1,0:T(8,128)S(1)}, f32[4,16,8,256]{3,2,1,0:T(8,128)S(1)}, f32[1024,256]{1,0:T(8,128)}) custom-call(s32[4]{0:T(128)S(1)} %pad_add_fusion.place, f32[6,256,256]{2,1,0:T(8,128)} %prepare.1.small, f32[256,256]{1,0:T(8,128)} %uio.5, f32[512,1024]{1,0:T(8,128)} %all-gather.3.cloned.1.call-done.lower, f32[1024,2048]{1,0:T(8,128)} %trail.3, ...), custom_call_target="tpu_custom_call" | custom-call | flops 8858370048 | bytes 16777216 | tf_op jit(solution)/shard_map/panel_products/pallas_call | solution.py:176
  70.8 2.9 %collective-permute-start.12 = (f32[4,16,8,256]{3,2,1,0:T(8,128)S(1)}, f32[4,16,8,256]{3,2,1,0:T(8,128)S(1)}, u32[]{:S(2)}, u32[]{:S(2)}) collective-permute-start(f32[4,16,8,256]{3,2,1,0:T(8,128)S(1)} %get-tuple-element.56), channel_id=1, source_target_pairs={{0,1},{1,0},{2,3},{3,2},{4,5},{5,4},{6,7},{7,6},{8,9},{9,8},{10,11... | collective-permute-start | bytes 1572872 | tf_op jit(solution)/shard_map/ppermute | solution.py:279
  73.7 1.5 collective-permute-done.12
  75.3 1.3 collective-permute-start.13
  76.6 2.5 %collective-permute-start.14 = (f32[16,8,256]{2,1,0:T(8,128)S(1)}, f32[16,8,256]{2,1,0:T(8,128)S(1)}, u32[]{:S(2)}, u32[]{:S(2)}) collective-permute-start(f32[16,8,256]{2,1,0:T(8,128)S(1)} %get-tuple-element.67), channel_id=1, source_target_pairs={{0,4},{2,6},{4,0},{6,2},{1,5},{3,7},{5,1},{7,3},{8,12},{10,14},{12... | collective-permute-start | bytes 393224 | tf_op jit(solution)/shard_map/ppermute | solution.py:279
  79.3 1.0 collective-permute-done.13
  80.2 5.1 %collective-permute-done.14 = f32[16,8,256]{2,1,0:T(8,128)S(1)} collective-permute-done((f32[16,8,256]{2,1,0:T(8,128)S(1)}, f32[16,8,256]{2,1,0:T(8,128)S(1)}, u32[]{:S(2)}, u32[]{:S(2)}) %collective-permute-start.14) | collective-permute-done | bytes 131104 | tf_op jit(solution)/shard_map/ppermute | solution.py:279
  85.3 2.4 %collective-permute-done.15 = f32[16,8,256]{2,1,0:T(8,128)S(1)} collective-permute-done((f32[16,8,256]{2,1,0:T(8,128)S(1)}, f32[16,8,256]{2,1,0:T(8,128)S(1)}, u32[]{:S(2)}, u32[]{:S(2)}) %collective-permute-start.15) | collective-permute-done | bytes 131104 | tf_op jit(solution)/shard_map/ppermute | solution.py:279
  87.7 2.4 %reduce_sum.27 = f32[16,2048]{1,0:T(8,128)} reduce(f32[16,16,2048]{2,1,0:T(8,128)} %all-to-all-done, f32[]{:T(128)} %constant.7.clone.1), dimensions={0}, to_apply=%region_0.0 | reduce | flops 491520 | bytes 2228228 | tf_op jit(solution)/shard_map/reduce_sum | solution.py:341
  90.1 13.5 %all_to_all.27 = f32[16,8,256]{2,1,0:T(8,128)S(1)} all-to-all(f32[16,8,256]{2,1,0:T(8,128)S(1)} %fusion), channel_id=1, replica_groups=mesh['z'=4,'y'=4,'x'=4,'c'=2] {'z','y'}, dimensions={0} | all-to-all | bytes 262144 | tf_op jit(solution)/shard_map/all_to_all | solution.py:283
  103.7 9.9 %all_to_all.25 = f32[16,8,256]{2,1,0:T(8,128)S(1)} all-to-all(f32[16,8,256]{2,1,0:T(8,128)S(1)} %broadcast_in_dim.4), channel_id=1, replica_groups=mesh['z'=4,'y'=4,'x'=4,'c'=2] {'z','y'}, dimensions={0} | all-to-all | bytes 262144 | tf_op jit(solution)/shard_map/all_to_all | solution.py:283
  113.6 9.3 %all_to_all.26.mine = f32[4,16,8,256]{3,2,1,0:T(8,128)S(1)} all-to-all(f32[4,16,8,256]{3,2,1,0:T(8,128)S(1)} %broadcast_in_dim.5), channel_id=1, replica_groups=mesh['z'=4,'y'=4,'x'=4,'c'=2] {'x'}, dimensions={0} | all-to-all | bytes 1048576 | tf_op jit(solution)/shard_map/all_to_all | solution.py:283
  123.0 8.2 %all-to-all-start.4 = ((f32[8,128,256]{2,1,0:T(8,128)}), f32[8,128,256]{2,1,0:T(8,128)S(1)}, u32[]{:S(2)}, u32[]{:S(2)}) async-start(f32[8,128,256]{2,1,0:T(8,128)} %bitcast.10), calls=%async_computation.4 | async-start | bytes 2097152 | tf_op jit(solution)/shard_map/all_to_all | solution.py:283
  131.4 1.7 %collective-permute-done.16.other = f32[4,16,8,256]{3,2,1,0:T(8,128)S(1)} collective-permute-done((f32[4,16,8,256]{3,2,1,0:T(8,128)S(1)}, f32[4,16,8,256]{3,2,1,0:T(8,128)S(1)}, u32[]{:S(2)}, u32[]{:S(2)}) %collective-permute-start.16) | collective-permute-done | bytes 524320 | tf_op jit(solution)/shard_map/ppermute | solution.py:279
  133.1 0.8 copy-done.4
  133.9 6.3 %finish.1 = (f32[256,256]{1,0:T(8,128)}, f32[256,256]{1,0:T(8,128)}, f32[256,256]{1,0:T(8,128)}) custom-call(s32[4]{0:T(128)} %copy-done, f32[4,16,8,256]{3,2,1,0:T(8,128)} %copy-done.1, f32[4,16,8,256]{3,2,1,0:T(8,128)} %copy-done.4, f32[6,256,256]{2,1,0:T(8,128)} %prepare.1.small, f32[256,256]{1,0:T(8,128)} %lot.3, f32[256,256]{1,0:T(8,128)} %uol.3, ...), custom_call_target="tpu_custom_call" | custom-call | flops 4026531840 | bytes 5505024 | tf_op jit(solution)/shard_map/finish/pallas_call | solution.py:264
  140.2 6.1 %all-to-all-done.4 = f32[8,128,256]{2,1,0:T(8,128)S(1)} async-done(((f32[8,128,256]{2,1,0:T(8,128)}), f32[8,128,256]{2,1,0:T(8,128)S(1)}, u32[]{:S(2)}, u32[]{:S(2)}) %all-to-all-start.4) | async-done | bytes 1048608 | tf_op jit(solution)/shard_map/all_to_all | solution.py:283
  147.0 3.1 %copy.32 = f32[256,2048]{1,0:T(8,128)} copy(f32[256,2048]{1,0:T(8,128)} %all-gather.5.cloned.1.call-done) | data formatting | bytes 4194304
  (49 shorter events, 3.0 us)
Async XLA Ops:
  7.2 33.4 %all-gather.3.cloned.1.call-start = ((), (), s32[]{:S(2)}) async-start(), calls=%async_computation.5 | async-start | bytes 2359296 | tf_op jit(solution)/shard_map/all_gather | solution.py:325
  8.9 9.8 %collective-permute-start = (f32[16,2048]{1,0:T(8,128)}, f32[16,2048]{1,0:T(8,128)S(1)}, u32[]{:S(2)}, u32[]{:S(2)}) collective-permute-start(f32[16,2048]{1,0:T(8,128)} %param.17), channel_id=1, source_target_pairs={{0,32},{32,0},{64,96},{96,64},{1,33},{33,1},{65,97},{97,65},{2,34}... | collective-permute-start | bytes 393224 | tf_op jit(solution)/shard_map/ppermute | solution.py:279
  11.5 11.2 %collective-permute-start.1 = (f32[16,2048]{1,0:T(8,128)}, f32[16,2048]{1,0:T(8,128)S(1)}, u32[]{:S(2)}, u32[]{:S(2)}) collective-permute-start(f32[16,2048]{1,0:T(8,128)} %param.17), channel_id=1, source_target_pairs={{0,64},{32,96},{64,0},{96,32},{1,65},{33,97},{65,1},{97,33},{2,66}... | collective-permute-start | bytes 393224 | tf_op jit(solution)/shard_map/ppermute | solution.py:279
  14.8 8.4 %collective-permute-start.2 = (f32[16,2048]{1,0:T(8,128)}, f32[16,2048]{1,0:T(8,128)S(1)}, u32[]{:S(2)}, u32[]{:S(2)}) collective-permute-start(f32[16,2048]{1,0:T(8,128)} %param.17), channel_id=1, source_target_pairs={{0,96},{32,64},{64,32},{96,0},{1,97},{33,65},{65,33},{97,1},{2,98}... | collective-permute-start | bytes 393224 | tf_op jit(solution)/shard_map/ppermute | solution.py:279
  14.8 8.4 %collective-permute-start.3 = (f32[16,2048]{1,0:T(8,128)}, f32[16,2048]{1,0:T(8,128)S(1)}, u32[]{:S(2)}, u32[]{:S(2)}) collective-permute-start(f32[16,2048]{1,0:T(8,128)} %param.21), channel_id=1, source_target_pairs={{0,8},{8,0},{16,24},{24,16},{1,9},{9,1},{17,25},{25,17},{2,10},{10... | collective-permute-start | bytes 393224 | tf_op jit(solution)/shard_map/ppermute | solution.py:279
  16.1 7.6 %collective-permute-start.4 = (f32[16,2048]{1,0:T(8,128)}, f32[16,2048]{1,0:T(8,128)S(1)}, u32[]{:S(2)}, u32[]{:S(2)}) collective-permute-start(f32[16,2048]{1,0:T(8,128)} %param.21), channel_id=1, source_target_pairs={{0,16},{8,24},{16,0},{24,8},{1,17},{9,25},{17,1},{25,9},{2,18},{10... | collective-permute-start | bytes 393224 | tf_op jit(solution)/shard_map/ppermute | solution.py:279
  18.7 7.8 %collective-permute-start.5 = (f32[16,2048]{1,0:T(8,128)}, f32[16,2048]{1,0:T(8,128)S(1)}, u32[]{:S(2)}, u32[]{:S(2)}) collective-permute-start(f32[16,2048]{1,0:T(8,128)} %param.21), channel_id=1, source_target_pairs={{0,24},{8,16},{16,8},{24,0},{1,25},{9,17},{17,9},{25,1},{2,26},{10... | collective-permute-start | bytes 393224 | tf_op jit(solution)/shard_map/ppermute | solution.py:279
  18.7 7.9 %copy-start.2 = (f32[16,2048]{1,0:T(8,128)S(1)}, f32[16,2048]{1,0:T(8,128)}, u32[]{:S(2)}) copy-start(f32[16,2048]{1,0:T(8,128)} %param.17) | copy-start | bytes 393220
  18.7 8.0 %copy-start.3 = (f32[16,2048]{1,0:T(8,128)S(1)}, f32[16,2048]{1,0:T(8,128)}, u32[]{:S(2)}) copy-start(f32[16,2048]{1,0:T(8,128)} %param.21) | copy-start | bytes 393220
  26.8 13.5 %collective-permute-start.10 = (f32[64,2048]{1,0:T(8,128)S(1)}, f32[64,2048]{1,0:T(8,128)S(1)}, u32[]{:S(2)}, u32[]{:S(2)}) collective-permute-start(f32[64,2048]{1,0:T(8,128)S(1)} %get-tuple-element.51.rest_4_), channel_id=1, source_target_pairs={{0,64},{32,96},{64,0},{96,32},{1,65},{33,97},{65,1},{97,33},{2,66}... | collective-permute-start | bytes 1572872 | tf_op jit(solution)/shard_map/ppermute | solution.py:279
  27.9 27.6 %collective-permute-start.11 = (f32[64,2048]{1,0:T(8,128)S(1)}, f32[64,2048]{1,0:T(8,128)S(1)}, u32[]{:S(2)}, u32[]{:S(2)}) collective-permute-start(f32[64,2048]{1,0:T(8,128)S(1)} %get-tuple-element.51.rest_4_), channel_id=1, source_target_pairs={{0,96},{32,64},{64,32},{96,0},{1,97},{33,65},{65,33},{97,1},{2,98}... | collective-permute-start | bytes 1572872 | tf_op jit(solution)/shard_map/ppermute | solution.py:279
  29.4 26.2 %collective-permute-start.6 = (f32[64,2048]{1,0:T(8,128)S(1)}, f32[64,2048]{1,0:T(8,128)S(1)}, u32[]{:S(2)}, u32[]{:S(2)}) collective-permute-start(f32[64,2048]{1,0:T(8,128)S(1)} %get-tuple-element.47.rest_0_), channel_id=1, source_target_pairs={{0,8},{8,0},{16,24},{24,16},{1,9},{9,1},{17,25},{25,17},{2,10},{10... | collective-permute-start | bytes 1572872 | tf_op jit(solution)/shard_map/ppermute | solution.py:279
  29.4 26.2 %collective-permute-start.7 = (f32[64,2048]{1,0:T(8,128)S(1)}, f32[64,2048]{1,0:T(8,128)S(1)}, u32[]{:S(2)}, u32[]{:S(2)}) collective-permute-start(f32[64,2048]{1,0:T(8,128)S(1)} %get-tuple-element.47.rest_0_), channel_id=1, source_target_pairs={{0,16},{8,24},{16,0},{24,8},{1,17},{9,25},{17,1},{25,9},{2,18},{10... | collective-permute-start | bytes 1572872 | tf_op jit(solution)/shard_map/ppermute | solution.py:279
  31.6 24.0 %collective-permute-start.8 = (f32[64,2048]{1,0:T(8,128)S(1)}, f32[64,2048]{1,0:T(8,128)}, u32[]{:S(2)}, u32[]{:S(2)}) collective-permute-start(f32[64,2048]{1,0:T(8,128)S(1)} %get-tuple-element.47.rest_0_), channel_id=1, source_target_pairs={{0,24},{8,16},{16,8},{24,0},{1,25},{9,17},{17,9},{25,1},{2,26},{10... | collective-permute-start | bytes 1572872 | tf_op jit(solution)/shard_map/ppermute | solution.py:279
  40.3 15.2 %collective-permute-start.9 = (f32[64,2048]{1,0:T(8,128)S(1)}, f32[64,2048]{1,0:T(8,128)}, u32[]{:S(2)}, u32[]{:S(2)}) collective-permute-start(f32[64,2048]{1,0:T(8,128)S(1)} %get-tuple-element.51.rest_4_), channel_id=1, source_target_pairs={{0,32},{32,0},{64,96},{96,64},{1,33},{33,1},{65,97},{97,65},{2,34}... | collective-permute-start | bytes 1572872 | tf_op jit(solution)/shard_map/ppermute | solution.py:279
  49.8 38.0 %all-to-all-start = ((f32[16,16,2048]{2,1,0:T(8,128)}), f32[16,16,2048]{2,1,0:T(8,128)}, u32[]{:S(2)}, u32[]{:S(2)}) async-start(f32[16,16,2048]{2,1,0:T(8,128)} %band_products.1), calls=%async_computation | async-start | bytes 4194304 | tf_op jit(solution)/shard_map/all_to_all | solution.py:333
  55.4 91.6 %all-gather.5.cloned.1.call-start = ((), (), s32[]{:S(2)}) async-start(), calls=%async_computation.6 | async-start | bytes 2228224 | tf_op jit(solution)/shard_map/all_gather | solution.py:342
  55.5 15.3 %copy-start = (s32[4]{0:T(128)}, s32[4]{0:T(128)S(1)}, u32[]{:S(2)}) copy-start(s32[4]{0:T(128)S(1)} %pad_add_fusion.place) | copy-start | bytes 52
  70.8 4.4 %collective-permute-start.12 = (f32[4,16,8,256]{3,2,1,0:T(8,128)S(1)}, f32[4,16,8,256]{3,2,1,0:T(8,128)S(1)}, u32[]{:S(2)}, u32[]{:S(2)}) collective-permute-start(f32[4,16,8,256]{3,2,1,0:T(8,128)S(1)} %get-tuple-element.56), channel_id=1, source_target_pairs={{0,1},{1,0},{2,3},{3,2},{4,5},{5,4},{6,7},{7,6},{8,9},{9,8},{10,11... | collective-permute-start | bytes 1572872 | tf_op jit(solution)/shard_map/ppermute | solution.py:279
  75.3 4.9 %collective-permute-start.13 = (f32[16,8,256]{2,1,0:T(8,128)S(1)}, f32[16,8,256]{2,1,0:T(8,128)S(1)}, u32[]{:S(2)}, u32[]{:S(2)}) collective-permute-start(f32[16,8,256]{2,1,0:T(8,128)S(1)} %get-tuple-element.69), channel_id=1, source_target_pairs={{0,2},{2,0},{4,6},{6,4},{1,3},{3,1},{5,7},{7,5},{8,10},{10,8},{12,... | collective-permute-start | bytes 393224 | tf_op jit(solution)/shard_map/ppermute | solution.py:279
  76.6 8.7 %collective-permute-start.14 = (f32[16,8,256]{2,1,0:T(8,128)S(1)}, f32[16,8,256]{2,1,0:T(8,128)S(1)}, u32[]{:S(2)}, u32[]{:S(2)}) collective-permute-start(f32[16,8,256]{2,1,0:T(8,128)S(1)} %get-tuple-element.67), channel_id=1, source_target_pairs={{0,4},{2,6},{4,0},{6,2},{1,5},{3,7},{5,1},{7,3},{8,12},{10,14},{12... | collective-permute-start | bytes 393224 | tf_op jit(solution)/shard_map/ppermute | solution.py:279
  79.1 8.6 %collective-permute-start.15 = (f32[16,8,256]{2,1,0:T(8,128)S(1)}, f32[16,8,256]{2,1,0:T(8,128)S(1)}, u32[]{:S(2)}, u32[]{:S(2)}) collective-permute-start(f32[16,8,256]{2,1,0:T(8,128)S(1)} %get-tuple-element.68), channel_id=1, source_target_pairs={{0,6},{2,4},{4,2},{6,0},{1,7},{3,5},{5,3},{7,1},{8,14},{10,12},{12... | collective-permute-start | bytes 393224 | tf_op jit(solution)/shard_map/ppermute | solution.py:279
  123.0 10.1 %copy-start.1 = (f32[4,16,8,256]{3,2,1,0:T(8,128)}, f32[4,16,8,256]{3,2,1,0:T(8,128)S(1)}, u32[]{:S(2)}) copy-start(f32[4,16,8,256]{3,2,1,0:T(8,128)S(1)} %all_to_all.26.mine) | copy-start | bytes 1572868
  123.0 23.3 %all-to-all-start.4 = ((f32[8,128,256]{2,1,0:T(8,128)}), f32[8,128,256]{2,1,0:T(8,128)S(1)}, u32[]{:S(2)}, u32[]{:S(2)}) async-start(f32[8,128,256]{2,1,0:T(8,128)} %bitcast.10), calls=%async_computation.4 | async-start | bytes 2097152 | tf_op jit(solution)/shard_map/all_to_all | solution.py:283
  131.2 1.9 %collective-permute-start.16 = (f32[4,16,8,256]{3,2,1,0:T(8,128)S(1)}, f32[4,16,8,256]{3,2,1,0:T(8,128)S(1)}, u32[]{:S(2)}, u32[]{:S(2)}) collective-permute-start(f32[4,16,8,256]{3,2,1,0:T(8,128)S(1)} %all_to_all.26.mine), channel_id=1, source_target_pairs={{0,1},{1,0},{2,3},{3,2},{4,5},{5,4},{6,7},{7,6},{8,9},{9,8},{10,11... | collective-permute-start | bytes 1572872 | tf_op jit(solution)/shard_map/ppermute | solution.py:279
  133.1 0.8 copy-start.4
Sparse Core Ops, SparseCore 0:
  10.3 28.7 all-gather.2
  90.2 43.7 all-gather.4

commit v2 on v1

v2 whole, which is shorter than its diff:
```python
import functools

import jax
import jax.numpy as jnp
from jax import lax
from jax.experimental import pallas as pl
from jax.experimental.pallas import tpu as pltpu
from jax.sharding import Mesh, PartitionSpec as P

HALF = jnp.bfloat16
FULL = jnp.float32
VMEM = pl.BlockSpec(memory_space=pltpu.VMEM)


def mul(left, right, dims):
    return lax.dot_general(left, right, (dims, ((), ())), preferred_element_type=FULL)


def parts(value):
    high = value.astype(HALF)
    return high, (value - high.astype(FULL)).astype(HALF)


def close(left, right, dims=((1,), (0,))):
    (lh, ll), (rh, rl) = left, right
    return mul(lh, rl, dims) + mul(ll, rh, dims) + mul(lh, rh, dims)


def times(left, right):
    return close(parts(left), parts(right))


def far(*arrays):
    return [pltpu.with_memory_space_constraint(a, pltpu.HBM) for a in arrays]


def prepare_kernel(lot, uol, ldn, udn, lin, uin, lio, uio, *out):
    x_new, y_new, upper_pair, upper_triple, lower_pair, lower_triple = out
    upper = times(uol[...].T, uio[...].T)
    lower = times(lio[...].T, lot[...].T)
    x_new[...] = times(ldn[...].T, lin[...].T)
    y_new[...] = times(uin[...].T, udn[...].T)
    upper_pair[...] = upper
    lower_pair[...] = lower
    upper_triple[...] = times(uin[...].T, upper)
    lower_triple[...] = times(lower, lin[...].T)


def prepare(*factors):
    width = factors[0].shape[0]
    return pl.pallas_call(
        prepare_kernel,
        out_shape=(jax.ShapeDtypeStruct((width, width), FULL),) * 6,
        in_specs=[VMEM] * len(factors),
        out_specs=(VMEM,) * 6,
        name="prepare",
        cost_estimate=pl.CostEstimate(
            flops=36 * width**3, bytes_accessed=56 * width**2, transcendentals=0
        ),
    )(*factors)


def lower_rows(lower, panel, count, piece):
    return jnp.concatenate(
        [
            lower[pl.ds((2 * k + panel) * piece, piece), :]
            for k in range(count)
        ],
        axis=0,
    )


def weight_kernel(count, triple, lio, lower, high, low):
    piece = lio.shape[0] // count
    new = parts(lower_rows(lower, 0, count, piece))
    old = parts(lower_rows(lower, 1, count, piece))
    high[...], low[...] = parts(close(parts(triple[...]), new) - close(parts(lio[...].T), old))


def band_weights(triple, lio, lower, count):
    width, rows = lio.shape[0], lower.shape[1]
    return pl.pallas_call(
        functools.partial(weight_kernel, count),
        out_shape=(jax.ShapeDtypeStruct((width, rows), HALF),) * 2,
        in_specs=[VMEM] * 3,
        out_specs=(VMEM,) * 2,
        compiler_params=pltpu.CompilerParams(vmem_limit_bytes=16 << 20),
        name="band_weights",
        cost_estimate=pl.CostEstimate(
            flops=12 * width * width * rows,
            bytes_accessed=12 * width * rows,
            transcendentals=0,
        ),
    )(triple, lio, lower)


def band_kernel(high, low, trail, out):
    size = out.shape[1]
    band = close((high[...], low[...]), parts(trail[...]))
    for k in range(out.shape[0]):
        out[k] = band[k * size : (k + 1) * size, :]


def band_products(high, low, trail, ranks, tile=256):
    rows, columns = trail.shape
    width = high.shape[0]
    once = pl.BlockSpec((width, rows), lambda j: (0, 0), pipeline_mode=pl.Buffered(1))
    (trail,) = far(trail)
    return pl.pallas_call(
        band_kernel,
        out_shape=jax.ShapeDtypeStruct((ranks, width // ranks, columns), FULL),
        grid=(columns // tile,),
        in_specs=[once, once, pl.BlockSpec((rows, tile), lambda j: (0, j))],
        out_specs=pl.BlockSpec((ranks, width // ranks, tile), lambda j: (0, 0, j)),
        compiler_params=pltpu.CompilerParams(vmem_limit_bytes=20 << 20),
        name="band_products",
        cost_estimate=pl.CostEstimate(
            flops=6 * width * rows * columns,
            bytes_accessed=4 * (rows * columns + width * rows + width * columns),
            transcendentals=0,
        ),
    )(high, low, trail)


def panel_kernel(count, tile, place, triple, uio, lower, trail, *rest):
    pieces = rest[:8]
    mine, other, strip, upper_high, upper_low, side_high, side_low, inner = rest[8:]
    width = uio.shape[0]
    z, y, x, c = place[0], place[1], place[2], place[3]
    piece = width // count

    def assemble():
        inner[...] = jnp.zeros_like(inner)
        side_high[:width, :], side_low[:width, :] = parts(triple[...])
        side_high[width:, :], side_low[width:, :] = parts(-uio[...].T)
        chunk = pieces[0].shape[0] // 4
        for k in range(8):
            for q in range(4):
                rank = 4 * (z ^ (k - 4)) + q if k >= 4 else 4 * q + (y ^ k)
                start = (k // 4) * width + rank * chunk
                at = pl.ds(pl.multiple_of(start, chunk), chunk)
                upper_high[at, :], upper_low[at, :] = parts(
                    pieces[k][q * chunk : (q + 1) * chunk, :]
                )

    def step(lower_tile, trail_tile, strip_tile):
        pl.when(pl.program_id(0) == 0)(assemble)
        product = close(
            parts(trail_tile[...]), (upper_high[...], upper_low[...]), ((1,), (1,))
        )
        product = parts(product)
        strip_tile[...] = close(product, (side_high[...], side_low[...]))
        for panel in range(2):
            left = parts(lower_rows(lower_tile, panel, count, piece))
            inner[panel * width : (panel + 1) * width, :] += close(left, product)

    pltpu.emit_pipeline(
        step,
        grid=(trail.shape[0] // tile,),
        in_specs=[
            pl.BlockSpec((lower.shape[0], tile), lambda i: (0, i)),
            pl.BlockSpec((tile, trail.shape[1]), lambda i: (i, 0)),
        ],
        out_specs=[pl.BlockSpec((tile, width), lambda i: (i, 0))],
    )(lower, trail, strip)

    rows, share = mine.shape[2], width // 4
    for k in range(4):
        for p in range(mine.shape[1]):
            start, column = (x ^ k) * share + rows * (p // 2), width * (p % 2)
            near = pl.ds(pl.multiple_of(c * width + start, rows), rows)
            beside = pl.ds(pl.multiple_of((1 - c) * width + start, rows), rows)
            mine[k, p] = inner[near, column : column + width]
            other[k, p] = inner[beside, column : column + width]


def panel_products(place, triple, uio, lower, trail, pieces, count, tile=256):
    rows, columns = trail.shape
    width = uio.shape[0]
    share = (4, 16, width // 32, width)
    lower, trail = far(lower, trail)
    hbm = pl.BlockSpec(memory_space=pltpu.HBM)
    return pl.pallas_call(
        functools.partial(panel_kernel, count, tile),
        out_shape=(
            jax.ShapeDtypeStruct(share, FULL),
            jax.ShapeDtypeStruct(share, FULL),
            jax.ShapeDtypeStruct((rows, width), FULL),
        ),
        in_specs=[pl.BlockSpec(memory_space=pltpu.SMEM), VMEM, VMEM, hbm, hbm] + [VMEM] * 8,
        out_specs=(VMEM, VMEM, hbm),
        scratch_shapes=[pltpu.VMEM((2 * width, columns), HALF)] * 2
        + [pltpu.VMEM((2 * width, width), HALF)] * 2
        + [pltpu.VMEM((2 * width, 2 * width), FULL)],
        compiler_params=pltpu.CompilerParams(vmem_limit_bytes=36 << 20),
        name="panel_products",
        cost_estimate=pl.CostEstimate(
            flops=3 * (4 * width * rows * columns + 12 * width * width * rows),
            bytes_accessed=4 * (rows * columns + 2 * width * columns + 4 * width * rows),
            transcendentals=0,
        ),
    )(place, triple, uio, lower, trail, *pieces)


def finish_kernel(
    place,
    mine,
    other,
    x_new,
    y_new,
    upper_pair,
    upper_triple,
    lower_pair,
    lower_triple,
    lot,
    uol,
    lin,
    uin,
    ldo,
    udo,
    lio,
    uio,
    corner_out,
    top_out,
    left_out,
    inner,
):
    width = lin.shape[0]
    c = place[3]
    rows, share = mine.shape[2], width // 4
    for k in range(4):
        for p in range(mine.shape[1]):
            start, column = k * share + rows * (p // 2), width * (p % 2)
            near = pl.ds(pl.multiple_of(c * width + start, rows), rows)
            beside = pl.ds(pl.multiple_of((1 - c) * width + start, rows), rows)
            inner[near, column : column + width] = mine[k, p]
            inner[beside, column : column + width] = other[k, p]
    row = lax.broadcasted_iota(jnp.int32, (width, width), 0)
    column = lax.broadcasted_iota(jnp.int32, (width, width), 1)
    below = row > column
    g11, g12 = inner[:width, :width], inner[:width, width:]
    g21, g22 = inner[width:, :width], inner[width:, width:]
    lin_t, uin_t, lio_t, uio_t = lin[...].T, uin[...].T, lio[...].T, uio[...].T
    inside = jnp.where(below, times(x_new[...], g11), times(g11, y_new[...]))
    corner = times(times(lin_t, inside), uin_t)
    top = times(times(lin_t, g12), uio_t) - times(corner, upper_pair[...])
    left = times(lio_t, times(g21, uin_t)) - times(lower_pair[...], corner)
    top_out[...] = top
    left_out[...] = left
    outer = times(lower_triple[...], g12) - times(lio_t, g22)
    under = times(g21, upper_triple[...]) - times(g22, uio_t)
    lower_grad = -(times(left, uol[...].T) + outer)
    upper_grad = -(times(lot[...].T, top) + under)
    inside = jnp.where(
        below, times(ldo[...].T, lower_grad), times(upper_grad, udo[...].T)
    )
    corner_out[...] = times(times(lio_t, inside), uio_t)


def finish(place, mine, other, *factors):
    width = factors[0].shape[0]
    mine, other = (pltpu.with_memory_space_constraint(a, pltpu.VMEM) for a in (mine, other))
    return pl.pallas_call(
        finish_kernel,
        out_shape=(jax.ShapeDtypeStruct((width, width), FULL),) * 3,
        in_specs=[pl.BlockSpec(memory_space=pltpu.SMEM)] + [VMEM] * (2 + len(factors)),
        out_specs=(VMEM,) * 3,
        scratch_shapes=[pltpu.VMEM((2 * width, 2 * width), FULL)],
        name="finish",
        cost_estimate=pl.CostEstimate(
            flops=240 * width**3, bytes_accessed=84 * width**2, transcendentals=0
        ),
    )(place, mine, other, *factors)


def swap(value, axis, step):
    size = lax.axis_size(axis)
    return lax.ppermute(value, axis, [(i, i ^ step) for i in range(size)])


def exchange(value, axes):
    return lax.all_to_all(value, axes, 0, 0, tiled=True)


def pieces_of(value, axis):
    return [value] + [swap(value, axis, step) for step in range(1, lax.axis_size(axis))]


def placed(pieces, axis):
    me = lax.axis_index(axis)
    size = pieces[0].shape[0]
    out = jnp.zeros((len(pieces) * size, *pieces[0].shape[1:]), pieces[0].dtype)
    for step, piece in enumerate(pieces):
        out = lax.dynamic_update_slice_in_dim(out, piece, (me ^ step) * size, 0)
    return out


def together(*values):
    return lax.optimization_barrier(values)


def body(
    trail,
    lower_new,
    upper_new,
    lot,
    lower_old,
    uol,
    upper_old,
    ldn,
    udn,
    lin,
    uin,
    ldo,
    udo,
    lio,
    uio,
):
    row, col = ("z", "y"), ("x", "c")
    count = lax.axis_size(col)
    ranks = lax.axis_size(row)

    lower_mine = jnp.concatenate((lower_new.T, lower_old.T), axis=0)
    lower_stack = lax.all_gather(lower_mine, col, axis=0, tiled=True)
    small = prepare(lot, uol, ldn, udn, lin, uin, lio, uio)
    *near, small = together(*pieces_of(upper_new, "z"), *pieces_of(upper_old, "y"), small)
    near_new, near_old = together(placed(near[:4], "z"), placed(near[4:], "y"))
    upper_triple, lower_triple = small[3], small[5]
    weights = band_weights(lower_triple, lio, lower_stack, count)
    pieces = pieces_of(near_new, "y") + [near_old, swap(near_old, "z", 1), swap(near_old, "z", 2)]
    last, weights = together(near_old, weights)
    pieces.append(swap(last, "z", 3))

    band = band_products(*weights, trail, ranks)
    *pieces, _ = together(*pieces, band)
    band = lax.all_to_all(band, row, 0, 0, tiled=True)

    place = jnp.stack([lax.axis_index(a) for a in row + col]).astype(jnp.int32)
    mine, other, strip = panel_products(
        place, upper_triple, uio, lower_stack, trail, pieces, count
    )
    mine = mine + swap(other, "c", 1)
    mine = mine[0] + sum(swap(mine[k], "x", k) for k in (1, 2, 3))
    mine, band = together(mine, band.sum(0))
    band_right = -lax.all_gather(-band, row, axis=0, tiled=True)
    mine = exchange(mine, row).sum(0)
    mine = exchange(jnp.broadcast_to(mine[None], (ranks, *mine.shape)), row)
    mine = exchange(jnp.broadcast_to(mine[None], (4, *mine.shape)), "x")
    mine, strip = together(mine, strip)
    strip = exchange(strip.reshape(count, -1, strip.shape[1]), col)
    other = swap(mine, "c", 1)
    corner_old, strip_top, band_left = finish(
        place, mine, other, *small, lot, uol, lin, uin, ldo, udo, lio, uio
    )
    strip, corner_old, band_right = together(strip, corner_old, band_right)
    return corner_old, strip_top, strip.sum(0), band_left, band_right


def solution(mesh):
    fine = Mesh(mesh.devices.reshape(4, 4, 4, 2), ("z", "y", "x", "c"))
    row, col = ("z", "y"), ("x", "c")
    split, whole = P(row, col), P()
    return jax.shard_map(
        body,
        mesh=fine,
        in_specs=(split, split, split, whole, split, whole, split) + (whole,) * 8,
        out_specs=(whole, whole, P(row + col, None), whole, P(None, col)),
        check_vma=False,
    )
```

time: 158 us -> 160 us (1.013)
  local copies, waits for them, and re-layouts: 4.22 us -> 7.45 us
  other arithmetic: 4.97 us -> 8.15 us
  waiting for transfers between devices: 28.8 us -> 26.5 us
    ppermute x17, waiting for transfers between devices: 22.7 us -> 15.8 us  [swap(): return lax.ppermute(value, axis, [(i, i ^ step) for i in range(size)])]
    all_gather x1, waiting for transfers between devices: 0.01 us -> 5.32 us  [body(): lower_stack = lax.all_gather(lower_mine, col, axis=0, tiled=True)]
    neg x0 -> x2, other arithmetic: none -> 3.81 us  [body(): band_right = -lax.all_gather(-band, row, axis=0, tiled=True)]
    unnamed x11 -> x24, local copies, waits for them, and re-layouts: 3.95 us -> 7.18 us
    all_to_all x1, waiting for transfers between devices: 6.1 us -> 4.07 us  [exchange(): return lax.all_to_all(value, axes, 0, 0, tiled=True)]
    pallas_call x3 -> x4, Pallas kernels: 28.3 us -> 28.2 us  [the longest x1 14.6 us: panel_products(): pl.pallas_call(functools.partial(panel_kernel, count, tile), out_shape=(j...]
  transfers between devices with their start and end apart: 21 -> 21, of which waited for: 10 -> 11; matrix products, arithmetic and copies ran while one was open for 1% -> 2% of each run, Pallas kernels for 22% -> 21%
where the time goes in v2:
time: 160 us; the launch traced here: 159 us
  starting transfers between devices  37.3 us (23%)
  Pallas kernels  34.2 us (21%)
  blocking collectives  31.4 us (20%)
  waiting for transfers between devices  26.5 us (17%)
  between operations  14.3 us (9%)
  other arithmetic  8.15 us (5%)
  local copies, waits for them, and re-layouts  7.45 us (5%)
    all_to_all x3, blocking collectives, exchange(): return lax.all_to_all(value, axes, 0, 0, tiled=True)  31.4 us
    ppermute x17, starting transfers between devices, swap(): return lax.ppermute(value, axis, [(i, i ^ step) for i in range(size)])  24.4 us
    ppermute x17, waiting for transfers between devices, swap(): return lax.ppermute(value, axis, [(i, i ^ step) for i in range(size)])  15.8 us
    pallas_call x1, Pallas kernels, panel_products(): pl.pallas_call(functools.partial(panel_kernel, count, tile), out_shape=(j...  14.6 us
    pallas_call x1, Pallas kernels, band_products(): pl.pallas_call(band_kernel, out_shape=jax.ShapeDtypeStruct((ranks, width...  9.08 us
    all_to_all x1, starting transfers between devices, exchange(): return lax.all_to_all(value, axes, 0, 0, tiled=True)  8.21 us
    unnamed x24, local copies, waits for them, and re-layouts  7.18 us
    pallas_call x1, Pallas kernels, finish(): pl.pallas_call(finish_kernel, out_shape=(jax.ShapeDtypeStruct((width, wid...  5.99 us
  transfers between devices with their start and end apart: 21, of which 11 were waited for; matrix products, arithmetic and copies ran while one was open for 2% of the time, Pallas kernels for 21%

profile of v2, /device:TPU:1, one launch (start us, length us, event | category | flops | bytes accessed | tf_op | source)
XLA Modules:
  0.0 159.3 jit_solution(8942082624459973893)
XLA Ops:
  7.2 1.7 %pad_maximum_fusion = f32[64,1024]{1,0:T(8,128)} fusion(f32[32,1024]{1,0:T(8,128)} %bitcast.17, f32[32,1024]{1,0:T(8,128)} %bitcast.18), kind=kLoop, calls=%fused_computation | loop fusion | flops 65536 | bytes 524288 | tf_op jit(solution)/shard_map/concatenate | solution.py:323
  9.0 2.5 %collective-permute-start = (f32[16,2048]{1,0:T(8,128)}, f32[16,2048]{1,0:T(8,128)S(1)}, u32[]{:S(2)}, u32[]{:S(2)}) collective-permute-start(f32[16,2048]{1,0:T(8,128)} %param.17), channel_id=1, source_target_pairs={{0,32},{32,0},{64,96},{96,64},{1,33},{33,1},{65,97},{97,65},{2,34}... | collective-permute-start | bytes 393224 | tf_op jit(solution)/shard_map/ppermute | solution.py:278
  11.5 3.3 %collective-permute-start.1 = (f32[16,2048]{1,0:T(8,128)}, f32[16,2048]{1,0:T(8,128)S(1)}, u32[]{:S(2)}, u32[]{:S(2)}) collective-permute-start(f32[16,2048]{1,0:T(8,128)} %param.17), channel_id=1, source_target_pairs={{0,64},{32,96},{64,0},{96,32},{1,65},{33,97},{65,1},{97,33},{2,66}... | collective-permute-start | bytes 393224 | tf_op jit(solution)/shard_map/ppermute | solution.py:278
  14.8 1.3 collective-permute-start.3
  16.1 2.6 %collective-permute-start.4 = (f32[16,2048]{1,0:T(8,128)}, f32[16,2048]{1,0:T(8,128)S(1)}, u32[]{:S(2)}, u32[]{:S(2)}) collective-permute-start(f32[16,2048]{1,0:T(8,128)} %param.21), channel_id=1, source_target_pairs={{0,16},{8,24},{16,0},{24,8},{1,17},{9,25},{17,1},{25,9},{2,18},{10... | collective-permute-start | bytes 393224 | tf_op jit(solution)/shard_map/ppermute | solution.py:278
  18.8 3.5 %prepare.1 = (f32[256,256]{1,0:T(8,128)}, f32[256,256]{1,0:T(8,128)}, f32[256,256]{1,0:T(8,128)}, f32[256,256]{1,0:T(8,128)}, f32[256,256]{1,0:T(8,128)}, /*index=5*/f32[256,256]{1,0:T(8,128)}) custom-call(f32[256,256]{1,0:T(8,128)} %lot.3, f32[256,256]{1,0:T(8,128)} %uol.3, f32[256,256]{1,0:T(8,128)} %ldn.1, f32[256,256]{1,0:T(8,128)} %udn.1, ...), custom_call_target="tpu_custom_call" | custom-call | flops 603979776 | bytes 3670016 | tf_op jit(solution)/shard_map/prepare/pallas_call | solution.py:51
  23.8 2.8 %collective-permute-done.5 = f32[16,2048]{1,0:T(8,128)S(1)} collective-permute-done((f32[16,2048]{1,0:T(8,128)}, f32[16,2048]{1,0:T(8,128)S(1)}, u32[]{:S(2)}, u32[]{:S(2)}) %collective-permute-start.5) | collective-permute-done | bytes 131104 | tf_op jit(solution)/shard_map/ppermute | solution.py:278
  26.9 1.1 collective-permute-start.10
  28.0 2.5 %collective-permute-start.7 = (f32[64,2048]{1,0:T(8,128)S(1)}, f32[64,2048]{1,0:T(8,128)S(1)}, u32[]{:S(2)}, u32[]{:S(2)}) collective-permute-start(f32[64,2048]{1,0:T(8,128)S(1)} %get-tuple-element.76.rest_0_), channel_id=1, source_target_pairs={{0,16},{8,24},{16,0},{24,8},{1,17},{9,25},{17,1},{25,9},{2,18},{10... | collective-permute-start | bytes 1572872 | tf_op jit(solution)/shard_map/ppermute | solution.py:278
  30.5 1.3 collective-permute-start.8
  31.8 1.9 %collective-permute-start.9 = (f32[64,2048]{1,0:T(8,128)S(1)}, f32[64,2048]{1,0:T(8,128)}, u32[]{:S(2)}, u32[]{:S(2)}) collective-permute-start(f32[64,2048]{1,0:T(8,128)S(1)} %get-tuple-element.80.rest_4_), channel_id=1, source_target_pairs={{0,32},{32,0},{64,96},{96,64},{1,33},{33,1},{65,97},{97,65},{2,34}... | collective-permute-start | bytes 1572872 | tf_op jit(solution)/shard_map/ppermute | solution.py:278
  33.8 5.3 %all-gather.3.cloned.1.call-done.lower = f32[512,1024]{1,0:T(8,128)} async-done(((f32[64,1024]{1,0:T(8,128)}), f32[512,1024]{1,0:T(8,128)}) %all-gather.3.cloned.1.call-update) | async-done | bytes 2097168 | tf_op jit(solution)/shard_map/all_gather | solution.py:324
  39.1 1.6 copy-done.1
  44.3 2.7 %collective-permute-start.11 = (f32[64,2048]{1,0:T(8,128)S(1)}, f32[64,2048]{1,0:T(8,128)}, u32[]{:S(2)}, u32[]{:S(2)}) collective-permute-start(f32[64,2048]{1,0:T(8,128)S(1)} %get-tuple-element.80.rest_4_), channel_id=1, source_target_pairs={{0,96},{32,64},{64,32},{96,0},{1,97},{33,65},{65,33},{97,1},{2,98}... | collective-permute-start | bytes 1572872 | tf_op jit(solution)/shard_map/ppermute | solution.py:278
  49.0 9.1 %band_products.1 = f32[16,16,2048]{2,1,0:T(8,128)} custom-call(bf16[256,1024]{1,0:T(8,128)(2,1)S(1)} %copy-done.7, bf16[256,1024]{1,0:T(8,128)(2,1)S(1)} %copy-done.9, f32[1024,2048]{1,0:T(8,128)} %trail.3), custom_call_target="tpu_custom_call" | custom-call | flops 3221225472 | bytes 11534336 | tf_op jit(solution)/shard_map/band_products/pallas_call | solution.py:109
  58.1 4.6 %all-to-all-start = ((f32[16,16,2048]{2,1,0:T(8,128)}), f32[16,16,2048]{2,1,0:T(8,128)}, u32[]{:S(2)}, u32[]{:S(2)}) async-start(f32[16,16,2048]{2,1,0:T(8,128)} %band_products.1), calls=%async_computation | async-start | bytes 4194304 | tf_op jit(solution)/shard_map/all_to_all | solution.py:336
  63.8 14.6 %panel_products.1 = (f32[4,16,8,256]{3,2,1,0:T(8,128)S(1)}, f32[4,16,8,256]{3,2,1,0:T(8,128)S(1)}, f32[1024,256]{1,0:T(8,128)}) custom-call(s32[4]{0:T(128)S(1)} %pad_add_fusion.place, f32[256,256]{1,0:T(8,128)S(1)} %copy-done.4, f32[256,256]{1,0:T(8,128)S(1)} %copy-done.3, f32[512,1024]{1,0:T(8,128)} %all-gather.3.cloned.1.call-done.lower, ...), custom_call_target="tpu_custom_call" | custom-call | flops 8858370048 | bytes 16777216 | tf_op jit(solution)/shard_map/panel_products/pallas_call | solution.py:183
  79.2 1.5 collective-permute-done.12
  80.9 1.3 collective-permute-start.13
  82.2 2.4 %collective-permute-start.14 = (f32[16,8,256]{2,1,0:T(8,128)S(1)}, f32[16,8,256]{2,1,0:T(8,128)S(1)}, u32[]{:S(2)}, u32[]{:S(2)}) collective-permute-start(f32[16,8,256]{2,1,0:T(8,128)S(1)} %get-tuple-element.101), channel_id=1, source_target_pairs={{0,4},{2,6},{4,0},{6,2},{1,5},{3,7},{5,1},{7,3},{8,12},{10,14},{12... | collective-permute-start | bytes 393224 | tf_op jit(solution)/shard_map/ppermute | solution.py:278
  85.8 4.9 %collective-permute-done.14 = f32[16,8,256]{2,1,0:T(8,128)S(1)} collective-permute-done((f32[16,8,256]{2,1,0:T(8,128)S(1)}, f32[16,8,256]{2,1,0:T(8,128)S(1)}, u32[]{:S(2)}, u32[]{:S(2)}) %collective-permute-start.14) | collective-permute-done | bytes 131104 | tf_op jit(solution)/shard_map/ppermute | solution.py:278
  90.7 2.5 %collective-permute-done.15 = f32[16,8,256]{2,1,0:T(8,128)S(1)} collective-permute-done((f32[16,8,256]{2,1,0:T(8,128)S(1)}, f32[16,8,256]{2,1,0:T(8,128)S(1)}, u32[]{:S(2)}, u32[]{:S(2)}) %collective-permute-start.15) | collective-permute-done | bytes 131104 | tf_op jit(solution)/shard_map/ppermute | solution.py:278
  93.2 1.3 all-to-all-done
  94.5 1.7 %reduce_sum.27 = f32[16,2048]{1,0:T(8,128)S(1)} reduce(f32[16,16,2048]{2,1,0:T(8,128)} %all-to-all-done, f32[]{:T(128)} %constant.7.clone.1), dimensions={0}, to_apply=%region_0.0 | reduce | flops 491520 | bytes 2228228 | tf_op jit(solution)/shard_map/reduce_sum | solution.py:344
  96.9 12.2 %all_to_all.27 = f32[16,8,256]{2,1,0:T(8,128)S(1)} all-to-all(f32[16,8,256]{2,1,0:T(8,128)S(1)} %fusion), channel_id=1, replica_groups=mesh['z'=4,'y'=4,'x'=4,'c'=2] {'z','y'}, dimensions={0} | all-to-all | bytes 262144 | tf_op jit(solution)/shard_map/all_to_all | solution.py:282
  109.1 9.9 %all_to_all.25 = f32[16,8,256]{2,1,0:T(8,128)S(1)} all-to-all(f32[16,8,256]{2,1,0:T(8,128)S(1)} %broadcast_in_dim.4), channel_id=1, replica_groups=mesh['z'=4,'y'=4,'x'=4,'c'=2] {'z','y'}, dimensions={0} | all-to-all | bytes 262144 | tf_op jit(solution)/shard_map/all_to_all | solution.py:282
  119.1 9.3 %all_to_all.26.mine = f32[4,16,8,256]{3,2,1,0:T(8,128)S(1)} all-to-all(f32[4,16,8,256]{3,2,1,0:T(8,128)S(1)} %broadcast_in_dim.5), channel_id=1, replica_groups=mesh['z'=4,'y'=4,'x'=4,'c'=2] {'x'}, dimensions={0} | all-to-all | bytes 1048576 | tf_op jit(solution)/shard_map/all_to_all | solution.py:282
  128.4 8.2 %all-to-all-start.4 = ((f32[8,128,256]{2,1,0:T(8,128)}), f32[8,128,256]{2,1,0:T(8,128)S(1)}, u32[]{:S(2)}, u32[]{:S(2)}) async-start(f32[8,128,256]{2,1,0:T(8,128)} %bitcast.10), calls=%async_computation.4 | async-start | bytes 2097152 | tf_op jit(solution)/shard_map/all_to_all | solution.py:282
  137.0 1.5 collective-permute-done.16.other
  138.5 6.0 %finish.1 = (f32[256,256]{1,0:T(8,128)}, f32[256,256]{1,0:T(8,128)}, f32[256,256]{1,0:T(8,128)}) custom-call(s32[4]{0:T(128)} %copy-done, f32[4,16,8,256]{3,2,1,0:T(8,128)S(1)} %all_to_all.26.mine, f32[4,16,8,256]{3,2,1,0:T(8,128)S(1)} %collective-permute-done.16.other, f32[256,256]{1,0:T(8,128)} %get-tuple-element.90.x_new, ...), custom_call_target="tpu_custom_call" | custom-call | flops 4026531840 | bytes 5505024 | tf_op jit(solution)/shard_map/finish/pallas_call | solution.py:263
  144.5 3.1 %neg.7 = f32[256,2048]{1,0:T(8,128)} negate(f32[256,2048]{1,0:T(8,128)} %all-gather.5.cloned.1.call-done) | non-fusion elementwise | flops 524288 | bytes 4194304 | tf_op jit(solution)/shard_map/neg | solution.py:345
  147.7 4.1 %all-to-all-done.4 = f32[8,128,256]{2,1,0:T(8,128)S(1)} async-done(((f32[8,128,256]{2,1,0:T(8,128)}), f32[8,128,256]{2,1,0:T(8,128)S(1)}, u32[]{:S(2)}, u32[]{:S(2)}) %all-to-all-start.4) | async-done | bytes 1048608 | tf_op jit(solution)/shard_map/all_to_all | solution.py:282
  (65 shorter events, 12.4 us)
Async XLA Ops:
  7.2 19.4 %copy-start.10 = (f32[16,2048]{1,0:T(8,128)S(1)}, f32[16,2048]{1,0:T(8,128)}, u32[]{:S(2)}) copy-start(f32[16,2048]{1,0:T(8,128)} %param.17) | copy-start | bytes 393220
  7.2 31.9 %all-gather.3.cloned.1.call-start = ((), (), s32[]{:S(2)}) async-start(), calls=%async_computation.5 | async-start | bytes 2359296 | tf_op jit(solution)/shard_map/all_gather | solution.py:324
  9.0 17.8 %copy-start.11 = (f32[16,2048]{1,0:T(8,128)S(1)}, f32[16,2048]{1,0:T(8,128)}, u32[]{:S(2)}) copy-start(f32[16,2048]{1,0:T(8,128)} %param.21) | copy-start | bytes 393220
  9.0 9.8 %collective-permute-start = (f32[16,2048]{1,0:T(8,128)}, f32[16,2048]{1,0:T(8,128)S(1)}, u32[]{:S(2)}, u32[]{:S(2)}) collective-permute-start(f32[16,2048]{1,0:T(8,128)} %param.17), channel_id=1, source_target_pairs={{0,32},{32,0},{64,96},{96,64},{1,33},{33,1},{65,97},{97,65},{2,34}... | collective-permute-start | bytes 393224 | tf_op jit(solution)/shard_map/ppermute | solution.py:278
  11.5 10.8 %collective-permute-start.1 = (f32[16,2048]{1,0:T(8,128)}, f32[16,2048]{1,0:T(8,128)S(1)}, u32[]{:S(2)}, u32[]{:S(2)}) collective-permute-start(f32[16,2048]{1,0:T(8,128)} %param.17), channel_id=1, source_target_pairs={{0,64},{32,96},{64,0},{96,32},{1,65},{33,97},{65,1},{97,33},{2,66}... | collective-permute-start | bytes 393224 | tf_op jit(solution)/shard_map/ppermute | solution.py:278
  14.8 8.4 %collective-permute-start.2 = (f32[16,2048]{1,0:T(8,128)}, f32[16,2048]{1,0:T(8,128)S(1)}, u32[]{:S(2)}, u32[]{:S(2)}) collective-permute-start(f32[16,2048]{1,0:T(8,128)} %param.17), channel_id=1, source_target_pairs={{0,96},{32,64},{64,32},{96,0},{1,97},{33,65},{65,33},{97,1},{2,98}... | collective-permute-start | bytes 393224 | tf_op jit(solution)/shard_map/ppermute | solution.py:278
  14.8 8.4 %collective-permute-start.3 = (f32[16,2048]{1,0:T(8,128)}, f32[16,2048]{1,0:T(8,128)S(1)}, u32[]{:S(2)}, u32[]{:S(2)}) collective-permute-start(f32[16,2048]{1,0:T(8,128)} %param.21), channel_id=1, source_target_pairs={{0,8},{8,0},{16,24},{24,16},{1,9},{9,1},{17,25},{25,17},{2,10},{10... | collective-permute-start | bytes 393224 | tf_op jit(solution)/shard_map/ppermute | solution.py:278
  16.1 7.6 %collective-permute-start.4 = (f32[16,2048]{1,0:T(8,128)}, f32[16,2048]{1,0:T(8,128)S(1)}, u32[]{:S(2)}, u32[]{:S(2)}) collective-permute-start(f32[16,2048]{1,0:T(8,128)} %param.21), channel_id=1, source_target_pairs={{0,16},{8,24},{16,0},{24,8},{1,17},{9,25},{17,1},{25,9},{2,18},{10... | collective-permute-start | bytes 393224 | tf_op jit(solution)/shard_map/ppermute | solution.py:278
  18.8 7.8 %collective-permute-start.5 = (f32[16,2048]{1,0:T(8,128)}, f32[16,2048]{1,0:T(8,128)S(1)}, u32[]{:S(2)}, u32[]{:S(2)}) collective-permute-start(f32[16,2048]{1,0:T(8,128)} %param.21), channel_id=1, source_target_pairs={{0,24},{8,16},{16,8},{24,0},{1,25},{9,17},{17,9},{25,1},{2,26},{10... | collective-permute-start | bytes 393224 | tf_op jit(solution)/shard_map/ppermute | solution.py:278
  22.3 16.8 %copy-start.2 = (f32[256,256]{1,0:T(8,128)S(1)}, f32[256,256]{1,0:T(8,128)}, u32[]{:S(2)}) copy-start(f32[256,256]{1,0:T(8,128)} %lio.5) | copy-start | bytes 786436
  26.9 17.4 %collective-permute-start.10 = (f32[64,2048]{1,0:T(8,128)S(1)}, f32[64,2048]{1,0:T(8,128)S(1)}, u32[]{:S(2)}, u32[]{:S(2)}) collective-permute-start(f32[64,2048]{1,0:T(8,128)S(1)} %get-tuple-element.80.rest_4_), channel_id=1, source_target_pairs={{0,64},{32,96},{64,0},{96,32},{1,65},{33,97},{65,1},{97,33},{2,66}... | collective-permute-start | bytes 1572872 | tf_op jit(solution)/shard_map/ppermute | solution.py:278
  28.0 34.9 %collective-permute-start.6 = (f32[64,2048]{1,0:T(8,128)S(1)}, f32[64,2048]{1,0:T(8,128)S(1)}, u32[]{:S(2)}, u32[]{:S(2)}) collective-permute-start(f32[64,2048]{1,0:T(8,128)S(1)} %get-tuple-element.76.rest_0_), channel_id=1, source_target_pairs={{0,8},{8,0},{16,24},{24,16},{1,9},{9,1},{17,25},{25,17},{2,10},{10... | collective-permute-start | bytes 1572872 | tf_op jit(solution)/shard_map/ppermute | solution.py:278
  28.0 34.9 %collective-permute-start.7 = (f32[64,2048]{1,0:T(8,128)S(1)}, f32[64,2048]{1,0:T(8,128)S(1)}, u32[]{:S(2)}, u32[]{:S(2)}) collective-permute-start(f32[64,2048]{1,0:T(8,128)S(1)} %get-tuple-element.76.rest_0_), channel_id=1, source_target_pairs={{0,16},{8,24},{16,0},{24,8},{1,17},{9,25},{17,1},{25,9},{2,18},{10... | collective-permute-start | bytes 1572872 | tf_op jit(solution)/shard_map/ppermute | solution.py:278
  30.5 32.3 %collective-permute-start.8 = (f32[64,2048]{1,0:T(8,128)S(1)}, f32[64,2048]{1,0:T(8,128)S(1)}, u32[]{:S(2)}, u32[]{:S(2)}) collective-permute-start(f32[64,2048]{1,0:T(8,128)S(1)} %get-tuple-element.76.rest_0_), channel_id=1, source_target_pairs={{0,24},{8,16},{16,8},{24,0},{1,25},{9,17},{17,9},{25,1},{2,26},{10... | collective-permute-start | bytes 1572872 | tf_op jit(solution)/shard_map/ppermute | solution.py:278
  31.8 31.0 %collective-permute-start.9 = (f32[64,2048]{1,0:T(8,128)S(1)}, f32[64,2048]{1,0:T(8,128)}, u32[]{:S(2)}, u32[]{:S(2)}) collective-permute-start(f32[64,2048]{1,0:T(8,128)S(1)} %get-tuple-element.80.rest_4_), channel_id=1, source_target_pairs={{0,32},{32,0},{64,96},{96,64},{1,33},{33,1},{65,97},{97,65},{2,34}... | collective-permute-start | bytes 1572872 | tf_op jit(solution)/shard_map/ppermute | solution.py:278
  39.1 1.6 copy-start.1
  40.7 0.9 copy-start.5
  43.5 0.8 copy-start.8
  44.3 18.6 %collective-permute-start.11 = (f32[64,2048]{1,0:T(8,128)S(1)}, f32[64,2048]{1,0:T(8,128)}, u32[]{:S(2)}, u32[]{:S(2)}) collective-permute-start(f32[64,2048]{1,0:T(8,128)S(1)} %get-tuple-element.80.rest_4_), channel_id=1, source_target_pairs={{0,96},{32,64},{64,32},{96,0},{1,97},{33,65},{65,33},{97,1},{2,98}... | collective-permute-start | bytes 1572872 | tf_op jit(solution)/shard_map/ppermute | solution.py:278
  46.9 1.0 copy-start.7
  48.0 1.0 copy-start.9
  58.1 4.8 %copy-start.3 = (f32[256,256]{1,0:T(8,128)S(1)}, f32[256,256]{1,0:T(8,128)}, u32[]{:S(2)}) copy-start(f32[256,256]{1,0:T(8,128)} %uio.5) | copy-start | bytes 786436
  58.1 36.4 %all-to-all-start = ((f32[16,16,2048]{2,1,0:T(8,128)}), f32[16,16,2048]{2,1,0:T(8,128)}, u32[]{:S(2)}, u32[]{:S(2)}) async-start(f32[16,16,2048]{2,1,0:T(8,128)} %band_products.1), calls=%async_computation | async-start | bytes 4194304 | tf_op jit(solution)/shard_map/all_to_all | solution.py:336
  62.7 81.8 %all-gather.5.cloned.1.call-start = ((), (), s32[]{:S(2)}) async-start(), calls=%async_computation.6 | async-start | bytes 2228224 | tf_op jit(solution)/shard_map/all_gather | solution.py:345
  62.8 15.6 %copy-start = (s32[4]{0:T(128)}, s32[4]{0:T(128)S(1)}, u32[]{:S(2)}) copy-start(s32[4]{0:T(128)S(1)} %pad_add_fusion.place) | copy-start | bytes 52
  62.9 1.0 copy-start.4
  78.5 2.3 %collective-permute-start.12 = (f32[4,16,8,256]{3,2,1,0:T(8,128)S(1)}, f32[4,16,8,256]{3,2,1,0:T(8,128)S(1)}, u32[]{:S(2)}, u32[]{:S(2)}) collective-permute-start(f32[4,16,8,256]{3,2,1,0:T(8,128)S(1)} %get-tuple-element.85), channel_id=1, source_target_pairs={{0,1},{1,0},{2,3},{3,2},{4,5},{5,4},{6,7},{7,6},{8,9},{9,8},{10,11... | collective-permute-start | bytes 1572872 | tf_op jit(solution)/shard_map/ppermute | solution.py:278
  80.9 4.9 %collective-permute-start.13 = (f32[16,8,256]{2,1,0:T(8,128)S(1)}, f32[16,8,256]{2,1,0:T(8,128)S(1)}, u32[]{:S(2)}, u32[]{:S(2)}) collective-permute-start(f32[16,8,256]{2,1,0:T(8,128)S(1)} %get-tuple-element.103), channel_id=1, source_target_pairs={{0,2},{2,0},{4,6},{6,4},{1,3},{3,1},{5,7},{7,5},{8,10},{10,8},{12,... | collective-permute-start | bytes 393224 | tf_op jit(solution)/shard_map/ppermute | solution.py:278
  82.2 8.5 %collective-permute-start.14 = (f32[16,8,256]{2,1,0:T(8,128)S(1)}, f32[16,8,256]{2,1,0:T(8,128)S(1)}, u32[]{:S(2)}, u32[]{:S(2)}) collective-permute-start(f32[16,8,256]{2,1,0:T(8,128)S(1)} %get-tuple-element.101), channel_id=1, source_target_pairs={{0,4},{2,6},{4,0},{6,2},{1,5},{3,7},{5,1},{7,3},{8,12},{10,14},{12... | collective-permute-start | bytes 393224 | tf_op jit(solution)/shard_map/ppermute | solution.py:278
  84.6 8.6 %collective-permute-start.15 = (f32[16,8,256]{2,1,0:T(8,128)S(1)}, f32[16,8,256]{2,1,0:T(8,128)S(1)}, u32[]{:S(2)}, u32[]{:S(2)}) collective-permute-start(f32[16,8,256]{2,1,0:T(8,128)S(1)} %get-tuple-element.102), channel_id=1, source_target_pairs={{0,6},{2,4},{4,2},{6,0},{1,7},{3,5},{5,3},{7,1},{8,14},{10,12},{12... | collective-permute-start | bytes 393224 | tf_op jit(solution)/shard_map/ppermute | solution.py:278
  128.4 23.3 %all-to-all-start.4 = ((f32[8,128,256]{2,1,0:T(8,128)}), f32[8,128,256]{2,1,0:T(8,128)S(1)}, u32[]{:S(2)}, u32[]{:S(2)}) async-start(f32[8,128,256]{2,1,0:T(8,128)} %bitcast.10), calls=%async_computation.4 | async-start | bytes 2097152 | tf_op jit(solution)/shard_map/all_to_all | solution.py:282
  136.6 1.9 %collective-permute-start.16 = (f32[4,16,8,256]{3,2,1,0:T(8,128)S(1)}, f32[4,16,8,256]{3,2,1,0:T(8,128)S(1)}, u32[]{:S(2)}, u32[]{:S(2)}) collective-permute-start(f32[4,16,8,256]{3,2,1,0:T(8,128)S(1)} %all_to_all.26.mine), channel_id=1, source_target_pairs={{0,1},{1,0},{2,3},{3,2},{4,5},{5,4},{6,7},{7,6},{8,9},{9,8},{10,11... | collective-permute-start | bytes 1572872 | tf_op jit(solution)/shard_map/ppermute | solution.py:278
  (1 other events, 0.8 us)
Sparse Core Ops, SparseCore 0:
  10.3 28.7 all-gather.2
  97.0 42.4 all-gather.4

commit v3 on v2

--- a/solution.py
+++ b/solution.py
@@ -70,56 +70,50 @@
     )
 
 
-def weight_kernel(count, triple, lio, lower, high, low):
-    piece = lio.shape[0] // count
-    new = parts(lower_rows(lower, 0, count, piece))
-    old = parts(lower_rows(lower, 1, count, piece))
-    high[...], low[...] = parts(close(parts(triple[...]), new) - close(parts(lio[...].T), old))
-
-
-def band_weights(triple, lio, lower, count):
-    width, rows = lio.shape[0], lower.shape[1]
-    return pl.pallas_call(
-        functools.partial(weight_kernel, count),
-        out_shape=(jax.ShapeDtypeStruct((width, rows), HALF),) * 2,
-        in_specs=[VMEM] * 3,
-        out_specs=(VMEM,) * 2,
-        compiler_params=pltpu.CompilerParams(vmem_limit_bytes=16 << 20),
-        name="band_weights",
-        cost_estimate=pl.CostEstimate(
-            flops=12 * width * width * rows,
-            bytes_accessed=12 * width * rows,
-            transcendentals=0,
-        ),
-    )(triple, lio, lower)
-
-
-def band_kernel(high, low, trail, out):
+def band_kernel(count, triple, lio, lower, trail, out, weights):
+    width = lio.shape[0]
+    piece = width // count
+
+    @pl.when(pl.program_id(0) == 0)
+    def _():
+        new = parts(lower_rows(lower, 0, count, piece))
+        old = parts(lower_rows(lower, 1, count, piece))
+        weight = close(parts(triple[...]), new) - close(parts(lio[...].T), old)
+        weights[:width, :], weights[width:, :] = parts(weight)
+
+    high, low = parts(trail[...])
+    both = mul(weights[...], high, ((1,), (0,)))
+    band = mul(weights[:width, :], low, ((1,), (0,))) + both[width:, :] + both[:width, :]
     size = out.shape[1]
-    band = close((high[...], low[...]), parts(trail[...]))
     for k in range(out.shape[0]):
         out[k] = band[k * size : (k + 1) * size, :]
 
 
-def band_products(high, low, trail, ranks, tile=256):
+def band_products(triple, lio, lower, trail, ranks, count, tile=512):
     rows, columns = trail.shape
-    width = high.shape[0]
-    once = pl.BlockSpec((width, rows), lambda j: (0, 0), pipeline_mode=pl.Buffered(1))
-    (trail,) = far(trail)
+    width = lio.shape[0]
+    once = pl.Buffered(1)
+    triple, lio, lower, trail = far(triple, lio, lower, trail)
     return pl.pallas_call(
-        band_kernel,
+        functools.partial(band_kernel, count),
         out_shape=jax.ShapeDtypeStruct((ranks, width // ranks, columns), FULL),
         grid=(columns // tile,),
-        in_specs=[once, once, pl.BlockSpec((rows, tile), lambda j: (0, j))],
+        in_specs=[
+            pl.BlockSpec((width, width), lambda j: (0, 0), pipeline_mode=once),
+            pl.BlockSpec((width, width), lambda j: (0, 0), pipeline_mode=once),
+            pl.BlockSpec((2 * width, rows), lambda j: (0, 0), pipeline_mode=once),
+            pl.BlockSpec((rows, tile), lambda j: (0, j)),
+        ],
         out_specs=pl.BlockSpec((ranks, width // ranks, tile), lambda j: (0, 0, j)),
-        compiler_params=pltpu.CompilerParams(vmem_limit_bytes=20 << 20),
+        scratch_shapes=[pltpu.VMEM((2 * width, rows), HALF)],
+        compiler_params=pltpu.CompilerParams(vmem_limit_bytes=24 << 20),
         name="band_products",
         cost_estimate=pl.CostEstimate(
             flops=6 * width * rows * columns,
-            bytes_accessed=4 * (rows * columns + width * rows + width * columns),
+            bytes_accessed=4 * (rows * columns + 2 * width * rows + width * columns),
             transcendentals=0,
         ),
-    )(high, low, trail)
+    )(triple, lio, lower, trail)
 
 
 def panel_kernel(count, tile, place, triple, uio, lower, trail, *rest):
@@ -129,7 +123,7 @@
     z, y, x, c = place[0], place[1], place[2], place[3]
     piece = width // count
 
-    def assemble():
+    def assemble(triple, uio):
         inner[...] = jnp.zeros_like(inner)
         side_high[:width, :], side_low[:width, :] = parts(triple[...])
         side_high[width:, :], side_low[width:, :] = parts(-uio[...].T)
@@ -143,8 +137,11 @@
                     pieces[k][q * chunk : (q + 1) * chunk, :]
                 )
 
-    def step(lower_tile, trail_tile, strip_tile):
-        pl.when(pl.program_id(0) == 0)(assemble)
+    def step(triple_here, uio_here, lower_tile, trail_tile, strip_tile):
+        @pl.when(pl.program_id(0) == 0)
+        def _():
+            assemble(triple_here, uio_here)
+
         product = close(
             parts(trail_tile[...]), (upper_high[...], upper_low[...]), ((1,), (1,))
         )
@@ -158,11 +155,13 @@
         step,
         grid=(trail.shape[0] // tile,),
         in_specs=[
+            pl.BlockSpec((width, width), lambda i: (0, 0)),
+            pl.BlockSpec((width, width), lambda i: (0, 0)),
             pl.BlockSpec((lower.shape[0], tile), lambda i: (0, i)),
             pl.BlockSpec((tile, trail.shape[1]), lambda i: (i, 0)),
         ],
         out_specs=[pl.BlockSpec((tile, width), lambda i: (i, 0))],
-    )(lower, trail, strip)
+    )(triple, uio, lower, trail, strip)
 
     rows, share = mine.shape[2], width // 4
     for k in range(4):
@@ -178,7 +177,7 @@
     rows, columns = trail.shape
     width = uio.shape[0]
     share = (4, 16, width // 32, width)
-    lower, trail = far(lower, trail)
+    triple, uio, lower, trail = far(triple, uio, lower, trail)
     hbm = pl.BlockSpec(memory_space=pltpu.HBM)
     return pl.pallas_call(
         functools.partial(panel_kernel, count, tile),
@@ -187,7 +186,7 @@
             jax.ShapeDtypeStruct(share, FULL),
             jax.ShapeDtypeStruct((rows, width), FULL),
         ),
-        in_specs=[pl.BlockSpec(memory_space=pltpu.SMEM), VMEM, VMEM, hbm, hbm] + [VMEM] * 8,
+        in_specs=[pl.BlockSpec(memory_space=pltpu.SMEM)] + [hbm] * 4 + [VMEM] * 8,
         out_specs=(VMEM, VMEM, hbm),
         scratch_shapes=[pltpu.VMEM((2 * width, columns), HALF)] * 2
         + [pltpu.VMEM((2 * width, width), HALF)] * 2
@@ -325,13 +324,10 @@
     small = prepare(lot, uol, ldn, udn, lin, uin, lio, uio)
     *near, small = together(*pieces_of(upper_new, "z"), *pieces_of(upper_old, "y"), small)
     near_new, near_old = together(placed(near[:4], "z"), placed(near[4:], "y"))
+    pieces = pieces_of(near_new, "y") + pieces_of(near_old, "z")
     upper_triple, lower_triple = small[3], small[5]
-    weights = band_weights(lower_triple, lio, lower_stack, count)
-    pieces = pieces_of(near_new, "y") + [near_old, swap(near_old, "z", 1), swap(near_old, "z", 2)]
-    last, weights = together(near_old, weights)
-    pieces.append(swap(last, "z", 3))
-
-    band = band_products(*weights, trail, ranks)
+
+    band = band_products(lower_triple, lio, lower_stack, trail, ranks, count)
     *pieces, _ = together(*pieces, band)
     band = lax.all_to_all(band, row, 0, 0, tiled=True)
 

time: 160 us -> 156 us (0.975)
  local copies, waits for them, and re-layouts: 7.45 us -> 0.29 us
  blocking collectives: 31.4 us -> 33 us
    ppermute x17, waiting for transfers between devices: 15.8 us -> 23.1 us  [swap(): return lax.ppermute(value, axis, [(i, i ^ step) for i in range(size)])]
    unnamed x24 -> x6, local copies, waits for them, and re-layouts: 7.18 us -> 0.02 us
    all_gather x1, waiting for transfers between devices: 5.32 us -> 0.01 us  [body(): lower_stack = lax.all_gather(lower_mine, col, axis=0, tiled=True)]
    pallas_call x1, Pallas kernels: 14.6 us -> 16.5 us  [panel_products(): pl.pallas_call(functools.partial(panel_kernel, count, tile), out_shape=(j...]
    pallas_call x2 -> x1, Pallas kernels: 10.1 us -> 9.16 us  [band_products(): pl.pallas_call(functools.partial(band_kernel, count), out_shape=jax.Shape...]
  transfers between devices with their start and end apart: 21 -> 21, of which waited for: 11 -> 10; matrix products, arithmetic and copies ran while one was open for 2% -> 2% of each run, Pallas kernels for 21% -> 23%
where the time goes in v3:
time: 156 us; the launch traced here: 155 us
  starting transfers between devices  37.5 us (24%)
  Pallas kernels  35.2 us (23%)
  blocking collectives  33 us (21%)
  waiting for transfers between devices  27.2 us (17%)
  between operations  14.3 us (9%)
  other arithmetic  8.16 us (5%)
    all_to_all x3, blocking collectives, exchange(): return lax.all_to_all(value, axes, 0, 0, tiled=True)  33 us
    ppermute x17, starting transfers between devices, swap(): return lax.ppermute(value, axis, [(i, i ^ step) for i in range(size)])  23.5 us
    ppermute x17, waiting for transfers between devices, swap(): return lax.ppermute(value, axis, [(i, i ^ step) for i in range(size)])  23.1 us
    pallas_call x1, Pallas kernels, panel_products(): pl.pallas_call(functools.partial(panel_kernel, count, tile), out_shape=(j...  16.5 us
    pallas_call x1, Pallas kernels, band_products(): pl.pallas_call(functools.partial(band_kernel, count), out_shape=jax.Shape...  9.16 us
    all_to_all x1, starting transfers between devices, exchange(): return lax.all_to_all(value, axes, 0, 0, tiled=True)  8.2 us
    pallas_call x1, Pallas kernels, finish(): pl.pallas_call(finish_kernel, out_shape=(jax.ShapeDtypeStruct((width, wid...  5.99 us
    all_to_all x1, starting transfers between devices, body(): band = lax.all_to_all(band, row, 0, 0, tiled=True)  5.63 us
  transfers between devices with their start and end apart: 21, of which 10 were waited for; matrix products, arithmetic and copies ran while one was open for 2% of the time, Pallas kernels for 23%

profile of v3, /device:TPU:1, one launch (start us, length us, event | category | flops | bytes accessed | tf_op | source)
XLA Modules:
  0.0 155.5 jit_solution(6839050021103471297)
XLA Ops:
  7.2 1.7 %pad_maximum_fusion = f32[64,1024]{1,0:T(8,128)} fusion(f32[32,1024]{1,0:T(8,128)} %bitcast.17, f32[32,1024]{1,0:T(8,128)} %bitcast.18), kind=kLoop, calls=%fused_computation | loop fusion | flops 65536 | bytes 524288 | tf_op jit(solution)/shard_map/concatenate | solution.py:322
  9.0 2.5 %collective-permute-start = (f32[16,2048]{1,0:T(8,128)}, f32[16,2048]{1,0:T(8,128)S(1)}, u32[]{:S(2)}, u32[]{:S(2)}) collective-permute-start(f32[16,2048]{1,0:T(8,128)} %param.17), channel_id=1, source_target_pairs={{0,32},{32,0},{64,96},{96,64},{1,33},{33,1},{65,97},{97,65},{2,34}... | collective-permute-start | bytes 393224 | tf_op jit(solution)/shard_map/ppermute | solution.py:277
  11.5 3.3 %collective-permute-start.1 = (f32[16,2048]{1,0:T(8,128)}, f32[16,2048]{1,0:T(8,128)S(1)}, u32[]{:S(2)}, u32[]{:S(2)}) collective-permute-start(f32[16,2048]{1,0:T(8,128)} %param.17), channel_id=1, source_target_pairs={{0,64},{32,96},{64,0},{96,32},{1,65},{33,97},{65,1},{97,33},{2,66}... | collective-permute-start | bytes 393224 | tf_op jit(solution)/shard_map/ppermute | solution.py:277
  14.8 1.3 collective-permute-start.3
  16.1 2.6 %collective-permute-start.4 = (f32[16,2048]{1,0:T(8,128)}, f32[16,2048]{1,0:T(8,128)S(1)}, u32[]{:S(2)}, u32[]{:S(2)}) collective-permute-start(f32[16,2048]{1,0:T(8,128)} %param.21), channel_id=1, source_target_pairs={{0,16},{8,24},{16,0},{24,8},{1,17},{9,25},{17,1},{25,9},{2,18},{10... | collective-permute-start | bytes 393224 | tf_op jit(solution)/shard_map/ppermute | solution.py:277
  18.8 3.5 %prepare.1 = (f32[256,256]{1,0:T(8,128)}, f32[256,256]{1,0:T(8,128)}, f32[256,256]{1,0:T(8,128)}, f32[256,256]{1,0:T(8,128)}, f32[256,256]{1,0:T(8,128)}, /*index=5*/f32[256,256]{1,0:T(8,128)}) custom-call(f32[256,256]{1,0:T(8,128)} %lot.3, f32[256,256]{1,0:T(8,128)} %uol.3, f32[256,256]{1,0:T(8,128)} %ldn.1, f32[256,256]{1,0:T(8,128)} %udn.1, ...), custom_call_target="tpu_custom_call" | custom-call | flops 603979776 | bytes 3670016 | tf_op jit(solution)/shard_map/prepare/pallas_call | solution.py:51
  22.3 1.0 collective-permute-done.2
  23.8 2.8 %collective-permute-done.5 = f32[16,2048]{1,0:T(8,128)S(1)} collective-permute-done((f32[16,2048]{1,0:T(8,128)}, f32[16,2048]{1,0:T(8,128)S(1)}, u32[]{:S(2)}, u32[]{:S(2)}) %collective-permute-start.5) | collective-permute-done | bytes 131104 | tf_op jit(solution)/shard_map/ppermute | solution.py:277
  26.9 1.1 collective-permute-start.10
  28.0 1.5 collective-permute-start.11
  29.4 2.2 %collective-permute-start.7 = (f32[64,2048]{1,0:T(8,128)S(1)}, f32[64,2048]{1,0:T(8,128)S(1)}, u32[]{:S(2)}, u32[]{:S(2)}) collective-permute-start(f32[64,2048]{1,0:T(8,128)S(1)} %get-tuple-element.66.rest_0_), channel_id=1, source_target_pairs={{0,16},{8,24},{16,0},{24,8},{1,17},{9,25},{17,1},{25,9},{2,18},{10... | collective-permute-start | bytes 1572872 | tf_op jit(solution)/shard_map/ppermute | solution.py:277
  31.6 1.7 %collective-permute-start.8 = (f32[64,2048]{1,0:T(8,128)S(1)}, f32[64,2048]{1,0:T(8,128)}, u32[]{:S(2)}, u32[]{:S(2)}) collective-permute-start(f32[64,2048]{1,0:T(8,128)S(1)} %get-tuple-element.66.rest_0_), channel_id=1, source_target_pairs={{0,24},{8,16},{16,8},{24,0},{1,25},{9,17},{17,9},{25,1},{2,26},{10... | collective-permute-start | bytes 1572872 | tf_op jit(solution)/shard_map/ppermute | solution.py:277
  33.3 7.1 %collective-permute-done.10.rest_6_ = f32[64,2048]{1,0:T(8,128)S(1)} collective-permute-done((f32[64,2048]{1,0:T(8,128)S(1)}, f32[64,2048]{1,0:T(8,128)S(1)}, u32[]{:S(2)}, u32[]{:S(2)}) %collective-permute-start.10) | collective-permute-done | bytes 524320 | tf_op jit(solution)/shard_map/ppermute | solution.py:277
  40.6 9.2 %band_products.1 = f32[16,16,2048]{2,1,0:T(8,128)} custom-call(f32[256,256]{1,0:T(8,128)} %get-tuple-element.65.triple.lower_triple, f32[256,256]{1,0:T(8,128)} %lio.5, f32[512,1024]{1,0:T(8,128)} %all-gather.3.cloned.1.call-done.lower, f32[1024,2048]{1,0:T(8,128)} %trail.3), custom_call_target="tpu_custom_call" | custom-call | flops 3221225472 | bytes 12582912 | tf_op jit(solution)/shard_map/band_products/pallas_call | solution.py:97
  49.8 5.6 %all-to-all-start = ((f32[16,16,2048]{2,1,0:T(8,128)}), f32[16,16,2048]{2,1,0:T(8,128)}, u32[]{:S(2)}, u32[]{:S(2)}) async-start(f32[16,16,2048]{2,1,0:T(8,128)} %band_products.1), calls=%async_computation | async-start | bytes 4194304 | tf_op jit(solution)/shard_map/all_to_all | solution.py:332
  55.6 16.5 %panel_products.1 = (f32[4,16,8,256]{3,2,1,0:T(8,128)S(1)}, f32[4,16,8,256]{3,2,1,0:T(8,128)S(1)}, f32[1024,256]{1,0:T(8,128)}) custom-call(s32[4]{0:T(128)S(1)} %pad_add_fusion.place, f32[256,256]{1,0:T(8,128)} %get-tuple-element.54.triple.upper_triple, f32[256,256]{1,0:T(8,128)} %uio.5, f32[512,1024]{1,0:T(8,128)} %all-gather.3.cloned.1.call-done.lower, ...), custom_call_target="tpu_custom_call" | custom-call | flops 8858370048 | bytes 16777216 | tf_op jit(solution)/shard_map/panel_products/pallas_call | solution.py:182
  72.2 3.0 %collective-permute-start.12 = (f32[4,16,8,256]{3,2,1,0:T(8,128)S(1)}, f32[4,16,8,256]{3,2,1,0:T(8,128)S(1)}, u32[]{:S(2)}, u32[]{:S(2)}) collective-permute-start(f32[4,16,8,256]{3,2,1,0:T(8,128)S(1)} %get-tuple-element.75), channel_id=1, source_target_pairs={{0,1},{1,0},{2,3},{3,2},{4,5},{5,4},{6,7},{7,6},{8,9},{9,8},{10,11... | collective-permute-start | bytes 1572872 | tf_op jit(solution)/shard_map/ppermute | solution.py:277
  75.1 1.5 collective-permute-done.12
  76.8 1.3 collective-permute-start.13
  78.1 2.4 %collective-permute-start.14 = (f32[16,8,256]{2,1,0:T(8,128)S(1)}, f32[16,8,256]{2,1,0:T(8,128)S(1)}, u32[]{:S(2)}, u32[]{:S(2)}) collective-permute-start(f32[16,8,256]{2,1,0:T(8,128)S(1)} %get-tuple-element.91), channel_id=1, source_target_pairs={{0,4},{2,6},{4,0},{6,2},{1,5},{3,7},{5,1},{7,3},{8,12},{10,14},{12... | collective-permute-start | bytes 393224 | tf_op jit(solution)/shard_map/ppermute | solution.py:277
  80.7 0.9 collective-permute-done.13
  81.6 5.0 %collective-permute-done.14 = f32[16,8,256]{2,1,0:T(8,128)S(1)} collective-permute-done((f32[16,8,256]{2,1,0:T(8,128)S(1)}, f32[16,8,256]{2,1,0:T(8,128)S(1)}, u32[]{:S(2)}, u32[]{:S(2)}) %collective-permute-start.14) | collective-permute-done | bytes 131104 | tf_op jit(solution)/shard_map/ppermute | solution.py:277
  86.6 2.5 %collective-permute-done.15 = f32[16,8,256]{2,1,0:T(8,128)S(1)} collective-permute-done((f32[16,8,256]{2,1,0:T(8,128)S(1)}, f32[16,8,256]{2,1,0:T(8,128)S(1)}, u32[]{:S(2)}, u32[]{:S(2)}) %collective-permute-start.15) | collective-permute-done | bytes 131104 | tf_op jit(solution)/shard_map/ppermute | solution.py:277
  89.1 1.7 %reduce_sum.27 = f32[16,2048]{1,0:T(8,128)S(1)} reduce(f32[16,16,2048]{2,1,0:T(8,128)} %all-to-all-done, f32[]{:T(128)} %constant.7.clone.1), dimensions={0}, to_apply=%region_0.0 | reduce | flops 491520 | bytes 2228228 | tf_op jit(solution)/shard_map/reduce_sum | solution.py:340
  91.5 13.5 %all_to_all.27 = f32[16,8,256]{2,1,0:T(8,128)S(1)} all-to-all(f32[16,8,256]{2,1,0:T(8,128)S(1)} %fusion), channel_id=1, replica_groups=mesh['z'=4,'y'=4,'x'=4,'c'=2] {'z','y'}, dimensions={0} | all-to-all | bytes 262144 | tf_op jit(solution)/shard_map/all_to_all | solution.py:281
  105.1 9.9 %all_to_all.25 = f32[16,8,256]{2,1,0:T(8,128)S(1)} all-to-all(f32[16,8,256]{2,1,0:T(8,128)S(1)} %broadcast_in_dim.4), channel_id=1, replica_groups=mesh['z'=4,'y'=4,'x'=4,'c'=2] {'z','y'}, dimensions={0} | all-to-all | bytes 262144 | tf_op jit(solution)/shard_map/all_to_all | solution.py:281
  115.1 9.5 %all_to_all.26.mine = f32[4,16,8,256]{3,2,1,0:T(8,128)S(1)} all-to-all(f32[4,16,8,256]{3,2,1,0:T(8,128)S(1)} %broadcast_in_dim.5), channel_id=1, replica_groups=mesh['z'=4,'y'=4,'x'=4,'c'=2] {'x'}, dimensions={0} | all-to-all | bytes 1048576 | tf_op jit(solution)/shard_map/all_to_all | solution.py:281
  124.6 8.2 %all-to-all-start.4 = ((f32[8,128,256]{2,1,0:T(8,128)}), f32[8,128,256]{2,1,0:T(8,128)S(1)}, u32[]{:S(2)}, u32[]{:S(2)}) async-start(f32[8,128,256]{2,1,0:T(8,128)} %bitcast.10), calls=%async_computation.4 | async-start | bytes 2097152 | tf_op jit(solution)/shard_map/all_to_all | solution.py:281
  133.0 1.7 %collective-permute-done.16.other = f32[4,16,8,256]{3,2,1,0:T(8,128)S(1)} collective-permute-done((f32[4,16,8,256]{3,2,1,0:T(8,128)S(1)}, f32[4,16,8,256]{3,2,1,0:T(8,128)S(1)}, u32[]{:S(2)}, u32[]{:S(2)}) %collective-permute-start.16) | collective-permute-done | bytes 524320 | tf_op jit(solution)/shard_map/ppermute | solution.py:277
  134.7 6.0 %finish.1 = (f32[256,256]{1,0:T(8,128)}, f32[256,256]{1,0:T(8,128)}, f32[256,256]{1,0:T(8,128)}) custom-call(s32[4]{0:T(128)} %copy-done, f32[4,16,8,256]{3,2,1,0:T(8,128)S(1)} %all_to_all.26.mine, f32[4,16,8,256]{3,2,1,0:T(8,128)S(1)} %collective-permute-done.16.other, f32[256,256]{1,0:T(8,128)} %get-tuple-element.80.x_new, ...), custom_call_target="tpu_custom_call" | custom-call | flops 4026531840 | bytes 5505024 | tf_op jit(solution)/shard_map/finish/pallas_call | solution.py:262
  140.7 3.1 %neg.7 = f32[256,2048]{1,0:T(8,128)} negate(f32[256,2048]{1,0:T(8,128)} %all-gather.5.cloned.1.call-done) | non-fusion elementwise | flops 524288 | bytes 4194304 | tf_op jit(solution)/shard_map/neg | solution.py:341
  143.9 4.1 %all-to-all-done.4 = f32[8,128,256]{2,1,0:T(8,128)S(1)} async-done(((f32[8,128,256]{2,1,0:T(8,128)}), f32[8,128,256]{2,1,0:T(8,128)S(1)}, u32[]{:S(2)}, u32[]{:S(2)}) %all-to-all-start.4) | async-done | bytes 1048608 | tf_op jit(solution)/shard_map/all_to_all | solution.py:281
  (46 shorter events, 3.2 us)
Async XLA Ops:
  7.2 19.4 %copy-start.1 = (f32[16,2048]{1,0:T(8,128)S(1)}, f32[16,2048]{1,0:T(8,128)}, u32[]{:S(2)}) copy-start(f32[16,2048]{1,0:T(8,128)} %param.17) | copy-start | bytes 393220
  7.2 33.5 %all-gather.3.cloned.1.call-start = ((), (), s32[]{:S(2)}) async-start(), calls=%async_computation.5 | async-start | bytes 2359296 | tf_op jit(solution)/shard_map/all_gather | solution.py:323
  9.0 17.8 %copy-start.2 = (f32[16,2048]{1,0:T(8,128)S(1)}, f32[16,2048]{1,0:T(8,128)}, u32[]{:S(2)}) copy-start(f32[16,2048]{1,0:T(8,128)} %param.21) | copy-start | bytes 393220
  9.0 9.8 %collective-permute-start = (f32[16,2048]{1,0:T(8,128)}, f32[16,2048]{1,0:T(8,128)S(1)}, u32[]{:S(2)}, u32[]{:S(2)}) collective-permute-start(f32[16,2048]{1,0:T(8,128)} %param.17), channel_id=1, source_target_pairs={{0,32},{32,0},{64,96},{96,64},{1,33},{33,1},{65,97},{97,65},{2,34}... | collective-permute-start | bytes 393224 | tf_op jit(solution)/shard_map/ppermute | solution.py:277
  11.5 10.7 %collective-permute-start.1 = (f32[16,2048]{1,0:T(8,128)}, f32[16,2048]{1,0:T(8,128)S(1)}, u32[]{:S(2)}, u32[]{:S(2)}) collective-permute-start(f32[16,2048]{1,0:T(8,128)} %param.17), channel_id=1, source_target_pairs={{0,64},{32,96},{64,0},{96,32},{1,65},{33,97},{65,1},{97,33},{2,66}... | collective-permute-start | bytes 393224 | tf_op jit(solution)/shard_map/ppermute | solution.py:277
  14.8 8.4 %collective-permute-start.2 = (f32[16,2048]{1,0:T(8,128)}, f32[16,2048]{1,0:T(8,128)S(1)}, u32[]{:S(2)}, u32[]{:S(2)}) collective-permute-start(f32[16,2048]{1,0:T(8,128)} %param.17), channel_id=1, source_target_pairs={{0,96},{32,64},{64,32},{96,0},{1,97},{33,65},{65,33},{97,1},{2,98}... | collective-permute-start | bytes 393224 | tf_op jit(solution)/shard_map/ppermute | solution.py:277
  14.8 8.4 %collective-permute-start.3 = (f32[16,2048]{1,0:T(8,128)}, f32[16,2048]{1,0:T(8,128)S(1)}, u32[]{:S(2)}, u32[]{:S(2)}) collective-permute-start(f32[16,2048]{1,0:T(8,128)} %param.21), channel_id=1, source_target_pairs={{0,8},{8,0},{16,24},{24,16},{1,9},{9,1},{17,25},{25,17},{2,10},{10... | collective-permute-start | bytes 393224 | tf_op jit(solution)/shard_map/ppermute | solution.py:277
  16.1 7.6 %collective-permute-start.4 = (f32[16,2048]{1,0:T(8,128)}, f32[16,2048]{1,0:T(8,128)S(1)}, u32[]{:S(2)}, u32[]{:S(2)}) collective-permute-start(f32[16,2048]{1,0:T(8,128)} %param.21), channel_id=1, source_target_pairs={{0,16},{8,24},{16,0},{24,8},{1,17},{9,25},{17,1},{25,9},{2,18},{10... | collective-permute-start | bytes 393224 | tf_op jit(solution)/shard_map/ppermute | solution.py:277
  18.8 7.8 %collective-permute-start.5 = (f32[16,2048]{1,0:T(8,128)}, f32[16,2048]{1,0:T(8,128)S(1)}, u32[]{:S(2)}, u32[]{:S(2)}) collective-permute-start(f32[16,2048]{1,0:T(8,128)} %param.21), channel_id=1, source_target_pairs={{0,24},{8,16},{16,8},{24,0},{1,25},{9,17},{17,9},{25,1},{2,26},{10... | collective-permute-start | bytes 393224 | tf_op jit(solution)/shard_map/ppermute | solution.py:277
  26.9 13.5 %collective-permute-start.10 = (f32[64,2048]{1,0:T(8,128)S(1)}, f32[64,2048]{1,0:T(8,128)S(1)}, u32[]{:S(2)}, u32[]{:S(2)}) collective-permute-start(f32[64,2048]{1,0:T(8,128)S(1)} %get-tuple-element.70.rest_4_), channel_id=1, source_target_pairs={{0,64},{32,96},{64,0},{96,32},{1,65},{33,97},{65,1},{97,33},{2,66}... | collective-permute-start | bytes 1572872 | tf_op jit(solution)/shard_map/ppermute | solution.py:277
  28.0 27.6 %collective-permute-start.11 = (f32[64,2048]{1,0:T(8,128)S(1)}, f32[64,2048]{1,0:T(8,128)S(1)}, u32[]{:S(2)}, u32[]{:S(2)}) collective-permute-start(f32[64,2048]{1,0:T(8,128)S(1)} %get-tuple-element.70.rest_4_), channel_id=1, source_target_pairs={{0,96},{32,64},{64,32},{96,0},{1,97},{33,65},{65,33},{97,1},{2,98}... | collective-permute-start | bytes 1572872 | tf_op jit(solution)/shard_map/ppermute | solution.py:277
  29.4 26.2 %collective-permute-start.6 = (f32[64,2048]{1,0:T(8,128)S(1)}, f32[64,2048]{1,0:T(8,128)S(1)}, u32[]{:S(2)}, u32[]{:S(2)}) collective-permute-start(f32[64,2048]{1,0:T(8,128)S(1)} %get-tuple-element.66.rest_0_), channel_id=1, source_target_pairs={{0,8},{8,0},{16,24},{24,16},{1,9},{9,1},{17,25},{25,17},{2,10},{10... | collective-permute-start | bytes 1572872 | tf_op jit(solution)/shard_map/ppermute | solution.py:277
  29.4 26.2 %collective-permute-start.7 = (f32[64,2048]{1,0:T(8,128)S(1)}, f32[64,2048]{1,0:T(8,128)S(1)}, u32[]{:S(2)}, u32[]{:S(2)}) collective-permute-start(f32[64,2048]{1,0:T(8,128)S(1)} %get-tuple-element.66.rest_0_), channel_id=1, source_target_pairs={{0,16},{8,24},{16,0},{24,8},{1,17},{9,25},{17,1},{25,9},{2,18},{10... | collective-permute-start | bytes 1572872 | tf_op jit(solution)/shard_map/ppermute | solution.py:277
  31.6 24.0 %collective-permute-start.8 = (f32[64,2048]{1,0:T(8,128)S(1)}, f32[64,2048]{1,0:T(8,128)}, u32[]{:S(2)}, u32[]{:S(2)}) collective-permute-start(f32[64,2048]{1,0:T(8,128)S(1)} %get-tuple-element.66.rest_0_), channel_id=1, source_target_pairs={{0,24},{8,16},{16,8},{24,0},{1,25},{9,17},{17,9},{25,1},{2,26},{10... | collective-permute-start | bytes 1572872 | tf_op jit(solution)/shard_map/ppermute | solution.py:277
  40.4 15.2 %collective-permute-start.9 = (f32[64,2048]{1,0:T(8,128)S(1)}, f32[64,2048]{1,0:T(8,128)}, u32[]{:S(2)}, u32[]{:S(2)}) collective-permute-start(f32[64,2048]{1,0:T(8,128)S(1)} %get-tuple-element.70.rest_4_), channel_id=1, source_target_pairs={{0,32},{32,0},{64,96},{96,64},{1,33},{33,1},{65,97},{97,65},{2,34}... | collective-permute-start | bytes 1572872 | tf_op jit(solution)/shard_map/ppermute | solution.py:277
  49.8 39.3 %all-to-all-start = ((f32[16,16,2048]{2,1,0:T(8,128)}), f32[16,16,2048]{2,1,0:T(8,128)}, u32[]{:S(2)}, u32[]{:S(2)}) async-start(f32[16,16,2048]{2,1,0:T(8,128)} %band_products.1), calls=%async_computation | async-start | bytes 4194304 | tf_op jit(solution)/shard_map/all_to_all | solution.py:332
  55.5 85.3 %all-gather.5.cloned.1.call-start = ((), (), s32[]{:S(2)}) async-start(), calls=%async_computation.6 | async-start | bytes 2228224 | tf_op jit(solution)/shard_map/all_gather | solution.py:341
  55.6 16.6 %copy-start = (s32[4]{0:T(128)}, s32[4]{0:T(128)S(1)}, u32[]{:S(2)}) copy-start(s32[4]{0:T(128)S(1)} %pad_add_fusion.place) | copy-start | bytes 52
  72.2 4.5 %collective-permute-start.12 = (f32[4,16,8,256]{3,2,1,0:T(8,128)S(1)}, f32[4,16,8,256]{3,2,1,0:T(8,128)S(1)}, u32[]{:S(2)}, u32[]{:S(2)}) collective-permute-start(f32[4,16,8,256]{3,2,1,0:T(8,128)S(1)} %get-tuple-element.75), channel_id=1, source_target_pairs={{0,1},{1,0},{2,3},{3,2},{4,5},{5,4},{6,7},{7,6},{8,9},{9,8},{10,11... | collective-permute-start | bytes 1572872 | tf_op jit(solution)/shard_map/ppermute | solution.py:277
  76.8 4.8 %collective-permute-start.13 = (f32[16,8,256]{2,1,0:T(8,128)S(1)}, f32[16,8,256]{2,1,0:T(8,128)S(1)}, u32[]{:S(2)}, u32[]{:S(2)}) collective-permute-start(f32[16,8,256]{2,1,0:T(8,128)S(1)} %get-tuple-element.93), channel_id=1, source_target_pairs={{0,2},{2,0},{4,6},{6,4},{1,3},{3,1},{5,7},{7,5},{8,10},{10,8},{12,... | collective-permute-start | bytes 393224 | tf_op jit(solution)/shard_map/ppermute | solution.py:277
  78.1 8.5 %collective-permute-start.14 = (f32[16,8,256]{2,1,0:T(8,128)S(1)}, f32[16,8,256]{2,1,0:T(8,128)S(1)}, u32[]{:S(2)}, u32[]{:S(2)}) collective-permute-start(f32[16,8,256]{2,1,0:T(8,128)S(1)} %get-tuple-element.91), channel_id=1, source_target_pairs={{0,4},{2,6},{4,0},{6,2},{1,5},{3,7},{5,1},{7,3},{8,12},{10,14},{12... | collective-permute-start | bytes 393224 | tf_op jit(solution)/shard_map/ppermute | solution.py:277
  80.5 8.6 %collective-permute-start.15 = (f32[16,8,256]{2,1,0:T(8,128)S(1)}, f32[16,8,256]{2,1,0:T(8,128)S(1)}, u32[]{:S(2)}, u32[]{:S(2)}) collective-permute-start(f32[16,8,256]{2,1,0:T(8,128)S(1)} %get-tuple-element.92), channel_id=1, source_target_pairs={{0,6},{2,4},{4,2},{6,0},{1,7},{3,5},{5,3},{7,1},{8,14},{10,12},{12... | collective-permute-start | bytes 393224 | tf_op jit(solution)/shard_map/ppermute | solution.py:277
  124.6 23.3 %all-to-all-start.4 = ((f32[8,128,256]{2,1,0:T(8,128)}), f32[8,128,256]{2,1,0:T(8,128)S(1)}, u32[]{:S(2)}, u32[]{:S(2)}) async-start(f32[8,128,256]{2,1,0:T(8,128)} %bitcast.10), calls=%async_computation.4 | async-start | bytes 2097152 | tf_op jit(solution)/shard_map/all_to_all | solution.py:281
  132.8 1.9 %collective-permute-start.16 = (f32[4,16,8,256]{3,2,1,0:T(8,128)S(1)}, f32[4,16,8,256]{3,2,1,0:T(8,128)S(1)}, u32[]{:S(2)}, u32[]{:S(2)}) collective-permute-start(f32[4,16,8,256]{3,2,1,0:T(8,128)S(1)} %all_to_all.26.mine), channel_id=1, source_target_pairs={{0,1},{1,0},{2,3},{3,2},{4,5},{5,4},{6,7},{7,6},{8,9},{9,8},{10,11... | collective-permute-start | bytes 1572872 | tf_op jit(solution)/shard_map/ppermute | solution.py:277
Sparse Core Ops, SparseCore 0:
  10.3 28.7 all-gather.2
  91.7 43.7 all-gather.4

commit v4 on v3

--- a/solution.py
+++ b/solution.py
@@ -35,14 +35,18 @@
 
 
 def prepare_kernel(lot, uol, ldn, udn, lin, uin, lio, uio, *out):
-    x_new, y_new, upper_pair, upper_triple, lower_pair, lower_triple = out
+    x_new, y_new, upper_pair, upper_triple, lower_pair, lower_triple, side_high, side_low = out
+    width = lin.shape[0]
     upper = times(uol[...].T, uio[...].T)
     lower = times(lio[...].T, lot[...].T)
     x_new[...] = times(ldn[...].T, lin[...].T)
     y_new[...] = times(uin[...].T, udn[...].T)
     upper_pair[...] = upper
     lower_pair[...] = lower
-    upper_triple[...] = times(uin[...].T, upper)
+    triple = times(uin[...].T, upper)
+    upper_triple[...] = triple
+    side_high[:width, :], side_low[:width, :] = parts(triple)
+    side_high[width:, :], side_low[width:, :] = parts(-uio[...].T)
     lower_triple[...] = times(lower, lin[...].T)
 
 
@@ -50,9 +54,10 @@
     width = factors[0].shape[0]
     return pl.pallas_call(
         prepare_kernel,
-        out_shape=(jax.ShapeDtypeStruct((width, width), FULL),) * 6,
+        out_shape=(jax.ShapeDtypeStruct((width, width), FULL),) * 6
+        + (jax.ShapeDtypeStruct((2 * width, width), HALF),) * 2,
         in_specs=[VMEM] * len(factors),
-        out_specs=(VMEM,) * 6,
+        out_specs=(VMEM,) * 8,
         name="prepare",
         cost_estimate=pl.CostEstimate(
             flops=36 * width**3, bytes_accessed=56 * width**2, transcendentals=0
@@ -116,17 +121,15 @@
     )(triple, lio, lower, trail)
 
 
-def panel_kernel(count, tile, place, triple, uio, lower, trail, *rest):
+def panel_kernel(count, tile, place, side_high, side_low, lower, trail, *rest):
     pieces = rest[:8]
-    mine, other, strip, upper_high, upper_low, side_high, side_low, inner = rest[8:]
-    width = uio.shape[0]
+    mine, other, strip, upper_high, upper_low, inner = rest[8:]
+    width = side_high.shape[1]
     z, y, x, c = place[0], place[1], place[2], place[3]
     piece = width // count
 
-    def assemble(triple, uio):
+    def assemble():
         inner[...] = jnp.zeros_like(inner)
-        side_high[:width, :], side_low[:width, :] = parts(triple[...])
-        side_high[width:, :], side_low[width:, :] = parts(-uio[...].T)
         chunk = pieces[0].shape[0] // 4
         for k in range(8):
             for q in range(4):
@@ -137,11 +140,8 @@
                     pieces[k][q * chunk : (q + 1) * chunk, :]
                 )
 
-    def step(triple_here, uio_here, lower_tile, trail_tile, strip_tile):
-        @pl.when(pl.program_id(0) == 0)
-        def _():
-            assemble(triple_here, uio_here)
-
+    def step(lower_tile, trail_tile, strip_tile):
+        pl.when(pl.program_id(0) == 0)(assemble)
         product = close(
             parts(trail_tile[...]), (upper_high[...], upper_low[...]), ((1,), (1,))
         )
@@ -155,13 +155,11 @@
         step,
         grid=(trail.shape[0] // tile,),
         in_specs=[
-            pl.BlockSpec((width, width), lambda i: (0, 0)),
-            pl.BlockSpec((width, width), lambda i: (0, 0)),
             pl.BlockSpec((lower.shape[0], tile), lambda i: (0, i)),
             pl.BlockSpec((tile, trail.shape[1]), lambda i: (i, 0)),
         ],
         out_specs=[pl.BlockSpec((tile, width), lambda i: (i, 0))],
-    )(triple, uio, lower, trail, strip)
+    )(lower, trail, strip)
 
     rows, share = mine.shape[2], width // 4
     for k in range(4):
@@ -173,11 +171,11 @@
             other[k, p] = inner[beside, column : column + width]
 
 
-def panel_products(place, triple, uio, lower, trail, pieces, count, tile=256):
+def panel_products(place, sides, lower, trail, pieces, count, tile=256):
     rows, columns = trail.shape
-    width = uio.shape[0]
+    width = sides[0].shape[1]
     share = (4, 16, width // 32, width)
-    triple, uio, lower, trail = far(triple, uio, lower, trail)
+    *sides, lower, trail = far(*sides, lower, trail)
     hbm = pl.BlockSpec(memory_space=pltpu.HBM)
     return pl.pallas_call(
         functools.partial(panel_kernel, count, tile),
@@ -186,10 +184,9 @@
             jax.ShapeDtypeStruct(share, FULL),
             jax.ShapeDtypeStruct((rows, width), FULL),
         ),
-        in_specs=[pl.BlockSpec(memory_space=pltpu.SMEM)] + [hbm] * 4 + [VMEM] * 8,
+        in_specs=[pl.BlockSpec(memory_space=pltpu.SMEM)] + [VMEM] * 2 + [hbm] * 2 + [VMEM] * 8,
         out_specs=(VMEM, VMEM, hbm),
         scratch_shapes=[pltpu.VMEM((2 * width, columns), HALF)] * 2
-        + [pltpu.VMEM((2 * width, width), HALF)] * 2
         + [pltpu.VMEM((2 * width, 2 * width), FULL)],
         compiler_params=pltpu.CompilerParams(vmem_limit_bytes=36 << 20),
         name="panel_products",
@@ -198,7 +195,7 @@
             bytes_accessed=4 * (rows * columns + 2 * width * columns + 4 * width * rows),
             transcendentals=0,
         ),
-    )(place, triple, uio, lower, trail, *pieces)
+    )(place, *sides, lower, trail, *pieces)
 
 
 def finish_kernel(
@@ -226,14 +223,14 @@
 ):
     width = lin.shape[0]
     c = place[3]
-    rows, share = mine.shape[2], width // 4
+    rows, share = mine.shape[1], width // 4
     for k in range(4):
-        for p in range(mine.shape[1]):
+        for p in range(mine.shape[0] // 4):
             start, column = k * share + rows * (p // 2), width * (p % 2)
             near = pl.ds(pl.multiple_of(c * width + start, rows), rows)
             beside = pl.ds(pl.multiple_of((1 - c) * width + start, rows), rows)
-            inner[near, column : column + width] = mine[k, p]
-            inner[beside, column : column + width] = other[k, p]
+            inner[near, column : column + width] = mine[4 * p + k]
+            inner[beside, column : column + width] = other[4 * p + k]
     row = lax.broadcasted_iota(jnp.int32, (width, width), 0)
     column = lax.broadcasted_iota(jnp.int32, (width, width), 1)
     below = row > column
@@ -325,23 +322,22 @@
     *near, small = together(*pieces_of(upper_new, "z"), *pieces_of(upper_old, "y"), small)
     near_new, near_old = together(placed(near[:4], "z"), placed(near[4:], "y"))
     pieces = pieces_of(near_new, "y") + pieces_of(near_old, "z")
-    upper_triple, lower_triple = small[3], small[5]
-
-    band = band_products(lower_triple, lio, lower_stack, trail, ranks, count)
+    *small, side_high, side_low = small
+
+    band = band_products(small[5], lio, lower_stack, trail, ranks, count)
     *pieces, _ = together(*pieces, band)
     band = lax.all_to_all(band, row, 0, 0, tiled=True)
 
     place = jnp.stack([lax.axis_index(a) for a in row + col]).astype(jnp.int32)
     mine, other, strip = panel_products(
-        place, upper_triple, uio, lower_stack, trail, pieces, count
+        place, (side_high, side_low), lower_stack, trail, pieces, count
     )
     mine = mine + swap(other, "c", 1)
     mine = mine[0] + sum(swap(mine[k], "x", k) for k in (1, 2, 3))
     mine, band = together(mine, band.sum(0))
     band_right = -lax.all_gather(-band, row, axis=0, tiled=True)
     mine = exchange(mine, row).sum(0)
-    mine = exchange(jnp.broadcast_to(mine[None], (ranks, *mine.shape)), row)
-    mine = exchange(jnp.broadcast_to(mine[None], (4, *mine.shape)), "x")
+    mine = exchange(jnp.broadcast_to(mine[None], (4 * ranks, *mine.shape)), row + ("x",))
     mine, strip = together(mine, strip)
     strip = exchange(strip.reshape(count, -1, strip.shape[1]), col)
     other = swap(mine, "c", 1)

time: 156 us -> 148 us (0.949)
  blocking collectives: 33 us -> 28.7 us
  Pallas kernels: 35.2 us -> 33.4 us
  starting transfers between devices: 37.5 us -> 35.9 us
    all_to_all x3 -> x2, blocking collectives: 33 us -> 28.7 us  [exchange(): return lax.all_to_all(value, axes, 0, 0, tiled=True)]
    all_to_all x1, waiting for transfers between devices: 4.06 us -> 1.7 us  [exchange(): return lax.all_to_all(value, axes, 0, 0, tiled=True)]
    all_gather x1, waiting for transfers between devices: 0.01 us -> 2.28 us  [body(): band_right = -lax.all_gather(-band, row, axis=0, tiled=True)]
    pallas_call x1, Pallas kernels: 16.5 us -> 14.5 us  [panel_products(): pl.pallas_call(functools.partial(panel_kernel, count, tile), out_shape=(j...]
  transfers between devices with their start and end apart: 21 -> 21, of which waited for: 10 -> 11; matrix products, arithmetic and copies ran while one was open for 2% -> 2% of each run, Pallas kernels for 23% -> 23%
where the time goes in v4:
time: 148 us
  starting transfers between devices  35.9 us (24%)
  Pallas kernels  33.4 us (23%)
  blocking collectives  28.7 us (19%)
  waiting for transfers between devices  26.9 us (18%)
  between operations  14.2 us (10%)
  other arithmetic  8.15 us (6%)
    all_to_all x2, blocking collectives, exchange(): return lax.all_to_all(value, axes, 0, 0, tiled=True)  28.7 us
    ppermute x17, starting transfers between devices, swap(): return lax.ppermute(value, axis, [(i, i ^ step) for i in range(size)])  23.6 us
    ppermute x17, waiting for transfers between devices, swap(): return lax.ppermute(value, axis, [(i, i ^ step) for i in range(size)])  22.9 us
    pallas_call x1, Pallas kernels, panel_products(): pl.pallas_call(functools.partial(panel_kernel, count, tile), out_shape=(j...  14.5 us
    pallas_call x1, Pallas kernels, band_products(): pl.pallas_call(functools.partial(band_kernel, count), out_shape=jax.Shape...  9.16 us
    all_to_all x1, starting transfers between devices, exchange(): return lax.all_to_all(value, axes, 0, 0, tiled=True)  6.67 us
    pallas_call x1, Pallas kernels, finish(): pl.pallas_call(finish_kernel, out_shape=(jax.ShapeDtypeStruct((width, wid...  6.09 us
    all_to_all x1, starting transfers between devices, body(): band = lax.all_to_all(band, row, 0, 0, tiled=True)  5.63 us
  transfers between devices with their start and end apart: 21, of which 11 were waited for; matrix products, arithmetic and copies ran while one was open for 2% of the time, Pallas kernels for 23%

profile of v4, /device:TPU:1, one launch (start us, length us, event | category | flops | bytes accessed | tf_op | source)
XLA Modules:
  0.0 147.7 jit_solution(12821587912544583761)
XLA Ops:
  7.2 1.7 %pad_maximum_fusion = f32[64,1024]{1,0:T(8,128)} fusion(f32[32,1024]{1,0:T(8,128)} %bitcast.17, f32[32,1024]{1,0:T(8,128)} %bitcast.18), kind=kLoop, calls=%fused_computation | loop fusion | flops 65536 | bytes 524288 | tf_op jit(solution)/shard_map/concatenate | solution.py:319
  9.0 2.5 %collective-permute-start = (f32[16,2048]{1,0:T(8,128)}, f32[16,2048]{1,0:T(8,128)S(1)}, u32[]{:S(2)}, u32[]{:S(2)}) collective-permute-start(f32[16,2048]{1,0:T(8,128)} %param.17), channel_id=1, source_target_pairs={{0,32},{32,0},{64,96},{96,64},{1,33},{33,1},{65,97},{97,65},{2,34}... | collective-permute-start | bytes 393224 | tf_op jit(solution)/shard_map/ppermute | solution.py:274
  11.5 3.3 %collective-permute-start.1 = (f32[16,2048]{1,0:T(8,128)}, f32[16,2048]{1,0:T(8,128)S(1)}, u32[]{:S(2)}, u32[]{:S(2)}) collective-permute-start(f32[16,2048]{1,0:T(8,128)} %param.17), channel_id=1, source_target_pairs={{0,64},{32,96},{64,0},{96,32},{1,65},{33,97},{65,1},{97,33},{2,66}... | collective-permute-start | bytes 393224 | tf_op jit(solution)/shard_map/ppermute | solution.py:274
  14.8 1.3 collective-permute-start.3
  16.1 2.6 %collective-permute-start.4 = (f32[16,2048]{1,0:T(8,128)}, f32[16,2048]{1,0:T(8,128)S(1)}, u32[]{:S(2)}, u32[]{:S(2)}) collective-permute-start(f32[16,2048]{1,0:T(8,128)} %param.21), channel_id=1, source_target_pairs={{0,16},{8,24},{16,0},{24,8},{1,17},{9,25},{17,1},{25,9},{2,18},{10... | collective-permute-start | bytes 393224 | tf_op jit(solution)/shard_map/ppermute | solution.py:274
  18.8 3.7 %prepare.1 = (f32[256,256]{1,0:T(8,128)}, f32[256,256]{1,0:T(8,128)}, f32[256,256]{1,0:T(8,128)}, f32[256,256]{1,0:T(8,128)}, f32[256,256]{1,0:T(8,128)}, /*inde...) custom-call(f32[256,256]{1,0:T(8,128)} %lot.3, f32[256,256]{1,0:T(8,128)} %uol.3, ...), custom_call_target="tpu_custom_call" | custom-call | flops 603979776 | bytes 3670016 | tf_op jit(solution)/shard_map/prepare/pallas_call | solution.py:55
  22.4 0.8 collective-permute-done.2
  23.8 2.8 %collective-permute-done.5 = f32[16,2048]{1,0:T(8,128)S(1)} collective-permute-done((f32[16,2048]{1,0:T(8,128)}, f32[16,2048]{1,0:T(8,128)S(1)}, u32[]{:S(2)}, u32[]{:S(2)}) %collective-permute-start.5) | collective-permute-done | bytes 131104 | tf_op jit(solution)/shard_map/ppermute | solution.py:274
  26.9 1.1 collective-permute-start.10
  28.0 1.5 collective-permute-start.11
  29.4 2.2 %collective-permute-start.7 = (f32[64,2048]{1,0:T(8,128)S(1)}, f32[64,2048]{1,0:T(8,128)S(1)}, u32[]{:S(2)}, u32[]{:S(2)}) collective-permute-start(f32[64,2048]{1,0:T(8,128)S(1)} %get-tuple-element.73.rest_0_), channel_id=1, source_target_pairs={{0,16},{8,24},{16,0},{24,8},{1,17},{9,25},{17,1},{25,9},{2,18},{10... | collective-permute-start | bytes 1572872 | tf_op jit(solution)/shard_map/ppermute | solution.py:274
  31.6 1.7 %collective-permute-start.8 = (f32[64,2048]{1,0:T(8,128)S(1)}, f32[64,2048]{1,0:T(8,128)}, u32[]{:S(2)}, u32[]{:S(2)}) collective-permute-start(f32[64,2048]{1,0:T(8,128)S(1)} %get-tuple-element.73.rest_0_), channel_id=1, source_target_pairs={{0,24},{8,16},{16,8},{24,0},{1,25},{9,17},{17,9},{25,1},{2,26},{10... | collective-permute-start | bytes 1572872 | tf_op jit(solution)/shard_map/ppermute | solution.py:274
  33.3 7.1 %collective-permute-done.10.rest_6_ = f32[64,2048]{1,0:T(8,128)S(1)} collective-permute-done((f32[64,2048]{1,0:T(8,128)S(1)}, f32[64,2048]{1,0:T(8,128)S(1)}, u32[]{:S(2)}, u32[]{:S(2)}) %collective-permute-start.10) | collective-permute-done | bytes 524320 | tf_op jit(solution)/shard_map/ppermute | solution.py:274
  40.6 9.2 %band_products.1 = f32[16,16,2048]{2,1,0:T(8,128)} custom-call(f32[256,256]{1,0:T(8,128)} %get-tuple-element.72.triple.lower_triple, f32[256,256]{1,0:T(8,128)} %lio.5, f32[512,1024]{1,0:T(8,128)} %all-gather.3.cloned.1.call-done.lower, f32[1024,2048]{1,0:T(8,128)} %trail.3), custom_call_target="tpu_custom_call" | custom-call | flops 3221225472 | bytes 12582912 | tf_op jit(solution)/shard_map/band_products/pallas_call | solution.py:102
  49.8 5.6 %all-to-all-start = ((f32[16,16,2048]{2,1,0:T(8,128)}), f32[16,16,2048]{2,1,0:T(8,128)}, u32[]{:S(2)}, u32[]{:S(2)}) async-start(f32[16,16,2048]{2,1,0:T(8,128)} %band_products.1), calls=%async_computation | async-start | bytes 4194304 | tf_op jit(solution)/shard_map/all_to_all | solution.py:329
  55.6 14.5 %panel_products.1 = (f32[4,16,8,256]{3,2,1,0:T(8,128)S(1)}, f32[4,16,8,256]{3,2,1,0:T(8,128)S(1)}, f32[1024,256]{1,0:T(8,128)}) custom-call(s32[4]{0:T(128)S(1)} %pad_add_fusion.place, bf16[512,256]{1,0:T(8,128)(2,1)} %get-tuple-element.60.side_high, bf16[512,256]{1,0:T(8,128)(2,1)} %get-tuple-element.61.side_low, ...), custom_call_target="tpu_custom_call" | custom-call | flops 8858370048 | bytes 16777216 | tf_op jit(solution)/shard_map/panel_products/pallas_call | solution.py:180
  70.2 3.0 %collective-permute-start.12 = (f32[4,16,8,256]{3,2,1,0:T(8,128)S(1)}, f32[4,16,8,256]{3,2,1,0:T(8,128)S(1)}, u32[]{:S(2)}, u32[]{:S(2)}) collective-permute-start(f32[4,16,8,256]{3,2,1,0:T(8,128)S(1)} %get-tuple-element.82), channel_id=1, source_target_pairs={{0,1},{1,0},{2,3},{3,2},{4,5},{5,4},{6,7},{7,6},{8,9},{9,8},{10,11... | collective-permute-start | bytes 1572872 | tf_op jit(solution)/shard_map/ppermute | solution.py:274
  73.1 1.5 %collective-permute-done.12 = f32[4,16,8,256]{3,2,1,0:T(8,128)S(1)} collective-permute-done((f32[4,16,8,256]{3,2,1,0:T(8,128)S(1)}, f32[4,16,8,256]{3,2,1,0:T(8,128)S(1)}, u32[]{:S(2)}, u32[]{:S(2)}) %collective-permute-start.12) | collective-permute-done | bytes 524320 | tf_op jit(solution)/shard_map/ppermute | solution.py:274
  74.8 1.3 collective-permute-start.13
  76.1 2.4 %collective-permute-start.14 = (f32[16,8,256]{2,1,0:T(8,128)S(1)}, f32[16,8,256]{2,1,0:T(8,128)S(1)}, u32[]{:S(2)}, u32[]{:S(2)}) collective-permute-start(f32[16,8,256]{2,1,0:T(8,128)S(1)} %get-tuple-element.99), channel_id=1, source_target_pairs={{0,4},{2,6},{4,0},{6,2},{1,5},{3,7},{5,1},{7,3},{8,12},{10,14},{12... | collective-permute-start | bytes 393224 | tf_op jit(solution)/shard_map/ppermute | solution.py:274
  78.7 1.0 collective-permute-done.13
  79.7 5.0 %collective-permute-done.14 = f32[16,8,256]{2,1,0:T(8,128)S(1)} collective-permute-done((f32[16,8,256]{2,1,0:T(8,128)S(1)}, f32[16,8,256]{2,1,0:T(8,128)S(1)}, u32[]{:S(2)}, u32[]{:S(2)}) %collective-permute-start.14) | collective-permute-done | bytes 131104 | tf_op jit(solution)/shard_map/ppermute | solution.py:274
  84.7 2.4 %collective-permute-done.15 = f32[16,8,256]{2,1,0:T(8,128)S(1)} collective-permute-done((f32[16,8,256]{2,1,0:T(8,128)S(1)}, f32[16,8,256]{2,1,0:T(8,128)S(1)}, u32[]{:S(2)}, u32[]{:S(2)}) %collective-permute-start.15) | collective-permute-done | bytes 131104 | tf_op jit(solution)/shard_map/ppermute | solution.py:274
  87.2 1.7 %reduce_sum.27 = f32[16,2048]{1,0:T(8,128)S(1)} reduce(f32[16,16,2048]{2,1,0:T(8,128)} %all-to-all-done, f32[]{:T(128)} %constant.7.clone.1), dimensions={0}, to_apply=%region_0.0 | reduce | flops 491520 | bytes 2228228 | tf_op jit(solution)/shard_map/reduce_sum | solution.py:337
  89.6 13.5 %all_to_all.21 = f32[16,8,256]{2,1,0:T(8,128)S(1)} all-to-all(f32[16,8,256]{2,1,0:T(8,128)S(1)} %fusion), channel_id=1, replica_groups=mesh['z'=4,'y'=4,'x'=4,'c'=2] {'z','y'}, dimensions={0} | all-to-all | bytes 262144 | tf_op jit(solution)/shard_map/all_to_all | solution.py:278
  103.1 15.2 %all_to_all.20.mine = f32[64,8,256]{2,1,0:T(8,128)S(1)} all-to-all(f32[64,8,256]{2,1,0:T(8,128)S(1)} %broadcast_in_dim.2), channel_id=1, replica_groups=mesh['z'=4,'y'=4,'x'=4,'c'=2] {'z','y','x'}, dimensions={0} | all-to-all | bytes 1048576 | tf_op jit(solution)/shard_map/all_to_all | solution.py:278
  118.4 6.7 %all-to-all-start.3 = ((f32[8,128,256]{2,1,0:T(8,128)}), f32[8,128,256]{2,1,0:T(8,128)S(1)}, u32[]{:S(2)}, u32[]{:S(2)}) async-start(f32[8,128,256]{2,1,0:T(8,128)} %bitcast.10), calls=%async_computation.3 | async-start | bytes 2097152 | tf_op jit(solution)/shard_map/all_to_all | solution.py:278
  125.2 1.7 %collective-permute-done.16.other = f32[64,8,256]{2,1,0:T(8,128)S(1)} collective-permute-done((f32[64,8,256]{2,1,0:T(8,128)S(1)}, f32[64,8,256]{2,1,0:T(8,128)S(1)}, u32[]{:S(2)}, u32[]{:S(2)}) %collective-permute-start.16) | collective-permute-done | bytes 524320 | tf_op jit(solution)/shard_map/ppermute | solution.py:274
  126.9 6.1 %finish.1 = (f32[256,256]{1,0:T(8,128)}, f32[256,256]{1,0:T(8,128)}, f32[256,256]{1,0:T(8,128)}) custom-call(s32[4]{0:T(128)} %copy-done, f32[64,8,256]{2,1,0:T(8,128)S(1)} %all_to_all.20.mine, f32[64,8,256]{2,1,0:T(8,128)S(1)} %collective-permute-done.16.other, f32[256,256]{1,0:T(8,128)} %get-tuple-element.87.x_new, f32[256,256]{1,0:T(8,128)} %get-tuple-element.88.y_new, ...), custom_call_target="tpu_custom_call" | custom-call | flops 4026531840 | bytes 5505024 | tf_op jit(solution)/shard_map/finish/pallas_call | solution.py:259
  133.0 2.3 %all-gather.5.cloned.1.call-done = f32[256,2048]{1,0:T(8,128)} async-done(((f32[16,2048]{1,0:T(8,128)}), f32[256,2048]{1,0:T(8,128)}) %all-gather.5.cloned.1.call-update) | async-done | bytes 2097168 | tf_op jit(solution)/shard_map/all_gather | solution.py:338
  135.3 3.1 %neg.7 = f32[256,2048]{1,0:T(8,128)} negate(f32[256,2048]{1,0:T(8,128)} %all-gather.5.cloned.1.call-done) | non-fusion elementwise | flops 524288 | bytes 4194304 | tf_op jit(solution)/shard_map/neg | solution.py:338
  138.4 1.7 %all-to-all-done.3 = f32[8,128,256]{2,1,0:T(8,128)S(1)} async-done(((f32[8,128,256]{2,1,0:T(8,128)}), f32[8,128,256]{2,1,0:T(8,128)S(1)}, u32[]{:S(2)}, u32[]{:S(2)}) %all-to-all-start.3) | async-done | bytes 1048608 | tf_op jit(solution)/shard_map/all_to_all | solution.py:278
  (44 shorter events, 3.2 us)
Async XLA Ops:
  7.2 19.4 %copy-start.1 = (f32[16,2048]{1,0:T(8,128)S(1)}, f32[16,2048]{1,0:T(8,128)}, u32[]{:S(2)}) copy-start(f32[16,2048]{1,0:T(8,128)} %param.17) | copy-start | bytes 393220
  7.2 33.5 %all-gather.3.cloned.1.call-start = ((), (), s32[]{:S(2)}) async-start(), calls=%async_computation.4 | async-start | bytes 2359296 | tf_op jit(solution)/shard_map/all_gather | solution.py:320
  9.0 17.8 %copy-start.2 = (f32[16,2048]{1,0:T(8,128)S(1)}, f32[16,2048]{1,0:T(8,128)}, u32[]{:S(2)}) copy-start(f32[16,2048]{1,0:T(8,128)} %param.21) | copy-start | bytes 393220
  9.0 9.8 %collective-permute-start = (f32[16,2048]{1,0:T(8,128)}, f32[16,2048]{1,0:T(8,128)S(1)}, u32[]{:S(2)}, u32[]{:S(2)}) collective-permute-start(f32[16,2048]{1,0:T(8,128)} %param.17), channel_id=1, source_target_pairs={{0,32},{32,0},{64,96},{96,64},{1,33},{33,1},{65,97},{97,65},{2,34}... | collective-permute-start | bytes 393224 | tf_op jit(solution)/shard_map/ppermute | solution.py:274
  11.5 10.9 %collective-permute-start.1 = (f32[16,2048]{1,0:T(8,128)}, f32[16,2048]{1,0:T(8,128)S(1)}, u32[]{:S(2)}, u32[]{:S(2)}) collective-permute-start(f32[16,2048]{1,0:T(8,128)} %param.17), channel_id=1, source_target_pairs={{0,64},{32,96},{64,0},{96,32},{1,65},{33,97},{65,1},{97,33},{2,66}... | collective-permute-start | bytes 393224 | tf_op jit(solution)/shard_map/ppermute | solution.py:274
  14.8 8.4 %collective-permute-start.2 = (f32[16,2048]{1,0:T(8,128)}, f32[16,2048]{1,0:T(8,128)S(1)}, u32[]{:S(2)}, u32[]{:S(2)}) collective-permute-start(f32[16,2048]{1,0:T(8,128)} %param.17), channel_id=1, source_target_pairs={{0,96},{32,64},{64,32},{96,0},{1,97},{33,65},{65,33},{97,1},{2,98}... | collective-permute-start | bytes 393224 | tf_op jit(solution)/shard_map/ppermute | solution.py:274
  14.8 8.4 %collective-permute-start.3 = (f32[16,2048]{1,0:T(8,128)}, f32[16,2048]{1,0:T(8,128)S(1)}, u32[]{:S(2)}, u32[]{:S(2)}) collective-permute-start(f32[16,2048]{1,0:T(8,128)} %param.21), channel_id=1, source_target_pairs={{0,8},{8,0},{16,24},{24,16},{1,9},{9,1},{17,25},{25,17},{2,10},{10... | collective-permute-start | bytes 393224 | tf_op jit(solution)/shard_map/ppermute | solution.py:274
  16.1 7.6 %collective-permute-start.4 = (f32[16,2048]{1,0:T(8,128)}, f32[16,2048]{1,0:T(8,128)S(1)}, u32[]{:S(2)}, u32[]{:S(2)}) collective-permute-start(f32[16,2048]{1,0:T(8,128)} %param.21), channel_id=1, source_target_pairs={{0,16},{8,24},{16,0},{24,8},{1,17},{9,25},{17,1},{25,9},{2,18},{10... | collective-permute-start | bytes 393224 | tf_op jit(solution)/shard_map/ppermute | solution.py:274
  18.8 7.8 %collective-permute-start.5 = (f32[16,2048]{1,0:T(8,128)}, f32[16,2048]{1,0:T(8,128)S(1)}, u32[]{:S(2)}, u32[]{:S(2)}) collective-permute-start(f32[16,2048]{1,0:T(8,128)} %param.21), channel_id=1, source_target_pairs={{0,24},{8,16},{16,8},{24,0},{1,25},{9,17},{17,9},{25,1},{2,26},{10... | collective-permute-start | bytes 393224 | tf_op jit(solution)/shard_map/ppermute | solution.py:274
  26.9 13.5 %collective-permute-start.10 = (f32[64,2048]{1,0:T(8,128)S(1)}, f32[64,2048]{1,0:T(8,128)S(1)}, u32[]{:S(2)}, u32[]{:S(2)}) collective-permute-start(f32[64,2048]{1,0:T(8,128)S(1)} %get-tuple-element.77.rest_4_), channel_id=1, source_target_pairs={{0,64},{32,96},{64,0},{96,32},{1,65},{33,97},{65,1},{97,33},{2,66}... | collective-permute-start | bytes 1572872 | tf_op jit(solution)/shard_map/ppermute | solution.py:274
  28.0 27.6 %collective-permute-start.11 = (f32[64,2048]{1,0:T(8,128)S(1)}, f32[64,2048]{1,0:T(8,128)S(1)}, u32[]{:S(2)}, u32[]{:S(2)}) collective-permute-start(f32[64,2048]{1,0:T(8,128)S(1)} %get-tuple-element.77.rest_4_), channel_id=1, source_target_pairs={{0,96},{32,64},{64,32},{96,0},{1,97},{33,65},{65,33},{97,1},{2,98}... | collective-permute-start | bytes 1572872 | tf_op jit(solution)/shard_map/ppermute | solution.py:274
  29.4 26.2 %collective-permute-start.6 = (f32[64,2048]{1,0:T(8,128)S(1)}, f32[64,2048]{1,0:T(8,128)S(1)}, u32[]{:S(2)}, u32[]{:S(2)}) collective-permute-start(f32[64,2048]{1,0:T(8,128)S(1)} %get-tuple-element.73.rest_0_), channel_id=1, source_target_pairs={{0,8},{8,0},{16,24},{24,16},{1,9},{9,1},{17,25},{25,17},{2,10},{10... | collective-permute-start | bytes 1572872 | tf_op jit(solution)/shard_map/ppermute | solution.py:274
  29.4 26.2 %collective-permute-start.7 = (f32[64,2048]{1,0:T(8,128)S(1)}, f32[64,2048]{1,0:T(8,128)S(1)}, u32[]{:S(2)}, u32[]{:S(2)}) collective-permute-start(f32[64,2048]{1,0:T(8,128)S(1)} %get-tuple-element.73.rest_0_), channel_id=1, source_target_pairs={{0,16},{8,24},{16,0},{24,8},{1,17},{9,25},{17,1},{25,9},{2,18},{10... | collective-permute-start | bytes 1572872 | tf_op jit(solution)/shard_map/ppermute | solution.py:274
  31.6 24.0 %collective-permute-start.8 = (f32[64,2048]{1,0:T(8,128)S(1)}, f32[64,2048]{1,0:T(8,128)}, u32[]{:S(2)}, u32[]{:S(2)}) collective-permute-start(f32[64,2048]{1,0:T(8,128)S(1)} %get-tuple-element.73.rest_0_), channel_id=1, source_target_pairs={{0,24},{8,16},{16,8},{24,0},{1,25},{9,17},{17,9},{25,1},{2,26},{10... | collective-permute-start | bytes 1572872 | tf_op jit(solution)/shard_map/ppermute | solution.py:274
  40.4 15.2 %collective-permute-start.9 = (f32[64,2048]{1,0:T(8,128)S(1)}, f32[64,2048]{1,0:T(8,128)}, u32[]{:S(2)}, u32[]{:S(2)}) collective-permute-start(f32[64,2048]{1,0:T(8,128)S(1)} %get-tuple-element.77.rest_4_), channel_id=1, source_target_pairs={{0,32},{32,0},{64,96},{96,64},{1,33},{33,1},{65,97},{97,65},{2,34}... | collective-permute-start | bytes 1572872 | tf_op jit(solution)/shard_map/ppermute | solution.py:274
  49.8 37.3 %all-to-all-start = ((f32[16,16,2048]{2,1,0:T(8,128)}), f32[16,16,2048]{2,1,0:T(8,128)}, u32[]{:S(2)}, u32[]{:S(2)}) async-start(f32[16,16,2048]{2,1,0:T(8,128)} %band_products.1), calls=%async_computation | async-start | bytes 4194304 | tf_op jit(solution)/shard_map/all_to_all | solution.py:329
  55.5 79.9 %all-gather.5.cloned.1.call-start = ((), (), s32[]{:S(2)}) async-start(), calls=%async_computation.5 | async-start | bytes 2228224 | tf_op jit(solution)/shard_map/all_gather | solution.py:338
  55.6 14.6 %copy-start = (s32[4]{0:T(128)}, s32[4]{0:T(128)S(1)}, u32[]{:S(2)}) copy-start(s32[4]{0:T(128)S(1)} %pad_add_fusion.place) | copy-start | bytes 52
  70.2 4.5 %collective-permute-start.12 = (f32[4,16,8,256]{3,2,1,0:T(8,128)S(1)}, f32[4,16,8,256]{3,2,1,0:T(8,128)S(1)}, u32[]{:S(2)}, u32[]{:S(2)}) collective-permute-start(f32[4,16,8,256]{3,2,1,0:T(8,128)S(1)} %get-tuple-element.82), channel_id=1, source_target_pairs={{0,1},{1,0},{2,3},{3,2},{4,5},{5,4},{6,7},{7,6},{8,9},{9,8},{10,11... | collective-permute-start | bytes 1572872 | tf_op jit(solution)/shard_map/ppermute | solution.py:274
  74.8 4.9 %collective-permute-start.13 = (f32[16,8,256]{2,1,0:T(8,128)S(1)}, f32[16,8,256]{2,1,0:T(8,128)S(1)}, u32[]{:S(2)}, u32[]{:S(2)}) collective-permute-start(f32[16,8,256]{2,1,0:T(8,128)S(1)} %get-tuple-element.101), channel_id=1, source_target_pairs={{0,2},{2,0},{4,6},{6,4},{1,3},{3,1},{5,7},{7,5},{8,10},{10,8},{12,... | collective-permute-start | bytes 393224 | tf_op jit(solution)/shard_map/ppermute | solution.py:274
  76.1 8.6 %collective-permute-start.14 = (f32[16,8,256]{2,1,0:T(8,128)S(1)}, f32[16,8,256]{2,1,0:T(8,128)S(1)}, u32[]{:S(2)}, u32[]{:S(2)}) collective-permute-start(f32[16,8,256]{2,1,0:T(8,128)S(1)} %get-tuple-element.99), channel_id=1, source_target_pairs={{0,4},{2,6},{4,0},{6,2},{1,5},{3,7},{5,1},{7,3},{8,12},{10,14},{12... | collective-permute-start | bytes 393224 | tf_op jit(solution)/shard_map/ppermute | solution.py:274
  78.5 8.6 %collective-permute-start.15 = (f32[16,8,256]{2,1,0:T(8,128)S(1)}, f32[16,8,256]{2,1,0:T(8,128)S(1)}, u32[]{:S(2)}, u32[]{:S(2)}) collective-permute-start(f32[16,8,256]{2,1,0:T(8,128)S(1)} %get-tuple-element.100), channel_id=1, source_target_pairs={{0,6},{2,4},{4,2},{6,0},{1,7},{3,5},{5,3},{7,1},{8,14},{10,12},{12... | collective-permute-start | bytes 393224 | tf_op jit(solution)/shard_map/ppermute | solution.py:274
  118.4 21.8 %all-to-all-start.3 = ((f32[8,128,256]{2,1,0:T(8,128)}), f32[8,128,256]{2,1,0:T(8,128)S(1)}, u32[]{:S(2)}, u32[]{:S(2)}) async-start(f32[8,128,256]{2,1,0:T(8,128)} %bitcast.10), calls=%async_computation.3 | async-start | bytes 2097152 | tf_op jit(solution)/shard_map/all_to_all | solution.py:278
  125.0 1.9 %collective-permute-start.16 = (f32[64,8,256]{2,1,0:T(8,128)S(1)}, f32[64,8,256]{2,1,0:T(8,128)S(1)}, u32[]{:S(2)}, u32[]{:S(2)}) collective-permute-start(f32[64,8,256]{2,1,0:T(8,128)S(1)} %all_to_all.20.mine), channel_id=1, source_target_pairs={{0,1},{1,0},{2,3},{3,2},{4,5},{5,4},{6,7},{7,6},{8,9},{9,8},{10,11... | collective-permute-start | bytes 1572872 | tf_op jit(solution)/shard_map/ppermute | solution.py:274
Sparse Core Ops, SparseCore 0:
  10.3 28.7 all-gather.2
  89.7 45.5 all-gather.4

commit v5 on v4

--- a/solution.py
+++ b/solution.py
@@ -83,7 +83,7 @@
     def _():
         new = parts(lower_rows(lower, 0, count, piece))
         old = parts(lower_rows(lower, 1, count, piece))
-        weight = close(parts(triple[...]), new) - close(parts(lio[...].T), old)
+        weight = close(parts(lio[...].T), old) - close(parts(triple[...]), new)
         weights[:width, :], weights[width:, :] = parts(weight)
 
     high, low = parts(trail[...])
@@ -94,7 +94,7 @@
         out[k] = band[k * size : (k + 1) * size, :]
 
 
-def band_products(triple, lio, lower, trail, ranks, count, tile=512):
+def band_products(triple, lio, lower, trail, ranks, count, tile=1024):
     rows, columns = trail.shape
     width = lio.shape[0]
     once = pl.Buffered(1)
@@ -335,7 +335,7 @@
     mine = mine + swap(other, "c", 1)
     mine = mine[0] + sum(swap(mine[k], "x", k) for k in (1, 2, 3))
     mine, band = together(mine, band.sum(0))
-    band_right = -lax.all_gather(-band, row, axis=0, tiled=True)
+    band = lax.all_gather(band, row, axis=0, tiled=True)
     mine = exchange(mine, row).sum(0)
     mine = exchange(jnp.broadcast_to(mine[None], (4 * ranks, *mine.shape)), row + ("x",))
     mine, strip = together(mine, strip)
@@ -344,8 +344,8 @@
     corner_old, strip_top, band_left = finish(
         place, mine, other, *small, lot, uol, lin, uin, ldo, udo, lio, uio
     )
-    strip, corner_old, band_right = together(strip, corner_old, band_right)
-    return corner_old, strip_top, strip.sum(0), band_left, band_right
+    band, strip_bottom = together(band, strip.sum(0))
+    return corner_old, strip_top, strip_bottom, band_left, -band
 
 
 def solution(mesh):

time: 148 us -> 154 us (1.041)
  waiting for transfers between devices: 26.9 us -> 30.1 us
  blocking collectives: 28.7 us -> 30.9 us
    all_to_all x1, waiting for transfers between devices: 1.7 us -> 7.13 us  [exchange(): return lax.all_to_all(value, axes, 0, 0, tiled=True)]
    all_gather x1, waiting for transfers between devices: 2.28 us -> 0.01 us  [body(): band = lax.all_gather(band, row, axis=0, tiled=True)]
    all_to_all x2, blocking collectives: 28.7 us -> 30.9 us  [exchange(): return lax.all_to_all(value, axes, 0, 0, tiled=True)]
    neg x2 -> x1, other arithmetic: 3.81 us -> 3.14 us  [body(): return (corner_old, strip_top, strip_bottom, band_left, -band)]
  transfers between devices with their start and end apart: 21 -> 21, of which waited for: 11 -> 10; matrix products, arithmetic and copies ran while one was open for 2% -> 1% of each run, Pallas kernels for 23% -> 22%
where the time goes in v5:
time: 154 us; the launch traced here: 153 us
  starting transfers between devices  36.4 us (24%)
  Pallas kernels  33 us (21%)
  blocking collectives  30.9 us (20%)
  waiting for transfers between devices  30.1 us (20%)
  between operations  14.2 us (9%)
  other arithmetic  8.14 us (5%)
    all_to_all x2, blocking collectives, exchange(): return lax.all_to_all(value, axes, 0, 0, tiled=True)  30.9 us
    ppermute x17, starting transfers between devices, swap(): return lax.ppermute(value, axis, [(i, i ^ step) for i in range(size)])  24 us
    ppermute x17, waiting for transfers between devices, swap(): return lax.ppermute(value, axis, [(i, i ^ step) for i in range(size)])  22.9 us
    pallas_call x1, Pallas kernels, panel_products(): pl.pallas_call(functools.partial(panel_kernel, count, tile), out_shape=(j...  14.5 us
    pallas_call x1, Pallas kernels, band_products(): pl.pallas_call(functools.partial(band_kernel, count), out_shape=jax.Shape...  8.7 us
    all_to_all x1, waiting for transfers between devices, exchange(): return lax.all_to_all(value, axes, 0, 0, tiled=True)  7.13 us
    all_to_all x1, starting transfers between devices, exchange(): return lax.all_to_all(value, axes, 0, 0, tiled=True)  6.75 us
    pallas_call x1, Pallas kernels, finish(): pl.pallas_call(finish_kernel, out_shape=(jax.ShapeDtypeStruct((width, wid...  6.08 us
  transfers between devices with their start and end apart: 21, of which 10 were waited for; matrix products, arithmetic and copies ran while one was open for 1% of the time, Pallas kernels for 22%

profile of v5, /device:TPU:1, one launch (start us, length us, event | category | flops | bytes accessed | tf_op | source)
XLA Modules:
  0.0 153.1 jit_solution(8301088084529134203)
XLA Ops:
  7.2 1.7 %pad_maximum_fusion = f32[64,1024]{1,0:T(8,128)} fusion(f32[32,1024]{1,0:T(8,128)} %bitcast.17, f32[32,1024]{1,0:T(8,128)} %bitcast.18), kind=kLoop, calls=%fused_computation | loop fusion | flops 65536 | bytes 524288 | tf_op jit(solution)/shard_map/concatenate | solution.py:319
  9.0 2.5 %collective-permute-start = (f32[16,2048]{1,0:T(8,128)}, f32[16,2048]{1,0:T(8,128)S(1)}, u32[]{:S(2)}, u32[]{:S(2)}) collective-permute-start(f32[16,2048]{1,0:T(8,128)} %param.17), channel_id=1, source_target_pairs={{0,32},{32,0},{64,96},{96,64},{1,33},{33,1},{65,97},{97,65},{2,34}... | collective-permute-start | bytes 393224 | tf_op jit(solution)/shard_map/ppermute | solution.py:274
  11.5 3.3 %collective-permute-start.1 = (f32[16,2048]{1,0:T(8,128)}, f32[16,2048]{1,0:T(8,128)S(1)}, u32[]{:S(2)}, u32[]{:S(2)}) collective-permute-start(f32[16,2048]{1,0:T(8,128)} %param.17), channel_id=1, source_target_pairs={{0,64},{32,96},{64,0},{96,32},{1,65},{33,97},{65,1},{97,33},{2,66}... | collective-permute-start | bytes 393224 | tf_op jit(solution)/shard_map/ppermute | solution.py:274
  14.8 1.3 collective-permute-start.3
  16.1 2.6 %collective-permute-start.4 = (f32[16,2048]{1,0:T(8,128)}, f32[16,2048]{1,0:T(8,128)S(1)}, u32[]{:S(2)}, u32[]{:S(2)}) collective-permute-start(f32[16,2048]{1,0:T(8,128)} %param.21), channel_id=1, source_target_pairs={{0,16},{8,24},{16,0},{24,8},{1,17},{9,25},{17,1},{25,9},{2,18},{10... | collective-permute-start | bytes 393224 | tf_op jit(solution)/shard_map/ppermute | solution.py:274
  18.8 3.7 %prepare.1 = (f32[256,256]{1,0:T(8,128)}, f32[256,256]{1,0:T(8,128)}, f32[256,256]{1,0:T(8,128)}, f32[256,256]{1,0:T(8,128)}, f32[256,256]{1,0:T(8,128)}, /*inde...) custom-call(f32[256,256]{1,0:T(8,128)} %lot.3, f32[256,256]{1,0:T(8,128)} %uol.3, ...), custom_call_target="tpu_custom_call" | custom-call | flops 603979776 | bytes 3670016 | tf_op jit(solution)/shard_map/prepare/pallas_call | solution.py:55
  22.4 0.8 collective-permute-done.2
  23.8 2.8 %collective-permute-done.5 = f32[16,2048]{1,0:T(8,128)S(1)} collective-permute-done((f32[16,2048]{1,0:T(8,128)}, f32[16,2048]{1,0:T(8,128)S(1)}, u32[]{:S(2)}, u32[]{:S(2)}) %collective-permute-start.5) | collective-permute-done | bytes 131104 | tf_op jit(solution)/shard_map/ppermute | solution.py:274
  26.9 1.1 collective-permute-start.10
  28.0 1.5 collective-permute-start.11
  29.4 2.2 %collective-permute-start.7 = (f32[64,2048]{1,0:T(8,128)S(1)}, f32[64,2048]{1,0:T(8,128)S(1)}, u32[]{:S(2)}, u32[]{:S(2)}) collective-permute-start(f32[64,2048]{1,0:T(8,128)S(1)} %get-tuple-element.72.rest_0_), channel_id=1, source_target_pairs={{0,16},{8,24},{16,0},{24,8},{1,17},{9,25},{17,1},{25,9},{2,18},{10... | collective-permute-start | bytes 1572872 | tf_op jit(solution)/shard_map/ppermute | solution.py:274
  31.6 1.7 %collective-permute-start.8 = (f32[64,2048]{1,0:T(8,128)S(1)}, f32[64,2048]{1,0:T(8,128)}, u32[]{:S(2)}, u32[]{:S(2)}) collective-permute-start(f32[64,2048]{1,0:T(8,128)S(1)} %get-tuple-element.72.rest_0_), channel_id=1, source_target_pairs={{0,24},{8,16},{16,8},{24,0},{1,25},{9,17},{17,9},{25,1},{2,26},{10... | collective-permute-start | bytes 1572872 | tf_op jit(solution)/shard_map/ppermute | solution.py:274
  33.3 7.1 %collective-permute-done.10.rest_6_ = f32[64,2048]{1,0:T(8,128)S(1)} collective-permute-done((f32[64,2048]{1,0:T(8,128)S(1)}, f32[64,2048]{1,0:T(8,128)S(1)}, u32[]{:S(2)}, u32[]{:S(2)}) %collective-permute-start.10) | collective-permute-done | bytes 524320 | tf_op jit(solution)/shard_map/ppermute | solution.py:274
  40.6 8.7 %band_products.1 = f32[16,16,2048]{2,1,0:T(8,128)} custom-call(f32[256,256]{1,0:T(8,128)} %get-tuple-element.71.triple.lower_triple, f32[256,256]{1,0:T(8,128)} %lio.5, f32[512,1024]{1,0:T(8,128)} %all-gather.3.cloned.1.call-done.lower, f32[1024,2048]{1,0:T(8,128)} %trail.3), custom_call_target="tpu_custom_call" | custom-call | flops 3221225472 | bytes 12582912 | tf_op jit(solution)/shard_map/band_products/pallas_call | solution.py:102
  49.3 5.6 %all-to-all-start = ((f32[16,16,2048]{2,1,0:T(8,128)}), f32[16,16,2048]{2,1,0:T(8,128)}, u32[]{:S(2)}, u32[]{:S(2)}) async-start(f32[16,16,2048]{2,1,0:T(8,128)} %band_products.1), calls=%async_computation | async-start | bytes 4194304 | tf_op jit(solution)/shard_map/all_to_all | solution.py:329
  55.2 14.5 %panel_products.1 = (f32[4,16,8,256]{3,2,1,0:T(8,128)S(1)}, f32[4,16,8,256]{3,2,1,0:T(8,128)S(1)}, f32[1024,256]{1,0:T(8,128)}) custom-call(s32[4]{0:T(128)S(1)} %pad_add_fusion.place, bf16[512,256]{1,0:T(8,128)(2,1)} %get-tuple-element.59.side_high, bf16[512,256]{1,0:T(8,128)(2,1)} %get-tuple-element.60.side_low, ...), custom_call_target="tpu_custom_call" | custom-call | flops 8858370048 | bytes 16777216 | tf_op jit(solution)/shard_map/panel_products/pallas_call | solution.py:180
  69.7 3.4 %collective-permute-start.12 = (f32[4,16,8,256]{3,2,1,0:T(8,128)S(1)}, f32[4,16,8,256]{3,2,1,0:T(8,128)S(1)}, u32[]{:S(2)}, u32[]{:S(2)}) collective-permute-start(f32[4,16,8,256]{3,2,1,0:T(8,128)S(1)} %get-tuple-element.81), channel_id=1, source_target_pairs={{0,1},{1,0},{2,3},{3,2},{4,5},{5,4},{6,7},{7,6},{8,9},{9,8},{10,11... | collective-permute-start | bytes 1572872 | tf_op jit(solution)/shard_map/ppermute | solution.py:274
  73.1 1.5 %collective-permute-done.12 = f32[4,16,8,256]{3,2,1,0:T(8,128)S(1)} collective-permute-done((f32[4,16,8,256]{3,2,1,0:T(8,128)S(1)}, f32[4,16,8,256]{3,2,1,0:T(8,128)S(1)}, u32[]{:S(2)}, u32[]{:S(2)}) %collective-permute-start.12) | collective-permute-done | bytes 524320 | tf_op jit(solution)/shard_map/ppermute | solution.py:274
  74.8 1.3 collective-permute-start.13
  76.1 2.4 %collective-permute-start.14 = (f32[16,8,256]{2,1,0:T(8,128)S(1)}, f32[16,8,256]{2,1,0:T(8,128)S(1)}, u32[]{:S(2)}, u32[]{:S(2)}) collective-permute-start(f32[16,8,256]{2,1,0:T(8,128)S(1)} %get-tuple-element.97), channel_id=1, source_target_pairs={{0,4},{2,6},{4,0},{6,2},{1,5},{3,7},{5,1},{7,3},{8,12},{10,14},{12... | collective-permute-start | bytes 393224 | tf_op jit(solution)/shard_map/ppermute | solution.py:274
  78.7 1.0 collective-permute-done.13
  79.7 5.1 %collective-permute-done.14 = f32[16,8,256]{2,1,0:T(8,128)S(1)} collective-permute-done((f32[16,8,256]{2,1,0:T(8,128)S(1)}, f32[16,8,256]{2,1,0:T(8,128)S(1)}, u32[]{:S(2)}, u32[]{:S(2)}) %collective-permute-start.14) | collective-permute-done | bytes 131104 | tf_op jit(solution)/shard_map/ppermute | solution.py:274
  84.7 2.4 %collective-permute-done.15 = f32[16,8,256]{2,1,0:T(8,128)S(1)} collective-permute-done((f32[16,8,256]{2,1,0:T(8,128)S(1)}, f32[16,8,256]{2,1,0:T(8,128)S(1)}, u32[]{:S(2)}, u32[]{:S(2)}) %collective-permute-start.15) | collective-permute-done | bytes 131104 | tf_op jit(solution)/shard_map/ppermute | solution.py:274
  87.1 2.4 %reduce_sum.27 = f32[16,2048]{1,0:T(8,128)} reduce(f32[16,16,2048]{2,1,0:T(8,128)} %all-to-all-done, f32[]{:T(128)} %constant.7.clone.1), dimensions={0}, to_apply=%region_0.0 | reduce | flops 491520 | bytes 2228228 | tf_op jit(solution)/shard_map/reduce_sum | solution.py:337
  89.5 15.8 %all_to_all.21 = f32[16,8,256]{2,1,0:T(8,128)S(1)} all-to-all(f32[16,8,256]{2,1,0:T(8,128)S(1)} %fusion), channel_id=1, replica_groups=mesh['z'=4,'y'=4,'x'=4,'c'=2] {'z','y'}, dimensions={0} | all-to-all | bytes 262144 | tf_op jit(solution)/shard_map/all_to_all | solution.py:278
  105.4 15.1 %all_to_all.20.mine = f32[64,8,256]{2,1,0:T(8,128)S(1)} all-to-all(f32[64,8,256]{2,1,0:T(8,128)S(1)} %broadcast_in_dim.2), channel_id=1, replica_groups=mesh['z'=4,'y'=4,'x'=4,'c'=2] {'z','y','x'}, dimensions={0} | all-to-all | bytes 1048576 | tf_op jit(solution)/shard_map/all_to_all | solution.py:278
  120.5 6.7 %all-to-all-start.3 = ((f32[8,128,256]{2,1,0:T(8,128)}), f32[8,128,256]{2,1,0:T(8,128)S(1)}, u32[]{:S(2)}, u32[]{:S(2)}) async-start(f32[8,128,256]{2,1,0:T(8,128)} %bitcast.10), calls=%async_computation.3 | async-start | bytes 2097152 | tf_op jit(solution)/shard_map/all_to_all | solution.py:278
  127.4 1.7 %collective-permute-done.16.other = f32[64,8,256]{2,1,0:T(8,128)S(1)} collective-permute-done((f32[64,8,256]{2,1,0:T(8,128)S(1)}, f32[64,8,256]{2,1,0:T(8,128)S(1)}, u32[]{:S(2)}, u32[]{:S(2)}) %collective-permute-start.16) | collective-permute-done | bytes 524320 | tf_op jit(solution)/shard_map/ppermute | solution.py:274
  129.2 6.1 %finish.1 = (f32[256,256]{1,0:T(8,128)}, f32[256,256]{1,0:T(8,128)}, f32[256,256]{1,0:T(8,128)}) custom-call(s32[4]{0:T(128)} %copy-done, f32[64,8,256]{2,1,0:T(8,128)S(1)} %all_to_all.20.mine, f32[64,8,256]{2,1,0:T(8,128)S(1)} %collective-permute-done.16.other, f32[256,256]{1,0:T(8,128)} %get-tuple-element.85.x_new, f32[256,256]{1,0:T(8,128)} %get-tuple-element.86.y_new, ...), custom_call_target="tpu_custom_call" | custom-call | flops 4026531840 | bytes 5505024 | tf_op jit(solution)/shard_map/finish/pallas_call | solution.py:259
  135.3 7.1 %all-to-all-done.3 = f32[8,128,256]{2,1,0:T(8,128)S(1)} async-done(((f32[8,128,256]{2,1,0:T(8,128)}), f32[8,128,256]{2,1,0:T(8,128)S(1)}, u32[]{:S(2)}, u32[]{:S(2)}) %all-to-all-start.3) | async-done | bytes 1048608 | tf_op jit(solution)/shard_map/all_to_all | solution.py:278
  142.4 0.7 reduce_sum.29
  143.1 3.1 %neg.3 = f32[256,2048]{1,0:T(8,128)} negate(f32[256,2048]{1,0:T(8,128)} %all-gather.5.cloned.1.call-done) | non-fusion elementwise | flops 524288 | bytes 4194304 | tf_op jit(solution)/shard_map/neg | solution.py:348
  (43 shorter events, 1.8 us)
Async XLA Ops:
  7.2 19.4 %copy-start.1 = (f32[16,2048]{1,0:T(8,128)S(1)}, f32[16,2048]{1,0:T(8,128)}, u32[]{:S(2)}) copy-start(f32[16,2048]{1,0:T(8,128)} %param.17) | copy-start | bytes 393220
  7.2 33.5 %all-gather.3.cloned.1.call-start = ((), (), s32[]{:S(2)}) async-start(), calls=%async_computation.4 | async-start | bytes 2359296 | tf_op jit(solution)/shard_map/all_gather | solution.py:320
  9.0 17.8 %copy-start.2 = (f32[16,2048]{1,0:T(8,128)S(1)}, f32[16,2048]{1,0:T(8,128)}, u32[]{:S(2)}) copy-start(f32[16,2048]{1,0:T(8,128)} %param.21) | copy-start | bytes 393220
  9.0 9.8 %collective-permute-start = (f32[16,2048]{1,0:T(8,128)}, f32[16,2048]{1,0:T(8,128)S(1)}, u32[]{:S(2)}, u32[]{:S(2)}) collective-permute-start(f32[16,2048]{1,0:T(8,128)} %param.17), channel_id=1, source_target_pairs={{0,32},{32,0},{64,96},{96,64},{1,33},{33,1},{65,97},{97,65},{2,34}... | collective-permute-start | bytes 393224 | tf_op jit(solution)/shard_map/ppermute | solution.py:274
  11.5 10.9 %collective-permute-start.1 = (f32[16,2048]{1,0:T(8,128)}, f32[16,2048]{1,0:T(8,128)S(1)}, u32[]{:S(2)}, u32[]{:S(2)}) collective-permute-start(f32[16,2048]{1,0:T(8,128)} %param.17), channel_id=1, source_target_pairs={{0,64},{32,96},{64,0},{96,32},{1,65},{33,97},{65,1},{97,33},{2,66}... | collective-permute-start | bytes 393224 | tf_op jit(solution)/shard_map/ppermute | solution.py:274
  14.8 8.4 %collective-permute-start.2 = (f32[16,2048]{1,0:T(8,128)}, f32[16,2048]{1,0:T(8,128)S(1)}, u32[]{:S(2)}, u32[]{:S(2)}) collective-permute-start(f32[16,2048]{1,0:T(8,128)} %param.17), channel_id=1, source_target_pairs={{0,96},{32,64},{64,32},{96,0},{1,97},{33,65},{65,33},{97,1},{2,98}... | collective-permute-start | bytes 393224 | tf_op jit(solution)/shard_map/ppermute | solution.py:274
  14.8 8.4 %collective-permute-start.3 = (f32[16,2048]{1,0:T(8,128)}, f32[16,2048]{1,0:T(8,128)S(1)}, u32[]{:S(2)}, u32[]{:S(2)}) collective-permute-start(f32[16,2048]{1,0:T(8,128)} %param.21), channel_id=1, source_target_pairs={{0,8},{8,0},{16,24},{24,16},{1,9},{9,1},{17,25},{25,17},{2,10},{10... | collective-permute-start | bytes 393224 | tf_op jit(solution)/shard_map/ppermute | solution.py:274
  16.1 7.6 %collective-permute-start.4 = (f32[16,2048]{1,0:T(8,128)}, f32[16,2048]{1,0:T(8,128)S(1)}, u32[]{:S(2)}, u32[]{:S(2)}) collective-permute-start(f32[16,2048]{1,0:T(8,128)} %param.21), channel_id=1, source_target_pairs={{0,16},{8,24},{16,0},{24,8},{1,17},{9,25},{17,1},{25,9},{2,18},{10... | collective-permute-start | bytes 393224 | tf_op jit(solution)/shard_map/ppermute | solution.py:274
  18.8 7.8 %collective-permute-start.5 = (f32[16,2048]{1,0:T(8,128)}, f32[16,2048]{1,0:T(8,128)S(1)}, u32[]{:S(2)}, u32[]{:S(2)}) collective-permute-start(f32[16,2048]{1,0:T(8,128)} %param.21), channel_id=1, source_target_pairs={{0,24},{8,16},{16,8},{24,0},{1,25},{9,17},{17,9},{25,1},{2,26},{10... | collective-permute-start | bytes 393224 | tf_op jit(solution)/shard_map/ppermute | solution.py:274
  26.9 13.5 %collective-permute-start.10 = (f32[64,2048]{1,0:T(8,128)S(1)}, f32[64,2048]{1,0:T(8,128)S(1)}, u32[]{:S(2)}, u32[]{:S(2)}) collective-permute-start(f32[64,2048]{1,0:T(8,128)S(1)} %get-tuple-element.76.rest_4_), channel_id=1, source_target_pairs={{0,64},{32,96},{64,0},{96,32},{1,65},{33,97},{65,1},{97,33},{2,66}... | collective-permute-start | bytes 1572872 | tf_op jit(solution)/shard_map/ppermute | solution.py:274
  28.0 27.2 %collective-permute-start.11 = (f32[64,2048]{1,0:T(8,128)S(1)}, f32[64,2048]{1,0:T(8,128)S(1)}, u32[]{:S(2)}, u32[]{:S(2)}) collective-permute-start(f32[64,2048]{1,0:T(8,128)S(1)} %get-tuple-element.76.rest_4_), channel_id=1, source_target_pairs={{0,96},{32,64},{64,32},{96,0},{1,97},{33,65},{65,33},{97,1},{2,98}... | collective-permute-start | bytes 1572872 | tf_op jit(solution)/shard_map/ppermute | solution.py:274
  29.4 25.7 %collective-permute-start.6 = (f32[64,2048]{1,0:T(8,128)S(1)}, f32[64,2048]{1,0:T(8,128)S(1)}, u32[]{:S(2)}, u32[]{:S(2)}) collective-permute-start(f32[64,2048]{1,0:T(8,128)S(1)} %get-tuple-element.72.rest_0_), channel_id=1, source_target_pairs={{0,8},{8,0},{16,24},{24,16},{1,9},{9,1},{17,25},{25,17},{2,10},{10... | collective-permute-start | bytes 1572872 | tf_op jit(solution)/shard_map/ppermute | solution.py:274
  29.4 25.7 %collective-permute-start.7 = (f32[64,2048]{1,0:T(8,128)S(1)}, f32[64,2048]{1,0:T(8,128)S(1)}, u32[]{:S(2)}, u32[]{:S(2)}) collective-permute-start(f32[64,2048]{1,0:T(8,128)S(1)} %get-tuple-element.72.rest_0_), channel_id=1, source_target_pairs={{0,16},{8,24},{16,0},{24,8},{1,17},{9,25},{17,1},{25,9},{2,18},{10... | collective-permute-start | bytes 1572872 | tf_op jit(solution)/shard_map/ppermute | solution.py:274
  31.6 23.5 %collective-permute-start.8 = (f32[64,2048]{1,0:T(8,128)S(1)}, f32[64,2048]{1,0:T(8,128)}, u32[]{:S(2)}, u32[]{:S(2)}) collective-permute-start(f32[64,2048]{1,0:T(8,128)S(1)} %get-tuple-element.72.rest_0_), channel_id=1, source_target_pairs={{0,24},{8,16},{16,8},{24,0},{1,25},{9,17},{17,9},{25,1},{2,26},{10... | collective-permute-start | bytes 1572872 | tf_op jit(solution)/shard_map/ppermute | solution.py:274
  40.4 14.8 %collective-permute-start.9 = (f32[64,2048]{1,0:T(8,128)S(1)}, f32[64,2048]{1,0:T(8,128)}, u32[]{:S(2)}, u32[]{:S(2)}) collective-permute-start(f32[64,2048]{1,0:T(8,128)S(1)} %get-tuple-element.76.rest_4_), channel_id=1, source_target_pairs={{0,32},{32,0},{64,96},{96,64},{1,33},{33,1},{65,97},{97,65},{2,34}... | collective-permute-start | bytes 1572872 | tf_op jit(solution)/shard_map/ppermute | solution.py:274
  49.3 37.8 %all-to-all-start = ((f32[16,16,2048]{2,1,0:T(8,128)}), f32[16,16,2048]{2,1,0:T(8,128)}, u32[]{:S(2)}, u32[]{:S(2)}) async-start(f32[16,16,2048]{2,1,0:T(8,128)} %band_products.1), calls=%async_computation | async-start | bytes 4194304 | tf_op jit(solution)/shard_map/all_to_all | solution.py:329
  55.0 88.1 %all-gather.5.cloned.1.call-start = ((), (), s32[]{:S(2)}) async-start(), calls=%async_computation.5 | async-start | bytes 2228224 | tf_op jit(solution)/shard_map/all_gather | solution.py:338
  55.1 14.6 %copy-start = (s32[4]{0:T(128)}, s32[4]{0:T(128)S(1)}, u32[]{:S(2)}) copy-start(s32[4]{0:T(128)S(1)} %pad_add_fusion.place) | copy-start | bytes 52
  69.7 4.9 %collective-permute-start.12 = (f32[4,16,8,256]{3,2,1,0:T(8,128)S(1)}, f32[4,16,8,256]{3,2,1,0:T(8,128)S(1)}, u32[]{:S(2)}, u32[]{:S(2)}) collective-permute-start(f32[4,16,8,256]{3,2,1,0:T(8,128)S(1)} %get-tuple-element.81), channel_id=1, source_target_pairs={{0,1},{1,0},{2,3},{3,2},{4,5},{5,4},{6,7},{7,6},{8,9},{9,8},{10,11... | collective-permute-start | bytes 1572872 | tf_op jit(solution)/shard_map/ppermute | solution.py:274
  74.8 4.9 %collective-permute-start.13 = (f32[16,8,256]{2,1,0:T(8,128)S(1)}, f32[16,8,256]{2,1,0:T(8,128)S(1)}, u32[]{:S(2)}, u32[]{:S(2)}) collective-permute-start(f32[16,8,256]{2,1,0:T(8,128)S(1)} %get-tuple-element.99), channel_id=1, source_target_pairs={{0,2},{2,0},{4,6},{6,4},{1,3},{3,1},{5,7},{7,5},{8,10},{10,8},{12,... | collective-permute-start | bytes 393224 | tf_op jit(solution)/shard_map/ppermute | solution.py:274
  76.1 8.7 %collective-permute-start.14 = (f32[16,8,256]{2,1,0:T(8,128)S(1)}, f32[16,8,256]{2,1,0:T(8,128)S(1)}, u32[]{:S(2)}, u32[]{:S(2)}) collective-permute-start(f32[16,8,256]{2,1,0:T(8,128)S(1)} %get-tuple-element.97), channel_id=1, source_target_pairs={{0,4},{2,6},{4,0},{6,2},{1,5},{3,7},{5,1},{7,3},{8,12},{10,14},{12... | collective-permute-start | bytes 393224 | tf_op jit(solution)/shard_map/ppermute | solution.py:274
  78.5 8.6 %collective-permute-start.15 = (f32[16,8,256]{2,1,0:T(8,128)S(1)}, f32[16,8,256]{2,1,0:T(8,128)S(1)}, u32[]{:S(2)}, u32[]{:S(2)}) collective-permute-start(f32[16,8,256]{2,1,0:T(8,128)S(1)} %get-tuple-element.98), channel_id=1, source_target_pairs={{0,6},{2,4},{4,2},{6,0},{1,7},{3,5},{5,3},{7,1},{8,14},{10,12},{12... | collective-permute-start | bytes 393224 | tf_op jit(solution)/shard_map/ppermute | solution.py:274
  120.5 21.9 %all-to-all-start.3 = ((f32[8,128,256]{2,1,0:T(8,128)}), f32[8,128,256]{2,1,0:T(8,128)S(1)}, u32[]{:S(2)}, u32[]{:S(2)}) async-start(f32[8,128,256]{2,1,0:T(8,128)} %bitcast.10), calls=%async_computation.3 | async-start | bytes 2097152 | tf_op jit(solution)/shard_map/all_to_all | solution.py:278
  127.3 1.9 %collective-permute-start.16 = (f32[64,8,256]{2,1,0:T(8,128)S(1)}, f32[64,8,256]{2,1,0:T(8,128)S(1)}, u32[]{:S(2)}, u32[]{:S(2)}) collective-permute-start(f32[64,8,256]{2,1,0:T(8,128)S(1)} %all_to_all.20.mine), channel_id=1, source_target_pairs={{0,1},{1,0},{2,3},{3,2},{4,5},{5,4},{6,7},{7,6},{8,9},{9,8},{10,11... | collective-permute-start | bytes 1572872 | tf_op jit(solution)/shard_map/ppermute | solution.py:274
Sparse Core Ops, SparseCore 0:
  10.3 28.7 all-gather.2
  89.6 47.7 all-gather.4

commit v6 on v4

--- a/solution.py
+++ b/solution.py
@@ -94,7 +94,7 @@
         out[k] = band[k * size : (k + 1) * size, :]
 
 
-def band_products(triple, lio, lower, trail, ranks, count, tile=512):
+def band_products(triple, lio, lower, trail, ranks, count, tile=1024):
     rows, columns = trail.shape
     width = lio.shape[0]
     once = pl.Buffered(1)
@@ -123,7 +123,7 @@
 
 def panel_kernel(count, tile, place, side_high, side_low, lower, trail, *rest):
     pieces = rest[:8]
-    mine, other, strip, upper_high, upper_low, inner = rest[8:]
+    mine, other, strip, strip_beside, upper_high, upper_low, inner = rest[8:]
     width = side_high.shape[1]
     z, y, x, c = place[0], place[1], place[2], place[3]
     piece = width // count
@@ -140,13 +140,16 @@
                     pieces[k][q * chunk : (q + 1) * chunk, :]
                 )
 
-    def step(lower_tile, trail_tile, strip_tile):
+    def step(lower_tile, trail_tile, near_tile, beside_tile):
         pl.when(pl.program_id(0) == 0)(assemble)
         product = close(
             parts(trail_tile[...]), (upper_high[...], upper_low[...]), ((1,), (1,))
         )
         product = parts(product)
-        strip_tile[...] = close(product, (side_high[...], side_low[...]))
+        result = close(product, (side_high[...], side_low[...]))
+        first, second = result[: tile // 2, :], result[tile // 2 :, :]
+        near_tile[...] = jnp.where(c == 0, first, second)
+        beside_tile[...] = jnp.where(c == 0, second, first)
         for panel in range(2):
             left = parts(lower_rows(lower_tile, panel, count, piece))
             inner[panel * width : (panel + 1) * width, :] += close(left, product)
@@ -158,8 +161,8 @@
             pl.BlockSpec((lower.shape[0], tile), lambda i: (0, i)),
             pl.BlockSpec((tile, trail.shape[1]), lambda i: (i, 0)),
         ],
-        out_specs=[pl.BlockSpec((tile, width), lambda i: (i, 0))],
-    )(lower, trail, strip)
+        out_specs=[pl.BlockSpec((tile // 2, width), lambda i: (i ^ x, 0))] * 2,
+    )(lower, trail, strip, strip_beside)
 
     rows, share = mine.shape[2], width // 4
     for k in range(4):
@@ -182,10 +185,11 @@
         out_shape=(
             jax.ShapeDtypeStruct(share, FULL),
             jax.ShapeDtypeStruct(share, FULL),
-            jax.ShapeDtypeStruct((rows, width), FULL),
+            jax.ShapeDtypeStruct((rows // 2, width), FULL),
+            jax.ShapeDtypeStruct((rows // 2, width), FULL),
         ),
         in_specs=[pl.BlockSpec(memory_space=pltpu.SMEM)] + [VMEM] * 2 + [hbm] * 2 + [VMEM] * 8,
-        out_specs=(VMEM, VMEM, hbm),
+        out_specs=(VMEM, VMEM, hbm, hbm),
         scratch_shapes=[pltpu.VMEM((2 * width, columns), HALF)] * 2
         + [pltpu.VMEM((2 * width, 2 * width), FULL)],
         compiler_params=pltpu.CompilerParams(vmem_limit_bytes=36 << 20),
@@ -329,23 +333,26 @@
     band = lax.all_to_all(band, row, 0, 0, tiled=True)
 
     place = jnp.stack([lax.axis_index(a) for a in row + col]).astype(jnp.int32)
-    mine, other, strip = panel_products(
+    mine, other, strip, beside = panel_products(
         place, (side_high, side_low), lower_stack, trail, pieces, count
     )
     mine = mine + swap(other, "c", 1)
     mine = mine[0] + sum(swap(mine[k], "x", k) for k in (1, 2, 3))
     mine, band = together(mine, band.sum(0))
     band_right = -lax.all_gather(-band, row, axis=0, tiled=True)
+    beside = swap(beside, "c", 1)
     mine = exchange(mine, row).sum(0)
+    mine, beside = together(mine, beside)
+    strip = (strip + beside).reshape(4, -1, strip.shape[1])
+    arrived = [swap(strip[k], "x", k) for k in (1, 2, 3)]
     mine = exchange(jnp.broadcast_to(mine[None], (4 * ranks, *mine.shape)), row + ("x",))
-    mine, strip = together(mine, strip)
-    strip = exchange(strip.reshape(count, -1, strip.shape[1]), col)
+    mine, *arrived = together(mine, *arrived)
+    strip_bottom = strip[0] + sum(arrived)
     other = swap(mine, "c", 1)
     corner_old, strip_top, band_left = finish(
         place, mine, other, *small, lot, uol, lin, uin, ldo, udo, lio, uio
     )
-    strip, corner_old, band_right = together(strip, corner_old, band_right)
-    return corner_old, strip_top, strip.sum(0), band_left, band_right
+    return corner_old, strip_top, strip_bottom, band_left, band_right
 
 
 def solution(mesh):

time: 148 us -> 150 us (1.014)
  blocking collectives: 28.7 us -> 15.1 us
  starting transfers between devices: 35.9 us -> 41.7 us
  local copies, waits for them, and re-layouts: 0.28 us -> 4.78 us
  waiting for transfers between devices: 26.9 us -> 31.1 us
    all_to_all x2 -> x1, blocking collectives: 28.7 us -> 15.1 us  [exchange(): return lax.all_to_all(value, axes, 0, 0, tiled=True)]
    ppermute x17 -> x21, waiting for transfers between devices: 22.9 us -> 31 us  [swap(): return lax.ppermute(value, axis, [(i, i ^ step) for i in range(size)])]
    ppermute x17 -> x21, starting transfers between devices: 23.6 us -> 31.3 us  [swap(): return lax.ppermute(value, axis, [(i, i ^ step) for i in range(size)])]
    unnamed x6 -> x14, local copies, waits for them, and re-layouts: 0.02 us -> 3.7 us
    all_gather x1, waiting for transfers between devices: 2.28 us -> 0.01 us  [body(): band_right = -lax.all_gather(-band, row, axis=0, tiled=True)]
    all_to_all x1, starting transfers between devices: 6.67 us -> 4.64 us  [exchange(): return lax.all_to_all(value, axes, 0, 0, tiled=True)]
    all_to_all x1, waiting for transfers between devices: 1.7 us -> 0.01 us  [exchange(): return lax.all_to_all(value, axes, 0, 0, tiled=True)]
  transfers between devices with their start and end apart: 21 -> 25, of which waited for: 11 -> 11; matrix products, arithmetic and copies ran while one was open for 2% -> 1% of each run, Pallas kernels for 23% -> 23%
where the time goes in v6:
time: 150 us; the launch traced here: 149 us
  starting transfers between devices  41.7 us (28%)
  Pallas kernels  33.8 us (23%)
  waiting for transfers between devices  31.1 us (21%)
  blocking collectives  15.1 us (10%)
  between operations  14.3 us (10%)
  other arithmetic  8.2 us (5%)
  local copies, waits for them, and re-layouts  4.78 us (3%)
    ppermute x21, starting transfers between devices, swap(): return lax.ppermute(value, axis, [(i, i ^ step) for i in range(size)])  31.3 us
    ppermute x21, waiting for transfers between devices, swap(): return lax.ppermute(value, axis, [(i, i ^ step) for i in range(size)])  31 us
    pallas_call x1, Pallas kernels, panel_products(): pl.pallas_call(functools.partial(panel_kernel, count, tile), out_shape=(j...  15.5 us
    all_to_all x1, blocking collectives, exchange(): return lax.all_to_all(value, axes, 0, 0, tiled=True)  15.1 us
    pallas_call x1, Pallas kernels, band_products(): pl.pallas_call(functools.partial(band_kernel, count), out_shape=jax.Shape...  8.66 us
    pallas_call x1, Pallas kernels, finish(): pl.pallas_call(finish_kernel, out_shape=(jax.ShapeDtypeStruct((width, wid...  6.04 us
    all_to_all x1, starting transfers between devices, body(): band = lax.all_to_all(band, row, 0, 0, tiled=True)  5.63 us
    all_to_all x1, starting transfers between devices, exchange(): return lax.all_to_all(value, axes, 0, 0, tiled=True)  4.64 us
  transfers between devices with their start and end apart: 25, of which 11 were waited for; matrix products, arithmetic and copies ran while one was open for 1% of the time, Pallas kernels for 23%

profile of v6, /device:TPU:1, one launch (start us, length us, event | category | flops | bytes accessed | tf_op | source)
XLA Modules:
  0.0 148.9 jit_solution(5862385914721219895)
XLA Ops:
  7.2 1.7 %pad_maximum_fusion = f32[64,1024]{1,0:T(8,128)} fusion(f32[32,1024]{1,0:T(8,128)} %bitcast.16, f32[32,1024]{1,0:T(8,128)} %bitcast.17), kind=kLoop, calls=%fused_computation | loop fusion | flops 65536 | bytes 524288 | tf_op jit(solution)/shard_map/concatenate | solution.py:323
  9.0 2.5 %collective-permute-start = (f32[16,2048]{1,0:T(8,128)}, f32[16,2048]{1,0:T(8,128)S(1)}, u32[]{:S(2)}, u32[]{:S(2)}) collective-permute-start(f32[16,2048]{1,0:T(8,128)} %param.17), channel_id=1, source_target_pairs={{0,32},{32,0},{64,96},{96,64},{1,33},{33,1},{65,97},{97,65},{2,34}... | collective-permute-start | bytes 393224 | tf_op jit(solution)/shard_map/ppermute | solution.py:278
  11.5 3.3 %collective-permute-start.1 = (f32[16,2048]{1,0:T(8,128)}, f32[16,2048]{1,0:T(8,128)S(1)}, u32[]{:S(2)}, u32[]{:S(2)}) collective-permute-start(f32[16,2048]{1,0:T(8,128)} %param.17), channel_id=1, source_target_pairs={{0,64},{32,96},{64,0},{96,32},{1,65},{33,97},{65,1},{97,33},{2,66}... | collective-permute-start | bytes 393224 | tf_op jit(solution)/shard_map/ppermute | solution.py:278
  14.8 1.3 collective-permute-start.3
  16.1 2.6 %collective-permute-start.4 = (f32[16,2048]{1,0:T(8,128)}, f32[16,2048]{1,0:T(8,128)S(1)}, u32[]{:S(2)}, u32[]{:S(2)}) collective-permute-start(f32[16,2048]{1,0:T(8,128)} %param.21), channel_id=1, source_target_pairs={{0,16},{8,24},{16,0},{24,8},{1,17},{9,25},{17,1},{25,9},{2,18},{10... | collective-permute-start | bytes 393224 | tf_op jit(solution)/shard_map/ppermute | solution.py:278
  18.8 3.7 %prepare.1 = (f32[256,256]{1,0:T(8,128)}, f32[256,256]{1,0:T(8,128)}, f32[256,256]{1,0:T(8,128)}, f32[256,256]{1,0:T(8,128)}, f32[256,256]{1,0:T(8,128)}, /*inde...) custom-call(f32[256,256]{1,0:T(8,128)} %lot.3, f32[256,256]{1,0:T(8,128)} %uol.3, ...), custom_call_target="tpu_custom_call" | custom-call | flops 603979776 | bytes 3670016 | tf_op jit(solution)/shard_map/prepare/pallas_call | solution.py:55
  23.8 2.8 %collective-permute-done.5 = f32[16,2048]{1,0:T(8,128)S(1)} collective-permute-done((f32[16,2048]{1,0:T(8,128)}, f32[16,2048]{1,0:T(8,128)S(1)}, u32[]{:S(2)}, u32[]{:S(2)}) %collective-permute-start.5) | collective-permute-done | bytes 131104 | tf_op jit(solution)/shard_map/ppermute | solution.py:278
  26.9 1.1 collective-permute-start.10
  28.0 1.5 collective-permute-start.11
  29.4 2.2 %collective-permute-start.7 = (f32[64,2048]{1,0:T(8,128)S(1)}, f32[64,2048]{1,0:T(8,128)S(1)}, u32[]{:S(2)}, u32[]{:S(2)}) collective-permute-start(f32[64,2048]{1,0:T(8,128)S(1)} %get-tuple-element.75.rest_0_), channel_id=1, source_target_pairs={{0,16},{8,24},{16,0},{24,8},{1,17},{9,25},{17,1},{25,9},{2,18},{10... | collective-permute-start | bytes 1572872 | tf_op jit(solution)/shard_map/ppermute | solution.py:278
  31.6 1.7 %collective-permute-start.8 = (f32[64,2048]{1,0:T(8,128)S(1)}, f32[64,2048]{1,0:T(8,128)}, u32[]{:S(2)}, u32[]{:S(2)}) collective-permute-start(f32[64,2048]{1,0:T(8,128)S(1)} %get-tuple-element.75.rest_0_), channel_id=1, source_target_pairs={{0,24},{8,16},{16,8},{24,0},{1,25},{9,17},{17,9},{25,1},{2,26},{10... | collective-permute-start | bytes 1572872 | tf_op jit(solution)/shard_map/ppermute | solution.py:278
  33.3 7.1 %collective-permute-done.10.rest_6_ = f32[64,2048]{1,0:T(8,128)S(1)} collective-permute-done((f32[64,2048]{1,0:T(8,128)S(1)}, f32[64,2048]{1,0:T(8,128)S(1)}, u32[]{:S(2)}, u32[]{:S(2)}) %collective-permute-start.10) | collective-permute-done | bytes 524320 | tf_op jit(solution)/shard_map/ppermute | solution.py:278
  40.6 8.7 %band_products.1 = f32[16,16,2048]{2,1,0:T(8,128)} custom-call(f32[256,256]{1,0:T(8,128)} %get-tuple-element.74.triple.lower_triple, f32[256,256]{1,0:T(8,128)} %lio.5, f32[512,1024]{1,0:T(8,128)} %all-gather.3.cloned.1.call-done.lower, f32[1024,2048]{1,0:T(8,128)} %trail.3), custom_call_target="tpu_custom_call" | custom-call | flops 3221225472 | bytes 12582912 | tf_op jit(solution)/shard_map/band_products/pallas_call | solution.py:102
  49.3 5.6 %all-to-all-start = ((f32[16,16,2048]{2,1,0:T(8,128)}), f32[16,16,2048]{2,1,0:T(8,128)}, u32[]{:S(2)}, u32[]{:S(2)}) async-start(f32[16,16,2048]{2,1,0:T(8,128)} %band_products.1), calls=%async_computation | async-start | bytes 4194304 | tf_op jit(solution)/shard_map/all_to_all | solution.py:333
  57.8 1.0 copy-done.4
  58.8 15.5 %panel_products.1 = (f32[4,16,8,256]{3,2,1,0:T(8,128)S(1)}, f32[4,16,8,256]{3,2,1,0:T(8,128)S(1)}, f32[512,256]{1,0:T(8,128)S(1)}, f32[512,256]{1,0:T(8,128)S(1)}) custom-call(s32[4]{0:T(128)S(1)} %pad_add_fusion.place, bf16[512,256]{1,0:T(8,128)(2,1)} %get-tuple-element.62.side_high, bf16[512,256]{1,0:T(8,128)(2,1)} %get-tuple-element.63.side_low, ...), custom_call_target="tpu_custom_call" | custom-call | flops 8858370048 | bytes 16777216 | tf_op jit(solution)/shard_map/panel_products/pallas_call | solution.py:183
  74.3 3.0 %collective-permute-start.12 = (f32[4,16,8,256]{3,2,1,0:T(8,128)S(1)}, f32[4,16,8,256]{3,2,1,0:T(8,128)S(1)}, u32[]{:S(2)}, u32[]{:S(2)}) collective-permute-start(f32[4,16,8,256]{3,2,1,0:T(8,128)S(1)} %get-tuple-element.84), channel_id=1, source_target_pairs={{0,1},{1,0},{2,3},{3,2},{4,5},{5,4},{6,7},{7,6},{8,9},{9,8},{10,11... | collective-permute-start | bytes 1572872 | tf_op jit(solution)/shard_map/ppermute | solution.py:278
  77.3 1.5 %collective-permute-done.12 = f32[4,16,8,256]{3,2,1,0:T(8,128)S(1)} collective-permute-done((f32[4,16,8,256]{3,2,1,0:T(8,128)S(1)}, f32[4,16,8,256]{3,2,1,0:T(8,128)S(1)}, u32[]{:S(2)}, u32[]{:S(2)}) %collective-permute-start.12) | collective-permute-done | bytes 524320 | tf_op jit(solution)/shard_map/ppermute | solution.py:278
  78.9 1.3 collective-permute-start.13
  80.2 2.4 %collective-permute-start.14 = (f32[16,8,256]{2,1,0:T(8,128)S(1)}, f32[16,8,256]{2,1,0:T(8,128)S(1)}, u32[]{:S(2)}, u32[]{:S(2)}) collective-permute-start(f32[16,8,256]{2,1,0:T(8,128)S(1)} %get-tuple-element.106), channel_id=1, source_target_pairs={{0,4},{2,6},{4,0},{6,2},{1,5},{3,7},{5,1},{7,3},{8,12},{10,14},{12... | collective-permute-start | bytes 393224 | tf_op jit(solution)/shard_map/ppermute | solution.py:278
  83.8 4.9 %collective-permute-done.14 = f32[16,8,256]{2,1,0:T(8,128)S(1)} collective-permute-done((f32[16,8,256]{2,1,0:T(8,128)S(1)}, f32[16,8,256]{2,1,0:T(8,128)S(1)}, u32[]{:S(2)}, u32[]{:S(2)}) %collective-permute-start.14) | collective-permute-done | bytes 131104 | tf_op jit(solution)/shard_map/ppermute | solution.py:278
  88.8 2.5 %collective-permute-done.15 = f32[16,8,256]{2,1,0:T(8,128)S(1)} collective-permute-done((f32[16,8,256]{2,1,0:T(8,128)S(1)}, f32[16,8,256]{2,1,0:T(8,128)S(1)}, u32[]{:S(2)}, u32[]{:S(2)}) %collective-permute-start.15) | collective-permute-done | bytes 131104 | tf_op jit(solution)/shard_map/ppermute | solution.py:278
  91.3 1.7 %reduce_sum.18 = f32[16,2048]{1,0:T(8,128)S(1)} reduce(f32[16,16,2048]{2,1,0:T(8,128)} %all-to-all-done, f32[]{:T(128)} %constant.7.clone.1), dimensions={0}, to_apply=%region_0.0 | reduce | flops 491520 | bytes 2228228 | tf_op jit(solution)/shard_map/reduce_sum | solution.py:341
  93.7 1.1 collective-permute-start.16
  94.8 15.1 %all_to_all.15 = f32[16,8,256]{2,1,0:T(8,128)S(1)} all-to-all(f32[16,8,256]{2,1,0:T(8,128)S(1)} %fusion), channel_id=1, replica_groups=mesh['z'=4,'y'=4,'x'=4,'c'=2] {'z','y'}, dimensions={0} | all-to-all | bytes 262144 | tf_op jit(solution)/shard_map/all_to_all | solution.py:282
  110.8 4.6 %all-to-all-start.2 = ((f32[64,8,256]{2,1,0:T(8,128)}), f32[64,8,256]{2,1,0:T(8,128)S(1)}, u32[]{:S(2)}, u32[]{:S(2)}) async-start(f32[64,8,256]{2,1,0:T(8,128)} %broadcast_in_dim.2), calls=%async_computation.2 | async-start | bytes 1048576 | tf_op jit(solution)/shard_map/all_to_all | solution.py:282
  116.5 2.4 %collective-permute-start.18 = (f32[128,256]{1,0:T(8,128)S(1)}, f32[128,256]{1,0:T(8,128)S(1)}, u32[]{:S(2)}, u32[]{:S(2)}) collective-permute-start(f32[128,256]{1,0:T(8,128)S(1)} %get-tuple-element.104), channel_id=1, source_target_pairs={{0,4},{2,6},{4,0},{6,2},{1,5},{3,7},{5,1},{7,3},{8,12},{10,14},{12... | collective-permute-start | bytes 393224 | tf_op jit(solution)/shard_map/ppermute | solution.py:278
  119.5 4.7 %collective-permute-done.17 = f32[128,256]{1,0:T(8,128)S(1)} collective-permute-done((f32[128,256]{1,0:T(8,128)S(1)}, f32[128,256]{1,0:T(8,128)S(1)}, u32[]{:S(2)}, u32[]{:S(2)}) %collective-permute-start.17) | collective-permute-done | bytes 131104 | tf_op jit(solution)/shard_map/ppermute | solution.py:278
  124.1 4.3 %collective-permute-done.18 = f32[128,256]{1,0:T(8,128)S(1)} collective-permute-done((f32[128,256]{1,0:T(8,128)S(1)}, f32[128,256]{1,0:T(8,128)S(1)}, u32[]{:S(2)}, u32[]{:S(2)}) %collective-permute-start.18) | collective-permute-done | bytes 131104 | tf_op jit(solution)/shard_map/ppermute | solution.py:278
  128.5 2.9 %collective-permute-start.20 = (f32[64,8,256]{2,1,0:T(8,128)S(1)}, f32[64,8,256]{2,1,0:T(8,128)S(1)}, u32[]{:S(2)}, u32[]{:S(2)}) collective-permute-start(f32[64,8,256]{2,1,0:T(8,128)S(1)} %all-to-all-done.2.mine), channel_id=1, source_target_pairs={{0,1},{1,0},{2,3},{3,2},{4,5},{5,4},{6,7},{7,6},{8,9},{9,8},{10,11... | collective-permute-start | bytes 1572872 | tf_op jit(solution)/shard_map/ppermute | solution.py:278
  132.9 6.0 %finish.1 = (f32[256,256]{1,0:T(8,128)}, f32[256,256]{1,0:T(8,128)}, f32[256,256]{1,0:T(8,128)}) custom-call(s32[4]{0:T(128)} %copy-done, f32[64,8,256]{2,1,0:T(8,128)S(1)} %all-to-all-done.2.mine, f32[64,8,256]{2,1,0:T(8,128)S(1)} %collective-permute-done.20.other, f32[256,256]{1,0:T(8,128)} %get-tuple-element.91.x_new, ...), custom_call_target="tpu_custom_call" | custom-call | flops 4026531840 | bytes 5505024 | tf_op jit(solution)/shard_map/finish/pallas_call | solution.py:263
  139.0 3.1 %neg.7 = f32[256,2048]{1,0:T(8,128)} negate(f32[256,2048]{1,0:T(8,128)} %all-gather.5.cloned.1.call-done) | non-fusion elementwise | flops 524288 | bytes 4194304 | tf_op jit(solution)/shard_map/neg | solution.py:342
  (61 shorter events, 10.7 us)
Async XLA Ops:
  7.2 19.4 %copy-start.5 = (f32[16,2048]{1,0:T(8,128)S(1)}, f32[16,2048]{1,0:T(8,128)}, u32[]{:S(2)}) copy-start(f32[16,2048]{1,0:T(8,128)} %param.17) | copy-start | bytes 393220
  7.2 33.5 %all-gather.3.cloned.1.call-start = ((), (), s32[]{:S(2)}) async-start(), calls=%async_computation.3 | async-start | bytes 2359296 | tf_op jit(solution)/shard_map/all_gather | solution.py:324
  9.0 17.8 %copy-start.6 = (f32[16,2048]{1,0:T(8,128)S(1)}, f32[16,2048]{1,0:T(8,128)}, u32[]{:S(2)}) copy-start(f32[16,2048]{1,0:T(8,128)} %param.21) | copy-start | bytes 393220
  9.0 9.8 %collective-permute-start = (f32[16,2048]{1,0:T(8,128)}, f32[16,2048]{1,0:T(8,128)S(1)}, u32[]{:S(2)}, u32[]{:S(2)}) collective-permute-start(f32[16,2048]{1,0:T(8,128)} %param.17), channel_id=1, source_target_pairs={{0,32},{32,0},{64,96},{96,64},{1,33},{33,1},{65,97},{97,65},{2,34}... | collective-permute-start | bytes 393224 | tf_op jit(solution)/shard_map/ppermute | solution.py:278
  11.5 10.9 %collective-permute-start.1 = (f32[16,2048]{1,0:T(8,128)}, f32[16,2048]{1,0:T(8,128)S(1)}, u32[]{:S(2)}, u32[]{:S(2)}) collective-permute-start(f32[16,2048]{1,0:T(8,128)} %param.17), channel_id=1, source_target_pairs={{0,64},{32,96},{64,0},{96,32},{1,65},{33,97},{65,1},{97,33},{2,66}... | collective-permute-start | bytes 393224 | tf_op jit(solution)/shard_map/ppermute | solution.py:278
  14.8 8.4 %collective-permute-start.2 = (f32[16,2048]{1,0:T(8,128)}, f32[16,2048]{1,0:T(8,128)S(1)}, u32[]{:S(2)}, u32[]{:S(2)}) collective-permute-start(f32[16,2048]{1,0:T(8,128)} %param.17), channel_id=1, source_target_pairs={{0,96},{32,64},{64,32},{96,0},{1,97},{33,65},{65,33},{97,1},{2,98}... | collective-permute-start | bytes 393224 | tf_op jit(solution)/shard_map/ppermute | solution.py:278
  14.8 8.4 %collective-permute-start.3 = (f32[16,2048]{1,0:T(8,128)}, f32[16,2048]{1,0:T(8,128)S(1)}, u32[]{:S(2)}, u32[]{:S(2)}) collective-permute-start(f32[16,2048]{1,0:T(8,128)} %param.21), channel_id=1, source_target_pairs={{0,8},{8,0},{16,24},{24,16},{1,9},{9,1},{17,25},{25,17},{2,10},{10... | collective-permute-start | bytes 393224 | tf_op jit(solution)/shard_map/ppermute | solution.py:278
  16.1 7.6 %collective-permute-start.4 = (f32[16,2048]{1,0:T(8,128)}, f32[16,2048]{1,0:T(8,128)S(1)}, u32[]{:S(2)}, u32[]{:S(2)}) collective-permute-start(f32[16,2048]{1,0:T(8,128)} %param.21), channel_id=1, source_target_pairs={{0,16},{8,24},{16,0},{24,8},{1,17},{9,25},{17,1},{25,9},{2,18},{10... | collective-permute-start | bytes 393224 | tf_op jit(solution)/shard_map/ppermute | solution.py:278
  18.8 7.8 %collective-permute-start.5 = (f32[16,2048]{1,0:T(8,128)}, f32[16,2048]{1,0:T(8,128)S(1)}, u32[]{:S(2)}, u32[]{:S(2)}) collective-permute-start(f32[16,2048]{1,0:T(8,128)} %param.21), channel_id=1, source_target_pairs={{0,24},{8,16},{16,8},{24,0},{1,25},{9,17},{17,9},{25,1},{2,26},{10... | collective-permute-start | bytes 393224 | tf_op jit(solution)/shard_map/ppermute | solution.py:278
  26.9 13.5 %collective-permute-start.10 = (f32[64,2048]{1,0:T(8,128)S(1)}, f32[64,2048]{1,0:T(8,128)S(1)}, u32[]{:S(2)}, u32[]{:S(2)}) collective-permute-start(f32[64,2048]{1,0:T(8,128)S(1)} %get-tuple-element.79.rest_4_), channel_id=1, source_target_pairs={{0,64},{32,96},{64,0},{96,32},{1,65},{33,97},{65,1},{97,33},{2,66}... | collective-permute-start | bytes 1572872 | tf_op jit(solution)/shard_map/ppermute | solution.py:278
  28.0 27.1 %collective-permute-start.11 = (f32[64,2048]{1,0:T(8,128)S(1)}, f32[64,2048]{1,0:T(8,128)S(1)}, u32[]{:S(2)}, u32[]{:S(2)}) collective-permute-start(f32[64,2048]{1,0:T(8,128)S(1)} %get-tuple-element.79.rest_4_), channel_id=1, source_target_pairs={{0,96},{32,64},{64,32},{96,0},{1,97},{33,65},{65,33},{97,1},{2,98}... | collective-permute-start | bytes 1572872 | tf_op jit(solution)/shard_map/ppermute | solution.py:278
  29.4 25.7 %collective-permute-start.6 = (f32[64,2048]{1,0:T(8,128)S(1)}, f32[64,2048]{1,0:T(8,128)S(1)}, u32[]{:S(2)}, u32[]{:S(2)}) collective-permute-start(f32[64,2048]{1,0:T(8,128)S(1)} %get-tuple-element.75.rest_0_), channel_id=1, source_target_pairs={{0,8},{8,0},{16,24},{24,16},{1,9},{9,1},{17,25},{25,17},{2,10},{10... | collective-permute-start | bytes 1572872 | tf_op jit(solution)/shard_map/ppermute | solution.py:278
  29.4 26.5 %collective-permute-start.7 = (f32[64,2048]{1,0:T(8,128)S(1)}, f32[64,2048]{1,0:T(8,128)S(1)}, u32[]{:S(2)}, u32[]{:S(2)}) collective-permute-start(f32[64,2048]{1,0:T(8,128)S(1)} %get-tuple-element.75.rest_0_), channel_id=1, source_target_pairs={{0,16},{8,24},{16,0},{24,8},{1,17},{9,25},{17,1},{25,9},{2,18},{10... | collective-permute-start | bytes 1572872 | tf_op jit(solution)/shard_map/ppermute | solution.py:278
  31.6 25.1 %collective-permute-start.8 = (f32[64,2048]{1,0:T(8,128)S(1)}, f32[64,2048]{1,0:T(8,128)}, u32[]{:S(2)}, u32[]{:S(2)}) collective-permute-start(f32[64,2048]{1,0:T(8,128)S(1)} %get-tuple-element.75.rest_0_), channel_id=1, source_target_pairs={{0,24},{8,16},{16,8},{24,0},{1,25},{9,17},{17,9},{25,1},{2,26},{10... | collective-permute-start | bytes 1572872 | tf_op jit(solution)/shard_map/ppermute | solution.py:278
  40.4 16.3 %collective-permute-start.9 = (f32[64,2048]{1,0:T(8,128)S(1)}, f32[64,2048]{1,0:T(8,128)}, u32[]{:S(2)}, u32[]{:S(2)}) collective-permute-start(f32[64,2048]{1,0:T(8,128)S(1)} %get-tuple-element.79.rest_4_), channel_id=1, source_target_pairs={{0,32},{32,0},{64,96},{96,64},{1,33},{33,1},{65,97},{97,65},{2,34}... | collective-permute-start | bytes 1572872 | tf_op jit(solution)/shard_map/ppermute | solution.py:278
  49.3 42.0 %all-to-all-start = ((f32[16,16,2048]{2,1,0:T(8,128)}), f32[16,16,2048]{2,1,0:T(8,128)}, u32[]{:S(2)}, u32[]{:S(2)}) async-start(f32[16,16,2048]{2,1,0:T(8,128)} %band_products.1), calls=%async_computation | async-start | bytes 4194304 | tf_op jit(solution)/shard_map/all_to_all | solution.py:333
  54.9 84.0 %all-gather.5.cloned.1.call-start = ((), (), s32[]{:S(2)}) async-start(), calls=%async_computation.4 | async-start | bytes 2228224 | tf_op jit(solution)/shard_map/all_gather | solution.py:342
  55.1 19.2 %copy-start = (s32[4]{0:T(128)}, s32[4]{0:T(128)S(1)}, u32[]{:S(2)}) copy-start(s32[4]{0:T(128)S(1)} %pad_add_fusion.place) | copy-start | bytes 52
  55.1 0.8 copy-start.1
  55.9 0.8 copy-start.3
  56.7 1.0 copy-start.2
  57.8 1.0 copy-start.4
  74.3 4.5 %collective-permute-start.12 = (f32[4,16,8,256]{3,2,1,0:T(8,128)S(1)}, f32[4,16,8,256]{3,2,1,0:T(8,128)S(1)}, u32[]{:S(2)}, u32[]{:S(2)}) collective-permute-start(f32[4,16,8,256]{3,2,1,0:T(8,128)S(1)} %get-tuple-element.84), channel_id=1, source_target_pairs={{0,1},{1,0},{2,3},{3,2},{4,5},{5,4},{6,7},{7,6},{8,9},{9,8},{10,11... | collective-permute-start | bytes 1572872 | tf_op jit(solution)/shard_map/ppermute | solution.py:278
  78.9 4.9 %collective-permute-start.13 = (f32[16,8,256]{2,1,0:T(8,128)S(1)}, f32[16,8,256]{2,1,0:T(8,128)S(1)}, u32[]{:S(2)}, u32[]{:S(2)}) collective-permute-start(f32[16,8,256]{2,1,0:T(8,128)S(1)} %get-tuple-element.108), channel_id=1, source_target_pairs={{0,2},{2,0},{4,6},{6,4},{1,3},{3,1},{5,7},{7,5},{8,10},{10,8},{12,... | collective-permute-start | bytes 393224 | tf_op jit(solution)/shard_map/ppermute | solution.py:278
  80.2 8.5 %collective-permute-start.14 = (f32[16,8,256]{2,1,0:T(8,128)S(1)}, f32[16,8,256]{2,1,0:T(8,128)S(1)}, u32[]{:S(2)}, u32[]{:S(2)}) collective-permute-start(f32[16,8,256]{2,1,0:T(8,128)S(1)} %get-tuple-element.106), channel_id=1, source_target_pairs={{0,4},{2,6},{4,0},{6,2},{1,5},{3,7},{5,1},{7,3},{8,12},{10,14},{12... | collective-permute-start | bytes 393224 | tf_op jit(solution)/shard_map/ppermute | solution.py:278
  82.7 8.6 %collective-permute-start.15 = (f32[16,8,256]{2,1,0:T(8,128)S(1)}, f32[16,8,256]{2,1,0:T(8,128)S(1)}, u32[]{:S(2)}, u32[]{:S(2)}) collective-permute-start(f32[16,8,256]{2,1,0:T(8,128)S(1)} %get-tuple-element.107), channel_id=1, source_target_pairs={{0,6},{2,4},{4,2},{6,0},{1,7},{3,5},{5,3},{7,1},{8,14},{10,12},{12... | collective-permute-start | bytes 393224 | tf_op jit(solution)/shard_map/ppermute | solution.py:278
  93.7 16.2 %collective-permute-start.16 = (f32[512,256]{1,0:T(8,128)S(1)}, f32[512,256]{1,0:T(8,128)S(1)}, u32[]{:S(2)}, u32[]{:S(2)}) collective-permute-start(f32[512,256]{1,0:T(8,128)S(1)} %get-tuple-element.86), channel_id=1, source_target_pairs={{0,1},{1,0},{2,3},{3,2},{4,5},{5,4},{6,7},{7,6},{8,9},{9,8},{10,11... | collective-permute-start | bytes 1572872 | tf_op jit(solution)/shard_map/ppermute | solution.py:278
  110.8 17.7 %all-to-all-start.2 = ((f32[64,8,256]{2,1,0:T(8,128)}), f32[64,8,256]{2,1,0:T(8,128)S(1)}, u32[]{:S(2)}, u32[]{:S(2)}) async-start(f32[64,8,256]{2,1,0:T(8,128)} %broadcast_in_dim.2), calls=%async_computation.2 | async-start | bytes 1048576 | tf_op jit(solution)/shard_map/all_to_all | solution.py:282
  115.5 8.6 %collective-permute-start.17 = (f32[128,256]{1,0:T(8,128)S(1)}, f32[128,256]{1,0:T(8,128)S(1)}, u32[]{:S(2)}, u32[]{:S(2)}) collective-permute-start(f32[128,256]{1,0:T(8,128)S(1)} %get-tuple-element.105), channel_id=1, source_target_pairs={{0,2},{2,0},{4,6},{6,4},{1,3},{3,1},{5,7},{7,5},{8,10},{10,8},{12,... | collective-permute-start | bytes 393224 | tf_op jit(solution)/shard_map/ppermute | solution.py:278
  116.5 12.0 %collective-permute-start.18 = (f32[128,256]{1,0:T(8,128)S(1)}, f32[128,256]{1,0:T(8,128)S(1)}, u32[]{:S(2)}, u32[]{:S(2)}) collective-permute-start(f32[128,256]{1,0:T(8,128)S(1)} %get-tuple-element.104), channel_id=1, source_target_pairs={{0,4},{2,6},{4,0},{6,2},{1,5},{3,7},{5,1},{7,3},{8,12},{10,14},{12... | collective-permute-start | bytes 393224 | tf_op jit(solution)/shard_map/ppermute | solution.py:278
  118.9 9.5 %collective-permute-start.19 = (f32[128,256]{1,0:T(8,128)S(1)}, f32[128,256]{1,0:T(8,128)S(1)}, u32[]{:S(2)}, u32[]{:S(2)}) collective-permute-start(f32[128,256]{1,0:T(8,128)S(1)} %get-tuple-element.103), channel_id=1, source_target_pairs={{0,6},{2,4},{4,2},{6,0},{1,7},{3,5},{5,3},{7,1},{8,14},{10,12},{12... | collective-permute-start | bytes 393224 | tf_op jit(solution)/shard_map/ppermute | solution.py:278
  128.5 4.4 %collective-permute-start.20 = (f32[64,8,256]{2,1,0:T(8,128)S(1)}, f32[64,8,256]{2,1,0:T(8,128)S(1)}, u32[]{:S(2)}, u32[]{:S(2)}) collective-permute-start(f32[64,8,256]{2,1,0:T(8,128)S(1)} %all-to-all-done.2.mine), channel_id=1, source_target_pairs={{0,1},{1,0},{2,3},{3,2},{4,5},{5,4},{6,7},{7,6},{8,9},{9,8},{10,11... | collective-permute-start | bytes 1572872 | tf_op jit(solution)/shard_map/ppermute | solution.py:278
Sparse Core Ops, SparseCore 0:
  10.3 28.7 all-gather.2
  93.8 45.0 all-gather.4

commit v7 on v4

--- a/solution.py
+++ b/solution.py
@@ -94,7 +94,7 @@
         out[k] = band[k * size : (k + 1) * size, :]
 
 
-def band_products(triple, lio, lower, trail, ranks, count, tile=512):
+def band_products(triple, lio, lower, trail, ranks, count, tile=1024):
     rows, columns = trail.shape
     width = lio.shape[0]
     once = pl.Buffered(1)

time: 148 us -> 151 us (1.020)
  blocking collectives: 28.7 us -> 31.1 us
    all_to_all x2, blocking collectives: 28.7 us -> 31.1 us  [exchange(): return lax.all_to_all(value, axes, 0, 0, tiled=True)]
  transfers between devices with their start and end apart: 21 -> 21, of which waited for: 11 -> 11; matrix products, arithmetic and copies ran while one was open for 2% -> 2% of each run, Pallas kernels for 23% -> 22%
where the time goes in v7:
time: 151 us; the launch traced here: 150 us
  starting transfers between devices  36.5 us (24%)
  Pallas kernels  32.9 us (22%)
  blocking collectives  31.1 us (21%)
  waiting for transfers between devices  26.9 us (18%)
  between operations  14.2 us (9%)
  other arithmetic  8.15 us (5%)
    all_to_all x2, blocking collectives, exchange(): return lax.all_to_all(value, axes, 0, 0, tiled=True)  31.1 us
    ppermute x17, starting transfers between devices, swap(): return lax.ppermute(value, axis, [(i, i ^ step) for i in range(size)])  24 us
    ppermute x17, waiting for transfers between devices, swap(): return lax.ppermute(value, axis, [(i, i ^ step) for i in range(size)])  22.9 us
    pallas_call x1, Pallas kernels, panel_products(): pl.pallas_call(functools.partial(panel_kernel, count, tile), out_shape=(j...  14.5 us
    pallas_call x1, Pallas kernels, band_products(): pl.pallas_call(functools.partial(band_kernel, count), out_shape=jax.Shape...  8.66 us
    all_to_all x1, starting transfers between devices, exchange(): return lax.all_to_all(value, axes, 0, 0, tiled=True)  6.75 us
    pallas_call x1, Pallas kernels, finish(): pl.pallas_call(finish_kernel, out_shape=(jax.ShapeDtypeStruct((width, wid...  6.08 us
    all_to_all x1, starting transfers between devices, body(): band = lax.all_to_all(band, row, 0, 0, tiled=True)  5.63 us
  transfers between devices with their start and end apart: 21, of which 11 were waited for; matrix products, arithmetic and copies ran while one was open for 2% of the time, Pallas kernels for 22%

profile of v7, /device:TPU:1, one launch (start us, length us, event | category | flops | bytes accessed | tf_op | source)
XLA Modules:
  0.0 150.1 jit_solution(8041808524547001998)
XLA Ops:
  7.2 1.7 %pad_maximum_fusion = f32[64,1024]{1,0:T(8,128)} fusion(f32[32,1024]{1,0:T(8,128)} %bitcast.17, f32[32,1024]{1,0:T(8,128)} %bitcast.18), kind=kLoop, calls=%fused_computation | loop fusion | flops 65536 | bytes 524288 | tf_op jit(solution)/shard_map/concatenate | solution.py:319
  9.0 2.5 %collective-permute-start = (f32[16,2048]{1,0:T(8,128)}, f32[16,2048]{1,0:T(8,128)S(1)}, u32[]{:S(2)}, u32[]{:S(2)}) collective-permute-start(f32[16,2048]{1,0:T(8,128)} %param.17), channel_id=1, source_target_pairs={{0,32},{32,0},{64,96},{96,64},{1,33},{33,1},{65,97},{97,65},{2,34}... | collective-permute-start | bytes 393224 | tf_op jit(solution)/shard_map/ppermute | solution.py:274
  11.5 3.3 %collective-permute-start.1 = (f32[16,2048]{1,0:T(8,128)}, f32[16,2048]{1,0:T(8,128)S(1)}, u32[]{:S(2)}, u32[]{:S(2)}) collective-permute-start(f32[16,2048]{1,0:T(8,128)} %param.17), channel_id=1, source_target_pairs={{0,64},{32,96},{64,0},{96,32},{1,65},{33,97},{65,1},{97,33},{2,66}... | collective-permute-start | bytes 393224 | tf_op jit(solution)/shard_map/ppermute | solution.py:274
  14.8 1.3 collective-permute-start.3
  16.1 2.6 %collective-permute-start.4 = (f32[16,2048]{1,0:T(8,128)}, f32[16,2048]{1,0:T(8,128)S(1)}, u32[]{:S(2)}, u32[]{:S(2)}) collective-permute-start(f32[16,2048]{1,0:T(8,128)} %param.21), channel_id=1, source_target_pairs={{0,16},{8,24},{16,0},{24,8},{1,17},{9,25},{17,1},{25,9},{2,18},{10... | collective-permute-start | bytes 393224 | tf_op jit(solution)/shard_map/ppermute | solution.py:274
  18.8 3.7 %prepare.1 = (f32[256,256]{1,0:T(8,128)}, f32[256,256]{1,0:T(8,128)}, f32[256,256]{1,0:T(8,128)}, f32[256,256]{1,0:T(8,128)}, f32[256,256]{1,0:T(8,128)}, /*inde...) custom-call(f32[256,256]{1,0:T(8,128)} %lot.3, f32[256,256]{1,0:T(8,128)} %uol.3, ...), custom_call_target="tpu_custom_call" | custom-call | flops 603979776 | bytes 3670016 | tf_op jit(solution)/shard_map/prepare/pallas_call | solution.py:55
  22.4 0.8 collective-permute-done.2
  23.8 2.8 %collective-permute-done.5 = f32[16,2048]{1,0:T(8,128)S(1)} collective-permute-done((f32[16,2048]{1,0:T(8,128)}, f32[16,2048]{1,0:T(8,128)S(1)}, u32[]{:S(2)}, u32[]{:S(2)}) %collective-permute-start.5) | collective-permute-done | bytes 131104 | tf_op jit(solution)/shard_map/ppermute | solution.py:274
  26.9 1.1 collective-permute-start.10
  28.0 1.5 collective-permute-start.11
  29.4 2.2 %collective-permute-start.7 = (f32[64,2048]{1,0:T(8,128)S(1)}, f32[64,2048]{1,0:T(8,128)S(1)}, u32[]{:S(2)}, u32[]{:S(2)}) collective-permute-start(f32[64,2048]{1,0:T(8,128)S(1)} %get-tuple-element.73.rest_0_), channel_id=1, source_target_pairs={{0,16},{8,24},{16,0},{24,8},{1,17},{9,25},{17,1},{25,9},{2,18},{10... | collective-permute-start | bytes 1572872 | tf_op jit(solution)/shard_map/ppermute | solution.py:274
  31.6 1.7 %collective-permute-start.8 = (f32[64,2048]{1,0:T(8,128)S(1)}, f32[64,2048]{1,0:T(8,128)}, u32[]{:S(2)}, u32[]{:S(2)}) collective-permute-start(f32[64,2048]{1,0:T(8,128)S(1)} %get-tuple-element.73.rest_0_), channel_id=1, source_target_pairs={{0,24},{8,16},{16,8},{24,0},{1,25},{9,17},{17,9},{25,1},{2,26},{10... | collective-permute-start | bytes 1572872 | tf_op jit(solution)/shard_map/ppermute | solution.py:274
  33.3 7.1 %collective-permute-done.10.rest_6_ = f32[64,2048]{1,0:T(8,128)S(1)} collective-permute-done((f32[64,2048]{1,0:T(8,128)S(1)}, f32[64,2048]{1,0:T(8,128)S(1)}, u32[]{:S(2)}, u32[]{:S(2)}) %collective-permute-start.10) | collective-permute-done | bytes 524320 | tf_op jit(solution)/shard_map/ppermute | solution.py:274
  40.6 8.7 %band_products.1 = f32[16,16,2048]{2,1,0:T(8,128)} custom-call(f32[256,256]{1,0:T(8,128)} %get-tuple-element.72.triple.lower_triple, f32[256,256]{1,0:T(8,128)} %lio.5, f32[512,1024]{1,0:T(8,128)} %all-gather.3.cloned.1.call-done.lower, f32[1024,2048]{1,0:T(8,128)} %trail.3), custom_call_target="tpu_custom_call" | custom-call | flops 3221225472 | bytes 12582912 | tf_op jit(solution)/shard_map/band_products/pallas_call | solution.py:102
  49.3 5.6 %all-to-all-start = ((f32[16,16,2048]{2,1,0:T(8,128)}), f32[16,16,2048]{2,1,0:T(8,128)}, u32[]{:S(2)}, u32[]{:S(2)}) async-start(f32[16,16,2048]{2,1,0:T(8,128)} %band_products.1), calls=%async_computation | async-start | bytes 4194304 | tf_op jit(solution)/shard_map/all_to_all | solution.py:329
  55.1 14.5 %panel_products.1 = (f32[4,16,8,256]{3,2,1,0:T(8,128)S(1)}, f32[4,16,8,256]{3,2,1,0:T(8,128)S(1)}, f32[1024,256]{1,0:T(8,128)}) custom-call(s32[4]{0:T(128)S(1)} %pad_add_fusion.place, bf16[512,256]{1,0:T(8,128)(2,1)} %get-tuple-element.60.side_high, bf16[512,256]{1,0:T(8,128)(2,1)} %get-tuple-element.61.side_low, ...), custom_call_target="tpu_custom_call" | custom-call | flops 8858370048 | bytes 16777216 | tf_op jit(solution)/shard_map/panel_products/pallas_call | solution.py:180
  69.7 3.5 %collective-permute-start.12 = (f32[4,16,8,256]{3,2,1,0:T(8,128)S(1)}, f32[4,16,8,256]{3,2,1,0:T(8,128)S(1)}, u32[]{:S(2)}, u32[]{:S(2)}) collective-permute-start(f32[4,16,8,256]{3,2,1,0:T(8,128)S(1)} %get-tuple-element.82), channel_id=1, source_target_pairs={{0,1},{1,0},{2,3},{3,2},{4,5},{5,4},{6,7},{7,6},{8,9},{9,8},{10,11... | collective-permute-start | bytes 1572872 | tf_op jit(solution)/shard_map/ppermute | solution.py:274
  73.1 1.5 %collective-permute-done.12 = f32[4,16,8,256]{3,2,1,0:T(8,128)S(1)} collective-permute-done((f32[4,16,8,256]{3,2,1,0:T(8,128)S(1)}, f32[4,16,8,256]{3,2,1,0:T(8,128)S(1)}, u32[]{:S(2)}, u32[]{:S(2)}) %collective-permute-start.12) | collective-permute-done | bytes 524320 | tf_op jit(solution)/shard_map/ppermute | solution.py:274
  74.8 1.3 collective-permute-start.13
  76.1 2.4 %collective-permute-start.14 = (f32[16,8,256]{2,1,0:T(8,128)S(1)}, f32[16,8,256]{2,1,0:T(8,128)S(1)}, u32[]{:S(2)}, u32[]{:S(2)}) collective-permute-start(f32[16,8,256]{2,1,0:T(8,128)S(1)} %get-tuple-element.99), channel_id=1, source_target_pairs={{0,4},{2,6},{4,0},{6,2},{1,5},{3,7},{5,1},{7,3},{8,12},{10,14},{12... | collective-permute-start | bytes 393224 | tf_op jit(solution)/shard_map/ppermute | solution.py:274
  78.7 1.0 collective-permute-done.13
  79.7 5.1 %collective-permute-done.14 = f32[16,8,256]{2,1,0:T(8,128)S(1)} collective-permute-done((f32[16,8,256]{2,1,0:T(8,128)S(1)}, f32[16,8,256]{2,1,0:T(8,128)S(1)}, u32[]{:S(2)}, u32[]{:S(2)}) %collective-permute-start.14) | collective-permute-done | bytes 131104 | tf_op jit(solution)/shard_map/ppermute | solution.py:274
  84.7 2.4 %collective-permute-done.15 = f32[16,8,256]{2,1,0:T(8,128)S(1)} collective-permute-done((f32[16,8,256]{2,1,0:T(8,128)S(1)}, f32[16,8,256]{2,1,0:T(8,128)S(1)}, u32[]{:S(2)}, u32[]{:S(2)}) %collective-permute-start.15) | collective-permute-done | bytes 131104 | tf_op jit(solution)/shard_map/ppermute | solution.py:274
  87.1 1.7 %reduce_sum.27 = f32[16,2048]{1,0:T(8,128)S(1)} reduce(f32[16,16,2048]{2,1,0:T(8,128)} %all-to-all-done, f32[]{:T(128)} %constant.7.clone.1), dimensions={0}, to_apply=%region_0.0 | reduce | flops 491520 | bytes 2228228 | tf_op jit(solution)/shard_map/reduce_sum | solution.py:337
  89.5 15.9 %all_to_all.21 = f32[16,8,256]{2,1,0:T(8,128)S(1)} all-to-all(f32[16,8,256]{2,1,0:T(8,128)S(1)} %fusion), channel_id=1, replica_groups=mesh['z'=4,'y'=4,'x'=4,'c'=2] {'z','y'}, dimensions={0} | all-to-all | bytes 262144 | tf_op jit(solution)/shard_map/all_to_all | solution.py:278
  105.5 15.1 %all_to_all.20.mine = f32[64,8,256]{2,1,0:T(8,128)S(1)} all-to-all(f32[64,8,256]{2,1,0:T(8,128)S(1)} %broadcast_in_dim.2), channel_id=1, replica_groups=mesh['z'=4,'y'=4,'x'=4,'c'=2] {'z','y','x'}, dimensions={0} | all-to-all | bytes 1048576 | tf_op jit(solution)/shard_map/all_to_all | solution.py:278
  120.7 6.7 %all-to-all-start.3 = ((f32[8,128,256]{2,1,0:T(8,128)}), f32[8,128,256]{2,1,0:T(8,128)S(1)}, u32[]{:S(2)}, u32[]{:S(2)}) async-start(f32[8,128,256]{2,1,0:T(8,128)} %bitcast.10), calls=%async_computation.3 | async-start | bytes 2097152 | tf_op jit(solution)/shard_map/all_to_all | solution.py:278
  127.6 1.7 %collective-permute-done.16.other = f32[64,8,256]{2,1,0:T(8,128)S(1)} collective-permute-done((f32[64,8,256]{2,1,0:T(8,128)S(1)}, f32[64,8,256]{2,1,0:T(8,128)S(1)}, u32[]{:S(2)}, u32[]{:S(2)}) %collective-permute-start.16) | collective-permute-done | bytes 524320 | tf_op jit(solution)/shard_map/ppermute | solution.py:274
  129.3 6.1 %finish.1 = (f32[256,256]{1,0:T(8,128)}, f32[256,256]{1,0:T(8,128)}, f32[256,256]{1,0:T(8,128)}) custom-call(s32[4]{0:T(128)} %copy-done, f32[64,8,256]{2,1,0:T(8,128)S(1)} %all_to_all.20.mine, f32[64,8,256]{2,1,0:T(8,128)S(1)} %collective-permute-done.16.other, f32[256,256]{1,0:T(8,128)} %get-tuple-element.87.x_new, f32[256,256]{1,0:T(8,128)} %get-tuple-element.88.y_new, ...), custom_call_target="tpu_custom_call" | custom-call | flops 4026531840 | bytes 5505024 | tf_op jit(solution)/shard_map/finish/pallas_call | solution.py:259
  135.4 2.2 %all-gather.5.cloned.1.call-done = f32[256,2048]{1,0:T(8,128)} async-done(((f32[16,2048]{1,0:T(8,128)}), f32[256,2048]{1,0:T(8,128)}) %all-gather.5.cloned.1.call-update) | async-done | bytes 2097168 | tf_op jit(solution)/shard_map/all_gather | solution.py:338
  137.6 3.1 %neg.7 = f32[256,2048]{1,0:T(8,128)} negate(f32[256,2048]{1,0:T(8,128)} %all-gather.5.cloned.1.call-done) | non-fusion elementwise | flops 524288 | bytes 4194304 | tf_op jit(solution)/shard_map/neg | solution.py:338
  140.7 1.8 %all-to-all-done.3 = f32[8,128,256]{2,1,0:T(8,128)S(1)} async-done(((f32[8,128,256]{2,1,0:T(8,128)}), f32[8,128,256]{2,1,0:T(8,128)S(1)}, u32[]{:S(2)}, u32[]{:S(2)}) %all-to-all-start.3) | async-done | bytes 1048608 | tf_op jit(solution)/shard_map/all_to_all | solution.py:278
  (44 shorter events, 3.1 us)
Async XLA Ops:
  7.2 19.4 %copy-start.1 = (f32[16,2048]{1,0:T(8,128)S(1)}, f32[16,2048]{1,0:T(8,128)}, u32[]{:S(2)}) copy-start(f32[16,2048]{1,0:T(8,128)} %param.17) | copy-start | bytes 393220
  7.2 33.5 %all-gather.3.cloned.1.call-start = ((), (), s32[]{:S(2)}) async-start(), calls=%async_computation.4 | async-start | bytes 2359296 | tf_op jit(solution)/shard_map/all_gather | solution.py:320
  9.0 17.8 %copy-start.2 = (f32[16,2048]{1,0:T(8,128)S(1)}, f32[16,2048]{1,0:T(8,128)}, u32[]{:S(2)}) copy-start(f32[16,2048]{1,0:T(8,128)} %param.21) | copy-start | bytes 393220
  9.0 9.8 %collective-permute-start = (f32[16,2048]{1,0:T(8,128)}, f32[16,2048]{1,0:T(8,128)S(1)}, u32[]{:S(2)}, u32[]{:S(2)}) collective-permute-start(f32[16,2048]{1,0:T(8,128)} %param.17), channel_id=1, source_target_pairs={{0,32},{32,0},{64,96},{96,64},{1,33},{33,1},{65,97},{97,65},{2,34}... | collective-permute-start | bytes 393224 | tf_op jit(solution)/shard_map/ppermute | solution.py:274
  11.5 10.9 %collective-permute-start.1 = (f32[16,2048]{1,0:T(8,128)}, f32[16,2048]{1,0:T(8,128)S(1)}, u32[]{:S(2)}, u32[]{:S(2)}) collective-permute-start(f32[16,2048]{1,0:T(8,128)} %param.17), channel_id=1, source_target_pairs={{0,64},{32,96},{64,0},{96,32},{1,65},{33,97},{65,1},{97,33},{2,66}... | collective-permute-start | bytes 393224 | tf_op jit(solution)/shard_map/ppermute | solution.py:274
  14.8 8.4 %collective-permute-start.2 = (f32[16,2048]{1,0:T(8,128)}, f32[16,2048]{1,0:T(8,128)S(1)}, u32[]{:S(2)}, u32[]{:S(2)}) collective-permute-start(f32[16,2048]{1,0:T(8,128)} %param.17), channel_id=1, source_target_pairs={{0,96},{32,64},{64,32},{96,0},{1,97},{33,65},{65,33},{97,1},{2,98}... | collective-permute-start | bytes 393224 | tf_op jit(solution)/shard_map/ppermute | solution.py:274
  14.8 8.4 %collective-permute-start.3 = (f32[16,2048]{1,0:T(8,128)}, f32[16,2048]{1,0:T(8,128)S(1)}, u32[]{:S(2)}, u32[]{:S(2)}) collective-permute-start(f32[16,2048]{1,0:T(8,128)} %param.21), channel_id=1, source_target_pairs={{0,8},{8,0},{16,24},{24,16},{1,9},{9,1},{17,25},{25,17},{2,10},{10... | collective-permute-start | bytes 393224 | tf_op jit(solution)/shard_map/ppermute | solution.py:274
  16.1 7.6 %collective-permute-start.4 = (f32[16,2048]{1,0:T(8,128)}, f32[16,2048]{1,0:T(8,128)S(1)}, u32[]{:S(2)}, u32[]{:S(2)}) collective-permute-start(f32[16,2048]{1,0:T(8,128)} %param.21), channel_id=1, source_target_pairs={{0,16},{8,24},{16,0},{24,8},{1,17},{9,25},{17,1},{25,9},{2,18},{10... | collective-permute-start | bytes 393224 | tf_op jit(solution)/shard_map/ppermute | solution.py:274
  18.8 7.8 %collective-permute-start.5 = (f32[16,2048]{1,0:T(8,128)}, f32[16,2048]{1,0:T(8,128)S(1)}, u32[]{:S(2)}, u32[]{:S(2)}) collective-permute-start(f32[16,2048]{1,0:T(8,128)} %param.21), channel_id=1, source_target_pairs={{0,24},{8,16},{16,8},{24,0},{1,25},{9,17},{17,9},{25,1},{2,26},{10... | collective-permute-start | bytes 393224 | tf_op jit(solution)/shard_map/ppermute | solution.py:274
  26.9 13.5 %collective-permute-start.10 = (f32[64,2048]{1,0:T(8,128)S(1)}, f32[64,2048]{1,0:T(8,128)S(1)}, u32[]{:S(2)}, u32[]{:S(2)}) collective-permute-start(f32[64,2048]{1,0:T(8,128)S(1)} %get-tuple-element.77.rest_4_), channel_id=1, source_target_pairs={{0,64},{32,96},{64,0},{96,32},{1,65},{33,97},{65,1},{97,33},{2,66}... | collective-permute-start | bytes 1572872 | tf_op jit(solution)/shard_map/ppermute | solution.py:274
  28.0 27.1 %collective-permute-start.11 = (f32[64,2048]{1,0:T(8,128)S(1)}, f32[64,2048]{1,0:T(8,128)S(1)}, u32[]{:S(2)}, u32[]{:S(2)}) collective-permute-start(f32[64,2048]{1,0:T(8,128)S(1)} %get-tuple-element.77.rest_4_), channel_id=1, source_target_pairs={{0,96},{32,64},{64,32},{96,0},{1,97},{33,65},{65,33},{97,1},{2,98}... | collective-permute-start | bytes 1572872 | tf_op jit(solution)/shard_map/ppermute | solution.py:274
  29.4 25.7 %collective-permute-start.6 = (f32[64,2048]{1,0:T(8,128)S(1)}, f32[64,2048]{1,0:T(8,128)S(1)}, u32[]{:S(2)}, u32[]{:S(2)}) collective-permute-start(f32[64,2048]{1,0:T(8,128)S(1)} %get-tuple-element.73.rest_0_), channel_id=1, source_target_pairs={{0,8},{8,0},{16,24},{24,16},{1,9},{9,1},{17,25},{25,17},{2,10},{10... | collective-permute-start | bytes 1572872 | tf_op jit(solution)/shard_map/ppermute | solution.py:274
  29.4 25.7 %collective-permute-start.7 = (f32[64,2048]{1,0:T(8,128)S(1)}, f32[64,2048]{1,0:T(8,128)S(1)}, u32[]{:S(2)}, u32[]{:S(2)}) collective-permute-start(f32[64,2048]{1,0:T(8,128)S(1)} %get-tuple-element.73.rest_0_), channel_id=1, source_target_pairs={{0,16},{8,24},{16,0},{24,8},{1,17},{9,25},{17,1},{25,9},{2,18},{10... | collective-permute-start | bytes 1572872 | tf_op jit(solution)/shard_map/ppermute | solution.py:274
  31.6 23.5 %collective-permute-start.8 = (f32[64,2048]{1,0:T(8,128)S(1)}, f32[64,2048]{1,0:T(8,128)}, u32[]{:S(2)}, u32[]{:S(2)}) collective-permute-start(f32[64,2048]{1,0:T(8,128)S(1)} %get-tuple-element.73.rest_0_), channel_id=1, source_target_pairs={{0,24},{8,16},{16,8},{24,0},{1,25},{9,17},{17,9},{25,1},{2,26},{10... | collective-permute-start | bytes 1572872 | tf_op jit(solution)/shard_map/ppermute | solution.py:274
  40.4 14.7 %collective-permute-start.9 = (f32[64,2048]{1,0:T(8,128)S(1)}, f32[64,2048]{1,0:T(8,128)}, u32[]{:S(2)}, u32[]{:S(2)}) collective-permute-start(f32[64,2048]{1,0:T(8,128)S(1)} %get-tuple-element.77.rest_4_), channel_id=1, source_target_pairs={{0,32},{32,0},{64,96},{96,64},{1,33},{33,1},{65,97},{97,65},{2,34}... | collective-permute-start | bytes 1572872 | tf_op jit(solution)/shard_map/ppermute | solution.py:274
  49.3 37.8 %all-to-all-start = ((f32[16,16,2048]{2,1,0:T(8,128)}), f32[16,16,2048]{2,1,0:T(8,128)}, u32[]{:S(2)}, u32[]{:S(2)}) async-start(f32[16,16,2048]{2,1,0:T(8,128)} %band_products.1), calls=%async_computation | async-start | bytes 4194304 | tf_op jit(solution)/shard_map/all_to_all | solution.py:329
  54.9 82.6 %all-gather.5.cloned.1.call-start = ((), (), s32[]{:S(2)}) async-start(), calls=%async_computation.5 | async-start | bytes 2228224 | tf_op jit(solution)/shard_map/all_gather | solution.py:338
  55.1 14.6 %copy-start = (s32[4]{0:T(128)}, s32[4]{0:T(128)S(1)}, u32[]{:S(2)}) copy-start(s32[4]{0:T(128)S(1)} %pad_add_fusion.place) | copy-start | bytes 52
  69.7 5.0 %collective-permute-start.12 = (f32[4,16,8,256]{3,2,1,0:T(8,128)S(1)}, f32[4,16,8,256]{3,2,1,0:T(8,128)S(1)}, u32[]{:S(2)}, u32[]{:S(2)}) collective-permute-start(f32[4,16,8,256]{3,2,1,0:T(8,128)S(1)} %get-tuple-element.82), channel_id=1, source_target_pairs={{0,1},{1,0},{2,3},{3,2},{4,5},{5,4},{6,7},{7,6},{8,9},{9,8},{10,11... | collective-permute-start | bytes 1572872 | tf_op jit(solution)/shard_map/ppermute | solution.py:274
  74.8 4.9 %collective-permute-start.13 = (f32[16,8,256]{2,1,0:T(8,128)S(1)}, f32[16,8,256]{2,1,0:T(8,128)S(1)}, u32[]{:S(2)}, u32[]{:S(2)}) collective-permute-start(f32[16,8,256]{2,1,0:T(8,128)S(1)} %get-tuple-element.101), channel_id=1, source_target_pairs={{0,2},{2,0},{4,6},{6,4},{1,3},{3,1},{5,7},{7,5},{8,10},{10,8},{12,... | collective-permute-start | bytes 393224 | tf_op jit(solution)/shard_map/ppermute | solution.py:274
  76.1 8.7 %collective-permute-start.14 = (f32[16,8,256]{2,1,0:T(8,128)S(1)}, f32[16,8,256]{2,1,0:T(8,128)S(1)}, u32[]{:S(2)}, u32[]{:S(2)}) collective-permute-start(f32[16,8,256]{2,1,0:T(8,128)S(1)} %get-tuple-element.99), channel_id=1, source_target_pairs={{0,4},{2,6},{4,0},{6,2},{1,5},{3,7},{5,1},{7,3},{8,12},{10,14},{12... | collective-permute-start | bytes 393224 | tf_op jit(solution)/shard_map/ppermute | solution.py:274
  78.5 8.6 %collective-permute-start.15 = (f32[16,8,256]{2,1,0:T(8,128)S(1)}, f32[16,8,256]{2,1,0:T(8,128)S(1)}, u32[]{:S(2)}, u32[]{:S(2)}) collective-permute-start(f32[16,8,256]{2,1,0:T(8,128)S(1)} %get-tuple-element.100), channel_id=1, source_target_pairs={{0,6},{2,4},{4,2},{6,0},{1,7},{3,5},{5,3},{7,1},{8,14},{10,12},{12... | collective-permute-start | bytes 393224 | tf_op jit(solution)/shard_map/ppermute | solution.py:274
  120.7 21.9 %all-to-all-start.3 = ((f32[8,128,256]{2,1,0:T(8,128)}), f32[8,128,256]{2,1,0:T(8,128)S(1)}, u32[]{:S(2)}, u32[]{:S(2)}) async-start(f32[8,128,256]{2,1,0:T(8,128)} %bitcast.10), calls=%async_computation.3 | async-start | bytes 2097152 | tf_op jit(solution)/shard_map/all_to_all | solution.py:278
  127.4 1.9 %collective-permute-start.16 = (f32[64,8,256]{2,1,0:T(8,128)S(1)}, f32[64,8,256]{2,1,0:T(8,128)S(1)}, u32[]{:S(2)}, u32[]{:S(2)}) collective-permute-start(f32[64,8,256]{2,1,0:T(8,128)S(1)} %all_to_all.20.mine), channel_id=1, source_target_pairs={{0,1},{1,0},{2,3},{3,2},{4,5},{5,4},{6,7},{7,6},{8,9},{9,8},{10,11... | collective-permute-start | bytes 1572872 | tf_op jit(solution)/shard_map/ppermute | solution.py:274
Sparse Core Ops, SparseCore 0:
  10.3 28.7 all-gather.2
  89.7 47.8 all-gather.4
